TPU v7x, 32 devices: a whole 2x2x4 slice. The times are simulated.
32 devices in a mesh: seq: 16 (over z, y, core), head: 2 (over x).
Axes of the slice: x: 2, y: 2, z: 4, core: 2. Of those that a mesh axis runs over, the one named last changes fastest.
Arguments:
- queries: bfloat16 [4096, 4096], P('seq', 'head'), may hold values from -8 to 8
- key_rows: bfloat16 [4096, 4096], P('seq', 'head'), may hold values from -8 to 8
- value_rows: bfloat16 [4096, 4096], P('seq', 'head'), may hold values from -12 to 12
- stream: bfloat16 [4096, 4096], P('seq', 'head'), may hold values from -6 to 11
- norm_gain: float32 [4096], P('head'), may hold values from 0.5 to 1.5
- norm_bias: float32 [4096], P('head'), may hold values from -3 to 3
- head_offsets: int32 [4, 32], replicated, may hold values from 0 to 15, as said below
- cotangent: bfloat16 [4096, 4096], P('seq', 'head'), may hold values from -24 to 24
Outputs:
- normed_out: bfloat16 [4096, 4096], P('seq', 'head')
- grad_queries: float32 [4096, 4096], P('seq', 'head')
- grad_keys: float32 [4096, 4096], P('seq', 'head')
- grad_values: float32 [4096, 4096], P('seq', 'head')
Inputs may be any that keep to these rules, and one draw needn't show every extreme that they name: `head_offsets`: row b - 1 holds the offsets of branch b; each value 0 to 2 ** b - 1 is the offset of exactly 32 / 2 ** b heads of that row.
All inputs are finite; a program needn't handle non-finite values.
Results may differ from a plain program's by a relative error of at most 0.0055.
Values may be sent and summed in bfloat16 or wider, within the bound.
No kernel may reach another device: no remote copies, remote signals or barrier semaphores. Data moves between devices by JAX's collectives and lax.ppermute only.
A program may use at most 192 MiB of HBM per device.

v0:
```python
import math

import jax
import jax.numpy as jnp
from jax import lax
from jax.sharding import PartitionSpec as P

HEAD_DIM = 128
BRANCHES = 4


alpha_res = (2.0 * 24.0) ** 0.25
eps_norm = 1e-05


def from_partner(block, axis, bit):
    count = lax.axis_size(axis)
    route = []
    for low in range(count):
        high = low | 1 << bit
        if high != low and high < count:
            route += [(low, high), (high, low)]
    return lax.ppermute(block, axis, route)


def pick_rows(source, stride, offsets_now):
    blocks = source.shape[0] // stride
    shaped = source.reshape((blocks, stride) + source.shape[1:])
    chosen = jnp.arange(stride, dtype=jnp.int32)[:, None] == offsets_now[None, :]
    member = chosen.reshape((1, stride, offsets_now.shape[0]) + (1,) * (source.ndim - 2))
    return jnp.sum(jnp.where(member, shaped, jnp.zeros((), source.dtype)), axis=1)


def place_rows(piece_rows, stride, offsets_now, filler):
    chosen = jnp.arange(stride, dtype=jnp.int32)[:, None] == offsets_now[None, :]
    member = chosen.reshape((1, stride, offsets_now.shape[0]) + (1,) * (piece_rows.ndim - 2))
    spread = jnp.where(member, piece_rows[:, None], jnp.asarray(filler, piece_rows.dtype))
    return spread.reshape((piece_rows.shape[0] * stride,) + piece_rows.shape[1:])


def split_blocks(source):
    length = source.shape[0]
    block_rows = math.gcd(length, 512)
    return source.reshape((length // block_rows, block_rows) + source.shape[1:])


def merge_blocks(source):
    return source.reshape((source.shape[0] * source.shape[1],) + source.shape[2:])


def forward_block(query_rows, key_set, value_set):
    scaling = HEAD_DIM ** (-0.5)
    scores = (
        jnp.einsum("qhe,khe->hqk", query_rows, key_set, preferred_element_type=jnp.float32)
        * scaling
    )
    maxima = jnp.max(scores, axis=2)
    weights = jnp.exp(scores - maxima[:, :, None])
    totals = jnp.sum(weights, axis=2)
    blended = jnp.einsum(
        "hqk,khe->qhe", weights.astype(jnp.bfloat16), value_set, preferred_element_type=jnp.float32
    )
    return (blended / totals.T[:, :, None], maxima.T, totals.T)


def forward_rows(query_rows, key_set, value_set):
    result = lax.map(
        lambda query_block: forward_block(query_block, key_set, value_set), split_blocks(query_rows)
    )
    return (merge_blocks(result[0]), merge_blocks(result[1]), merge_blocks(result[2]))


def backward_block(grouped_now, key_set, value_set):
    query_rows, grad_rows, lse_rows, delta_rows = grouped_now
    scaling = HEAD_DIM ** (-0.5)
    scores = (
        jnp.einsum("qhe,khe->hqk", query_rows, key_set, preferred_element_type=jnp.float32)
        * scaling
    )
    probs = jnp.exp(scores - lse_rows.T[:, :, None])
    dvalue = jnp.einsum(
        "hqk,qhe->khe", probs.astype(jnp.bfloat16), grad_rows, preferred_element_type=jnp.float32
    )
    dprob = jnp.einsum("qhe,khe->hqk", grad_rows, value_set, preferred_element_type=jnp.float32)
    dscore = (probs * (dprob - delta_rows.T[:, :, None]) * scaling).astype(jnp.bfloat16)
    dquery = jnp.einsum("hqk,khe->qhe", dscore, key_set, preferred_element_type=jnp.float32)
    dkey = jnp.einsum("hqk,qhe->khe", dscore, query_rows, preferred_element_type=jnp.float32)
    return (dquery, dkey, dvalue)


def query_block(grouped_now, key_set, value_set):
    query_rows, grad_rows, lse_rows, delta_rows = grouped_now
    scaling = HEAD_DIM ** (-0.5)
    scores = (
        jnp.einsum("qhe,khe->hqk", query_rows, key_set, preferred_element_type=jnp.float32)
        * scaling
    )
    probs = jnp.exp(scores - lse_rows.T[:, :, None])
    dprob = jnp.einsum("qhe,khe->hqk", grad_rows, value_set, preferred_element_type=jnp.float32)
    dscore = (probs * (dprob - delta_rows.T[:, :, None]) * scaling).astype(jnp.bfloat16)
    return jnp.einsum("hqk,khe->qhe", dscore, key_set, preferred_element_type=jnp.float32)


def backward_rows(query_rows, grad_rows, lse_rows, delta_rows, key_set, value_set):
    grouped = (
        split_blocks(query_rows),
        split_blocks(grad_rows),
        split_blocks(lse_rows),
        split_blocks(delta_rows),
    )
    result = lax.map(lambda grouped_now: backward_block(grouped_now, key_set, value_set), grouped)
    return (merge_blocks(result[0]), jnp.sum(result[1], axis=0), jnp.sum(result[2], axis=0))


def upper_side(seq_index, section):
    return seq_index >> section & 1 == 1


def grow_group(stacked, sections, seq_index):
    current = stacked
    for section in range(sections):
        other = from_partner(current, "seq", section)
        current = jnp.where(
            upper_side(seq_index, section),
            jnp.concatenate([other, current], 1),
            jnp.concatenate([current, other], 1),
        )
    return current


def shrink_group(partial_value, sections, seq_index):
    current = partial_value
    for section in reversed(range(sections)):
        half_rows = current.shape[1] // 2
        lower_rows = current[:, :half_rows]
        upper_rows = current[:, half_rows:]
        upper = upper_side(seq_index, section)
        kept_rows = jnp.where(upper, upper_rows, lower_rows)
        outgoing = jnp.where(upper, lower_rows, upper_rows)
        current = kept_rows + from_partner(outgoing.astype(jnp.bfloat16), "seq", section).astype(
            outgoing.dtype
        )
    return current


def width_sum(payload):
    return lax.psum(payload, "head")


def shards(queries, key_rows, value_rows, stream, norm_gain, norm_bias, head_offsets, cotangent):
    row_count = queries.shape[0]
    heads_here = queries.shape[1] // HEAD_DIM
    seq_index = lax.axis_index("seq")
    first_head = lax.axis_index("head") * heads_here
    offsets_here = lax.dynamic_slice_in_dim(head_offsets, first_head, heads_here, 1)
    shape_three = (row_count, heads_here, HEAD_DIM)
    query_all = queries.reshape(shape_three)
    key_all = key_rows.reshape(shape_three)
    value_all = value_rows.reshape(shape_three)
    branch_list = list(range(1, BRANCHES + 1))
    picked = []
    for branch in branch_list:
        stride = 2**branch
        offsets_now = offsets_here[branch - 1]
        picked.append(
            jnp.stack(
                [pick_rows(key_all, stride, offsets_now), pick_rows(value_all, stride, offsets_now)]
            )
        )
    gathered = [grow_group(picked[branch - 1], branch, seq_index) for branch in branch_list]
    local_result = forward_rows(query_all, key_all, value_all)
    blended_list = [local_result[0]]
    maxima_list = [local_result[1]]
    totals_list = [local_result[2]]
    for branch in branch_list:
        stride = 2**branch
        offsets_now = offsets_here[branch - 1]
        key_set = gathered[branch - 1]
        result = forward_rows(pick_rows(query_all, stride, offsets_now), key_set[0], key_set[1])
        blended_list.append(place_rows(result[0], stride, offsets_now, 0.0))
        maxima_list.append(place_rows(result[1], stride, offsets_now, -jnp.inf))
        totals_list.append(place_rows(result[2], stride, offsets_now, 0.0))
    row_peak = maxima_list[0]
    for maxima in maxima_list[1:]:
        row_peak = jnp.maximum(row_peak, maxima)
    shares = [
        totals * jnp.exp(maxima - row_peak) for totals, maxima in zip(totals_list, maxima_list)
    ]
    normaliser = shares[0]
    for shares_now in shares[1:]:
        normaliser = normaliser + shares_now
    attention = jnp.zeros(shape_three, jnp.float32)
    for shares_now, blended in zip(shares, blended_list):
        attention = attention + (shares_now / normaliser)[:, :, None] * blended
    pre_norm = alpha_res * stream.astype(jnp.float32) + attention.reshape(
        row_count, heads_here * HEAD_DIM
    )
    full_width = pre_norm.shape[1] * lax.axis_size("head")
    centre = width_sum(jnp.sum(pre_norm, axis=1)) / full_width
    centred = pre_norm - centre[:, None]
    inv_std = 1.0 / jnp.sqrt(width_sum(jnp.sum(centred * centred, axis=1)) / full_width + eps_norm)
    normed = centred * inv_std[:, None]
    normed_out = (norm_gain * normed + norm_bias).astype(jnp.bfloat16)
    grad_norm = cotangent.astype(jnp.float32) * norm_gain
    sums_pair = width_sum((jnp.sum(grad_norm, axis=1), jnp.sum(grad_norm * normed, axis=1)))
    mean_grad = sums_pair[0] / full_width
    mean_cross = sums_pair[1] / full_width
    grad_pre = inv_std[:, None] * (grad_norm - mean_grad[:, None] - normed * mean_cross[:, None])
    grad_attn = grad_pre.astype(jnp.bfloat16).reshape(shape_three)
    delta_all = jnp.sum(grad_attn.astype(jnp.float32) * attention, axis=2)
    lse_all = row_peak + jnp.log(normaliser)
    grad_query, grad_key, grad_value = backward_rows(
        query_all, grad_attn, lse_all, delta_all, key_all, value_all
    )
    partials = []
    for branch in branch_list:
        stride = 2**branch
        offsets_now = offsets_here[branch - 1]
        key_set = gathered[branch - 1]
        result = backward_rows(
            pick_rows(query_all, stride, offsets_now),
            pick_rows(grad_attn, stride, offsets_now),
            pick_rows(lse_all, stride, offsets_now),
            pick_rows(delta_all, stride, offsets_now),
            key_set[0],
            key_set[1],
        )
        grad_query = grad_query + place_rows(result[0], stride, offsets_now, 0.0)
        partials.append(jnp.stack([result[1], result[2]]))
    returned = [shrink_group(partials[branch - 1], branch, seq_index) for branch in branch_list]
    for branch in branch_list:
        stride = 2**branch
        offsets_now = offsets_here[branch - 1]
        grad_key = grad_key + place_rows(returned[branch - 1][0], stride, offsets_now, 0.0)
        grad_value = grad_value + place_rows(returned[branch - 1][1], stride, offsets_now, 0.0)
    flat_shape = (row_count, heads_here * HEAD_DIM)
    return (
        normed_out,
        grad_query.reshape(flat_shape),
        grad_key.reshape(flat_shape),
        grad_value.reshape(flat_shape),
    )


def solution(mesh):
    return jax.shard_map(
        shards,
        mesh=mesh,
        in_specs=(
            P("seq", "head"),
            P("seq", "head"),
            P("seq", "head"),
            P("seq", "head"),
            P("head"),
            P("head"),
            P(),
            P("seq", "head"),
        ),
        out_specs=(P("seq", "head"), P("seq", "head"), P("seq", "head"), P("seq", "head")),
        check_vma=False,
    )
```

profile of v0, /device:TPU:0, one launch (start us, length us, event | category | flops | bytes accessed | tf_op | source)
XLA Modules:
  0.0 346.0 jit_solution(546439796576332319)
XLA Ops:
  3.5 2.1 select_reduce_fusion.10
  14.8 2.4 select_reduce_fusion.5
  19.5 3.3 multiply_reduce_fusion
  23.9 3.0 collective-permute-start.7
  36.5 2.1 collective-permute-start.8
  38.7 3.6 %fusion.1 = f32[16,256]{1,0:T(8,128)} fusion(f32[16,256,256]{1,2,0:T(8,128)} %get-tuple-element.286, f32[16,256]{1,0:T(8,128)S(1)} %copy-done.88), kind=kLoop, calls=%fused_computation.12 | loop fusion | flops 3141632 | bytes 4227072 | tf_op jit(solution)/shard_map/while/body/eval_jaxpr/reduce_sum | solution.py:59
  45.5 5.7 %collective-permute-done.4 = bf16[2,64,16,128]{3,1,2,0:T(8,128)(2,1)S(1)} collective-permute-done((bf16[2,64,16,128]{3,1,2,0:T(8,128)(2,1)S(1)}, bf16[2,64,16,128]{3,1,2,0:T(8,128)(2,1)S(1)}, u32[]{:S(2)}, u32[]{:S(2)}) %collective-permute-start.4) | collective-permute-done | bytes 524320 | tf_op jit(solution)/shard_map/ppermute | solution.py:23
  55.4 2.6 collective-permute-start.9
  58.0 1.9 maximum_select_fusion
  67.4 2.0 copy.360
  69.3 3.2 collective-permute-done.2
  72.5 3.0 maximum_select_fusion.1
  81.5 2.0 copy.361
  83.6 13.0 %collective-permute-done.5 = bf16[2,128,16,128]{3,1,2,0:T(8,128)(2,1)} collective-permute-done((bf16[2,128,16,128]{3,1,2,0:T(8,128)(2,1)}, bf16[2,128,16,128]{3,1,2,0:T(8,128)(2,1)}, u32[]{:S(2)}, u32[]{:S(2)}) %collective-permute-start.5) | collective-permute-done | bytes 1048608 | tf_op jit(solution)/shard_map/ppermute | solution.py:23
  96.6 2.9 maximum_select_fusion.2
  101.3 1.8 copy.362
  104.7 3.0 maximum_select_fusion.3
  111.8 3.2 fusion.32
  115.1 2.0 copy.345
  117.3 1.8 copy.344
  119.3 1.8 copy.349
  121.3 1.8 copy.353
  123.3 1.8 copy.356
  125.3 2.2 copy-done.6
  127.5 9.1 %fusion.114 = (f32[256]{0:T(256)S(1)}, f32[256,2048]{1,0:T(8,128)S(1)}) fusion(f32[256,2048]{1,0:T(8,128)} %copy.356, pred[256,2048]{1,0:T(8,128)(4,1)S(1)} %copy-done.50, f32[32,8,16,128]{3,2,1,0:T(8,128)S(1)} %bitcast.463, f32[256,2048]{1,0:T(8,128)} %copy.353, pred[256,2048]{1,0:T(8,128)(4,1)} %copy.352, f32[32,8,16,128]{3,2,1,0:T(8,128)} %broadcast_bitcast_fusion, ...), kind=kLoop, calls=%fused_computation.278 | loop fusion | flops 8388352 | bytes 24118272 | tf_op jit(solution)/shard_map/reduce_sum | solution.py:199
  136.7 5.1 %psum.28 = f32[256]{0:T(256)S(1)} all-reduce(f32[256]{0:T(256)S(1)} %get-tuple-element.242), channel_id=1, replica_groups=mesh['seq'=16,'head'=2] {'head'}, use_global_device_ids=true, to_apply=%region_23.24 | all-reduce | flops 256 | bytes 2048 | tf_op jit(solution)/shard_map/psum | solution.py:147
  142.1 4.9 %psum.29 = f32[256]{0:T(256)S(1)} all-reduce(f32[256]{0:T(256)S(1)} %multiply_reduce_fusion.3), channel_id=1, replica_groups=mesh['seq'=16,'head'=2] {'head'}, use_global_device_ids=true, to_apply=%region_25.26 | all-reduce | flops 256 | bytes 2048 | tf_op jit(solution)/shard_map/psum | solution.py:147
  148.8 4.9 %all-reduce = (f32[256]{0:T(256)S(1)}, f32[256]{0:T(256)S(1)}) all-reduce(f32[256]{0:T(256)S(1)} %get-tuple-element.180, f32[256]{0:T(256)S(1)} %get-tuple-element.169), channel_id=1, replica_groups=mesh['seq'=16,'head'=2] {'head'}, use_global_device_ids=true, to_apply=%region_29.30 | all-reduce | flops 512 | bytes 4096 | tf_op jit(solution)/shard_map/psum | solution.py:147
  153.7 4.4 %select_reduce_fusion = (bf16[32,16,128]{2,1,0:T(8,128)(2,1)}, bf16[256,2048]{1,0:T(8,128)(2,1)S(1)}) fusion(pred[8,16]{0,1:T(8,128)(4,1)S(1)} %copy-done.115, f32[256]{0:T(256)S(1)} %broadcast_multiply_fusion, f32[256,2048]{1,0:T(8,128)S(1)} %get-tuple-element.243, f32[256]{0:T(256)S(1)} %broadcast_multiply_fusion.2, f32[256]{0:T(256)S(1)} %broadcast_multiply_fusion.1, ...), kind=kLoop, calls=%fused_computation.158 | loop fusion | flops 5701632 | bytes 4337792 | tf_op jit(solution)/shard_map/reduce_sum | solution.py:31
  160.5 2.0 copy.363
  162.6 7.0 %multiply_reduce_fusion.1 = f32[256,16]{0,1:T(8,128)} fusion(f32[256,16,128]{0,2,1:T(8,128)} %copy.363, f32[256,16,128]{0,2,1:T(8,128)} %copy.362, f32[256,16,128]{0,2,1:T(8,128)} %copy.361, f32[256,16,128]{0,2,1:T(8,128)} %copy-done.45, f32[256,16,128]{0,2,1:T(8,128)} %copy.360, f32[256,16]{0,1:T(8,128)S(1)} %copy-done.93, f32[256,16]{0,1:T(8,128)S(1)} %copy-done.95, ...), kind=kLoop, calls=%fused_computation.78 | loop fusion | flops 7860224 | bytes 11632640 | tf_op jit(solution)/shard_map/reduce_sum | solution.py:210
  171.3 3.5 %multiply_convert_fusion = bf16[16,256,256]{1,2,0:T(8,128)(2,1)S(1)} fusion(f32[16,256,256]{1,2,0:T(8,128)} %get-tuple-element.286, bf16[256,16,128]{0,2,1:T(8,128)(2,1)S(1)} %bitcast.488, f32[16,256]{1,0:T(8,128)} %bitcast.534, f32[16,256]{1,0:T(8,128)} %bitcast.523, bf16[256,2048]{1,0:T(8,128)(2,1)S(1)} %copy-done.62), kind=kOutput, calls=%fused_computation.8 | convolution fusion | flops 274726912 | bytes 8421376 | tf_op jit(solution)/shard_map/while/body/eval_jaxpr/qhe,khe->hqk/dot_general | solution.py:84
  174.9 1.8 fusion.122
  176.6 2.2 fusion.121
  182.0 1.8 convolution_bitcast_fusion.5
  183.8 1.9 convolution_bitcast_fusion.4
  189.8 2.2 copy.401
  192.1 2.4 multiply_convert_fusion.1
  195.9 1.8 convolution_bitcast_fusion.1
  197.7 2.3 convolution_bitcast_fusion
  201.4 2.2 fusion.44
  204.8 1.9 convolution_bitcast_fusion.3
  206.7 2.4 convolution_bitcast_fusion.2
  211.4 2.3 convolution_bitcast_fusion.12
  213.6 1.8 fusion.102
  220.1 2.2 fusion.3
  224.5 3.0 copy.375
  227.5 2.9 copy.405
  230.4 1.7 copy.373
  232.1 2.2 copy.381
  235.9 2.9 copy.426
  239.4 3.0 copy.419
  242.4 1.9 fusion.89
  244.3 3.3 copy.421
  247.6 2.6 select_convert_fusion
  250.2 1.8 collective-permute-start.16
  252.0 1.9 convert_add_fusion.1
  255.6 1.8 convert_add_fusion.3
  258.9 6.2 %collective-permute-done.11 = bf16[2,128,16,128]{3,1,2,0:T(8,128)(2,1)} collective-permute-done((bf16[2,128,16,128]{3,1,2,0:T(8,128)(2,1)}, bf16[2,128,16,128]{3,1,2,0:T(8,128)(2,1)}, u32[]{:S(2)}, u32[]{:S(2)}) %collective-permute-start.11) | collective-permute-done | bytes 1048608 | tf_op jit(solution)/shard_map/ppermute | solution.py:23
  265.2 2.0 convert_add_fusion.2
  267.4 30.8 %collective-permute-done.16 = bf16[2,128,16,128]{3,2,1,0:T(8,128)(2,1)S(1)} collective-permute-done((bf16[2,128,16,128]{3,2,1,0:T(8,128)(2,1)S(1)}, bf16[2,128,16,128]{3,2,1,0:T(8,128)(2,1)S(1)}, u32[]{:S(2)}, u32[]{:S(2)}) %collective-permute-start.16) | collective-permute-done | bytes 1048608 | tf_op jit(solution)/shard_map/ppermute | solution.py:23
  299.1 13.1 %collective-permute-done.17 = bf16[2,64,16,128]{3,2,1,0:T(8,128)(2,1)S(1)} collective-permute-done((bf16[2,64,16,128]{3,2,1,0:T(8,128)(2,1)S(1)}, bf16[2,64,16,128]{3,2,1,0:T(8,128)(2,1)S(1)}, u32[]{:S(2)}, u32[]{:S(2)}) %collective-permute-start.17) | collective-permute-done | bytes 524320 | tf_op jit(solution)/shard_map/ppermute | solution.py:23
  315.1 4.6 %collective-permute-done.18 = bf16[2,32,16,128]{3,2,1,0:T(8,128)(2,1)S(1)} collective-permute-done((bf16[2,32,16,128]{3,2,1,0:T(8,128)(2,1)S(1)}, bf16[2,32,16,128]{3,2,1,0:T(8,128)(2,1)S(1)}, u32[]{:S(2)}, u32[]{:S(2)}) %collective-permute-start.18) | collective-permute-done | bytes 262176 | tf_op jit(solution)/shard_map/ppermute | solution.py:23
  329.7 15.7 %fusion.11 = (f32[256,2048]{1,0:T(8,128)}, f32[256,2048]{1,0:T(8,128)}, f32[256,2048]{1,0:T(8,128)}) fusion(pred[256,2048]{1,0:T(8,128)(4,1)} %copy.355, f32[32,8,16,128]{3,2,1,0:T(8,128)} %bitcast.498, pred[256,2048]{1,0:T(8,128)(4,1)} %copy.348, f32[32,8,16,128]{3,2,1,0:T(8,128)S(1)} %bitcast.492, f32[256,2048]{1,0:T(8,128)S(1)} %copy-done.44, ...), kind=kLoop, calls=%fused_computation.22 | loop fusion | flops 12582912 | bytes 34340864 | tf_op jit(solution)/shard_map/add | solution.py:235
  (438 shorter events, 99.1 us)
Async XLA Ops:
  1.4 26.1 %copy-start.122 = (pred[2,16]{1,0:T(4,128)(4,1)}, pred[2,16]{1,0:T(4,128)(4,1)S(1)}, u32[]{:S(2)}) copy-start(pred[2,16]{1,0:T(4,128)(4,1)S(1)} %iota_compare_fusion.3) | copy-start | bytes 100
  7.7 50.3 %collective-permute-start = (bf16[2,128,16,128]{3,1,2,0:T(8,128)(2,1)}, bf16[2,128,16,128]{3,1,2,0:T(8,128)(2,1)}, u32[]{:S(2)}, u32[]{:S(2)}) collective-permute-start(bf16[2,128,16,128]{3,1,2,0:T(8,128)(2,1)} %pad_maximum_fusion.4), channel_id=1, source_target_pairs={{0,2},{2,0},{4,6},{6,4},{8,10},{10,8},{12,14},{14,12},{16,18},{18,... | collective-permute-start | bytes 3145736 | tf_op jit(solution)/shard_map/ppermute | solution.py:23
  9.7 65.9 %copy-start.65 = (bf16[64,16,128]{2,1,0:T(8,128)(2,1)}, bf16[64,16,128]{2,1,0:T(8,128)(2,1)S(1)}, u32[]{:S(2)}) copy-start(bf16[64,16,128]{2,1,0:T(8,128)(2,1)S(1)} %get-tuple-element.208) | copy-start | bytes 786436
  11.4 30.9 %collective-permute-start.1 = (bf16[2,64,16,128]{3,1,2,0:T(8,128)(2,1)}, bf16[2,64,16,128]{3,1,2,0:T(8,128)(2,1)}, u32[]{:S(2)}, u32[]{:S(2)}) collective-permute-start(bf16[2,64,16,128]{3,1,2,0:T(8,128)(2,1)} %pad_maximum_fusion.5), channel_id=1, source_target_pairs={{0,2},{2,0},{4,6},{6,4},{8,10},{10,8},{12,14},{14,12},{16,18},{18,... | collective-permute-start | bytes 1572872 | tf_op jit(solution)/shard_map/ppermute | solution.py:23
  11.4 16.3 %copy-start.109 = (pred[16,16]{1,0:T(8,128)(4,1)}, pred[16,16]{1,0:T(8,128)(4,1)S(1)}, u32[]{:S(2)}) copy-start(pred[16,16]{1,0:T(8,128)(4,1)S(1)} %iota_compare_fusion) | copy-start | bytes 772
  14.2 8.7 %collective-permute-start.6 = (bf16[2,16,16,128]{3,1,2,0:T(8,128)(2,1)}, bf16[2,16,16,128]{3,1,2,0:T(8,128)(2,1)}, u32[]{:S(2)}, u32[]{:S(2)}) collective-permute-start(bf16[2,16,16,128]{3,1,2,0:T(8,128)(2,1)} %pad_maximum_fusion.7), channel_id=1, source_target_pairs={{0,2},{2,0},{4,6},{6,4},{8,10},{10,8},{12,14},{14,12},{16,18},{18,... | collective-permute-start | bytes 393224 | tf_op jit(solution)/shard_map/ppermute | solution.py:23
  14.7 12.3 %copy-start.116 = (pred[8,16]{1,0:T(8,128)(4,1)}, pred[8,16]{1,0:T(8,128)(4,1)S(1)}, u32[]{:S(2)}) copy-start(pred[8,16]{1,0:T(8,128)(4,1)S(1)} %iota_compare_fusion.1) | copy-start | bytes 388
  17.2 82.3 %copy-start.73 = (bf16[32,16,128]{2,1,0:T(8,128)(2,1)}, bf16[32,16,128]{2,1,0:T(8,128)(2,1)S(1)}, u32[]{:S(2)}) copy-start(bf16[32,16,128]{2,1,0:T(8,128)(2,1)S(1)} %get-tuple-element.183) | copy-start | bytes 393220
  18.1 16.9 %collective-permute-start.3 = (bf16[2,32,16,128]{3,1,2,0:T(8,128)(2,1)}, bf16[2,32,16,128]{3,1,2,0:T(8,128)(2,1)}, u32[]{:S(2)}, u32[]{:S(2)}) collective-permute-start(bf16[2,32,16,128]{3,1,2,0:T(8,128)(2,1)} %pad_maximum_fusion.6), channel_id=1, source_target_pairs={{0,2},{2,0},{4,6},{6,4},{8,10},{10,8},{12,14},{14,12},{16,18},{18,... | collective-permute-start | bytes 786440 | tf_op jit(solution)/shard_map/ppermute | solution.py:23
  18.9 3.9 %copy-start.36 = (bf16[256,2048]{0,1:T(8,128)(2,1)}, bf16[256,2048]{0,1:T(8,128)(2,1)S(1)}, u32[]{:S(2)}) copy-start(bf16[256,2048]{0,1:T(8,128)(2,1)S(1)} %copy.449) | copy-start | bytes 3145732
  19.5 7.5 %copy-start.72 = (bf16[128,16,128]{2,1,0:T(8,128)(2,1)S(1)}, bf16[128,16,128]{2,1,0:T(8,128)(2,1)}, u32[]{:S(2)}) copy-start(bf16[128,16,128]{2,1,0:T(8,128)(2,1)} %get-tuple-element.207) | copy-start | bytes 1572868
  19.5 8.3 %copy-start.120 = (pred[4,16]{1,0:T(4,128)(4,1)S(1)}, pred[4,16]{1,0:T(4,128)(4,1)}, u32[]{:S(2)}) copy-start(pred[4,16]{1,0:T(4,128)(4,1)} %copy-done.119) | copy-start | bytes 196
  23.9 12.4 %collective-permute-start.7 = (bf16[2,32,16,128]{3,1,2,0:T(8,128)(2,1)S(1)}, bf16[2,32,16,128]{3,1,2,0:T(8,128)(2,1)S(1)}, u32[]{:S(2)}, u32[]{:S(2)}) collective-permute-start(bf16[2,32,16,128]{3,1,2,0:T(8,128)(2,1)S(1)} %maximum_select_fusion.9), channel_id=1, source_target_pairs={{0,4},{4,0},{2,6},{6,2},{8,12},{12,8},{10,14},{14,10},{16,20},{20,... | collective-permute-start | bytes 786440 | tf_op jit(solution)/shard_map/ppermute | solution.py:23
  27.5 32.4 %copy-start.51 = (bf16[128,16,128]{0,2,1:T(8,128)(2,1)}, bf16[128,16,128]{0,2,1:T(8,128)(2,1)S(1)}, u32[]{:S(2)}) copy-start(bf16[128,16,128]{0,2,1:T(8,128)(2,1)S(1)} %copy.399) | copy-start | bytes 1572868
  27.9 5.4 %copy-start.101 = (pred[256,16]{0,1:T(8,128)(4,1)}, pred[256,16]{0,1:T(8,128)(4,1)S(1)}, u32[]{:S(2)}) copy-start(pred[256,16]{0,1:T(8,128)(4,1)S(1)} %copy.316) | copy-start | bytes 12292
  28.0 5.3 %copy-start.103 = (pred[256,16]{0,1:T(8,128)(4,1)}, pred[256,16]{0,1:T(8,128)(4,1)S(1)}, u32[]{:S(2)}) copy-start(pred[256,16]{0,1:T(8,128)(4,1)S(1)} %copy.323) | copy-start | bytes 12292
  29.9 5.1 %copy-start.76 = (bf16[1,32,16,128]{3,1,2,0:T(8,128)(2,1)S(1)}, bf16[1,32,16,128]{3,1,2,0:T(8,128)(2,1)}, u32[]{:S(2)}) copy-start(bf16[1,32,16,128]{3,1,2,0:T(8,128)(2,1)} %copy-done.75) | copy-start | bytes 393220
  29.9 5.1 %copy-start.78 = (bf16[1,32,16,128]{3,1,2,0:T(8,128)(2,1)S(1)}, bf16[1,32,16,128]{3,1,2,0:T(8,128)(2,1)}, u32[]{:S(2)}) copy-start(bf16[1,32,16,128]{3,1,2,0:T(8,128)(2,1)} %copy-done.77) | copy-start | bytes 393220
  33.3 5.4 %copy-start.88 = (f32[16,256]{1,0:T(8,128)S(1)}, f32[16,256]{1,0:T(8,128)}, u32[]{:S(2)}) copy-start(f32[16,256]{1,0:T(8,128)} %get-tuple-element.285) | copy-start | bytes 49156
  36.3 14.9 %collective-permute-start.4 = (bf16[2,64,16,128]{3,1,2,0:T(8,128)(2,1)S(1)}, bf16[2,64,16,128]{3,1,2,0:T(8,128)(2,1)S(1)}, u32[]{:S(2)}, u32[]{:S(2)}) collective-permute-start(bf16[2,64,16,128]{3,1,2,0:T(8,128)(2,1)S(1)} %maximum_select_fusion.7), channel_id=1, source_target_pairs={{0,4},{4,0},{2,6},{6,2},{8,12},{12,8},{10,14},{14,10},{16,20},{20,... | collective-permute-start | bytes 1572872 | tf_op jit(solution)/shard_map/ppermute | solution.py:23
  36.5 17.5 %collective-permute-start.8 = (bf16[2,64,16,128]{3,1,2,0:T(8,128)(2,1)S(1)}, bf16[2,64,16,128]{3,1,2,0:T(8,128)(2,1)S(1)}, u32[]{:S(2)}, u32[]{:S(2)}) collective-permute-start(bf16[2,64,16,128]{3,1,2,0:T(8,128)(2,1)S(1)} %maximum_select_fusion.8), channel_id=1, source_target_pairs={{0,8},{8,0},{2,10},{10,2},{4,12},{12,4},{6,14},{14,6},{16,24},{24,... | collective-permute-start | bytes 1572872 | tf_op jit(solution)/shard_map/ppermute | solution.py:23
  38.7 3.6 %copy-start.70 = (bf16[1,64,16,128]{3,1,2,0:T(8,128)(2,1)S(1)}, bf16[1,64,16,128]{3,1,2,0:T(8,128)(2,1)}, u32[]{:S(2)}) copy-start(bf16[1,64,16,128]{3,1,2,0:T(8,128)(2,1)} %copy-done.69) | copy-start | bytes 786436
  43.9 11.6 %copy-start.59 = (bf16[2,128,16,128]{3,1,2,0:T(8,128)(2,1)}, bf16[2,128,16,128]{3,1,2,0:T(8,128)(2,1)S(1)}, u32[]{:S(2)}) copy-start(bf16[2,128,16,128]{3,1,2,0:T(8,128)(2,1)S(1)} %maximum_select_fusion.4) | copy-start | bytes 3145732
  43.9 14.1 %copy-start.55 = (bf16[1,128,16,128]{3,1,2,0:T(8,128)(2,1)S(1)}, bf16[1,128,16,128]{3,1,2,0:T(8,128)(2,1)}, u32[]{:S(2)}) copy-start(bf16[1,128,16,128]{3,1,2,0:T(8,128)(2,1)} %copy-done.54) | copy-start | bytes 1572868
  43.9 14.1 %copy-start.57 = (bf16[1,128,16,128]{3,1,2,0:T(8,128)(2,1)S(1)}, bf16[1,128,16,128]{3,1,2,0:T(8,128)(2,1)}, u32[]{:S(2)}) copy-start(bf16[1,128,16,128]{3,1,2,0:T(8,128)(2,1)} %copy-done.56) | copy-start | bytes 1572868
  43.9 28.6 %collective-permute-start.2 = (bf16[2,128,16,128]{3,1,2,0:T(8,128)(2,1)S(1)}, bf16[2,128,16,128]{3,1,2,0:T(8,128)(2,1)}, u32[]{:S(2)}, u32[]{:S(2)}) collective-permute-start(bf16[2,128,16,128]{3,1,2,0:T(8,128)(2,1)S(1)} %maximum_select_fusion.4), channel_id=1, source_target_pairs={{0,4},{4,0},{2,6},{6,2},{8,12},{12,8},{10,14},{14,10},{16,20},{20,... | collective-permute-start | bytes 3145736 | tf_op jit(solution)/shard_map/ppermute | solution.py:23
  52.5 44.1 %collective-permute-start.5 = (bf16[2,128,16,128]{3,1,2,0:T(8,128)(2,1)}, bf16[2,128,16,128]{3,1,2,0:T(8,128)(2,1)}, u32[]{:S(2)}, u32[]{:S(2)}) collective-permute-start(bf16[2,128,16,128]{3,1,2,0:T(8,128)(2,1)} %maximum_select_fusion.5), channel_id=1, source_target_pairs={{0,8},{8,0},{2,10},{10,2},{4,12},{12,4},{6,14},{14,6},{16,24},{24,... | collective-permute-start | bytes 3145736 | tf_op jit(solution)/shard_map/ppermute | solution.py:23
  55.4 49.3 %collective-permute-start.9 = (bf16[2,128,16,128]{3,1,2,0:T(8,128)(2,1)}, bf16[2,128,16,128]{3,1,2,0:T(8,128)(2,1)}, u32[]{:S(2)}, u32[]{:S(2)}) collective-permute-start(bf16[2,128,16,128]{3,1,2,0:T(8,128)(2,1)} %maximum_select_fusion.6), channel_id=1, source_target_pairs={{0,16},{16,0},{2,18},{18,2},{4,20},{20,4},{6,22},{22,6},{8,24},{24... | collective-permute-start | bytes 3145736 | tf_op jit(solution)/shard_map/ppermute | solution.py:23
  107.8 4.1 %copy-start.61 = (bf16[256,2048]{1,0:T(8,128)(2,1)S(1)}, bf16[256,2048]{1,0:T(8,128)(2,1)}, u32[]{:S(2)}) copy-start(bf16[256,2048]{1,0:T(8,128)(2,1)} %param.10) | copy-start | bytes 3145732
  125.3 11.3 %copy-start.8 = (f32[16,16,16,128]{3,2,1,0:T(8,128)}, f32[16,16,16,128]{3,2,1,0:T(8,128)S(1)}, u32[]{:S(2)}) copy-start(f32[16,16,16,128]{3,2,1,0:T(8,128)S(1)} %broadcast_in_dim.792) | copy-start | bytes 6291460
  136.6 10.4 %copy-start.58 = (bf16[256,2048]{1,0:T(8,128)(2,1)S(1)}, bf16[256,2048]{1,0:T(8,128)(2,1)}, u32[]{:S(2)}) copy-start(bf16[256,2048]{1,0:T(8,128)(2,1)} %param.15) | copy-start | bytes 3145732
  136.6 10.4 %copy-start.111 = (f32[2048]{0:T(1024)S(1)}, f32[2048]{0:T(1024)}, u32[]{:S(2)}) copy-start(f32[2048]{0:T(1024)} %param.12) | copy-start | bytes 24580
  136.7 10.4 %copy-start.118 = (f32[2048]{0:T(1024)S(1)}, f32[2048]{0:T(1024)}, u32[]{:S(2)}) copy-start(f32[2048]{0:T(1024)} %param.13) | copy-start | bytes 24580
  147.1 6.6 %copy-start.115 = (pred[8,16]{0,1:T(8,128)(4,1)S(1)}, pred[8,16]{0,1:T(8,128)(4,1)}, u32[]{:S(2)}) copy-start(pred[8,16]{0,1:T(8,128)(4,1)} %copy-done.114) | copy-start | bytes 388
  158.2 4.3 %copy-start.35 = (bf16[256,2048]{1,0:T(8,128)(2,1)}, bf16[256,2048]{1,0:T(8,128)(2,1)S(1)}, u32[]{:S(2)}) copy-start(bf16[256,2048]{1,0:T(8,128)(2,1)S(1)} %get-tuple-element.224) | copy-start | bytes 3145732
  162.6 8.7 %copy-start.40 = (bf16[256,2048]{0,1:T(8,128)(2,1)S(1)}, bf16[256,2048]{0,1:T(8,128)(2,1)}, u32[]{:S(2)}) copy-start(bf16[256,2048]{0,1:T(8,128)(2,1)} %copy.357) | copy-start | bytes 3145732
  162.6 8.7 %copy-start.62 = (bf16[256,2048]{1,0:T(8,128)(2,1)S(1)}, bf16[256,2048]{1,0:T(8,128)(2,1)}, u32[]{:S(2)}) copy-start(bf16[256,2048]{1,0:T(8,128)(2,1)} %param.10) | copy-start | bytes 3145732
  171.3 14.5 %copy-start.63 = (f32[256,16]{1,0:T(8,128)}, f32[256,16]{1,0:T(8,128)S(1)}, u32[]{:S(2)}) copy-start(f32[256,16]{1,0:T(8,128)S(1)} %copy.367) | copy-start | bytes 49156
  182.0 3.8 %copy-start.123 = (pred[2,16]{1,0:T(4,128)(4,1)S(1)}, pred[2,16]{1,0:T(4,128)(4,1)}, u32[]{:S(2)}) copy-start(pred[2,16]{1,0:T(4,128)(4,1)} %copy-done.122) | copy-start | bytes 100
  186.9 5.2 %copy-start.4 = (f32[16,128,256]{2,1,0:T(8,128)S(1)}, f32[16,128,256]{2,1,0:T(8,128)}, u32[]{:S(2)}) copy-start(f32[16,128,256]{2,1,0:T(8,128)} %copy-done.3) | copy-start | bytes 6291460
  209.1 4.6 %copy-start.86 = (bf16[16,16,128]{2,1,0:T(8,128)(2,1)S(1)}, bf16[16,16,128]{2,1,0:T(8,128)(2,1)}, u32[]{:S(2)}) copy-start(bf16[16,16,128]{2,1,0:T(8,128)(2,1)} %get-tuple-element.186) | copy-start | bytes 196612
  210.1 5.3 %copy-start.11 = (f32[1,256,16,128]{3,1,2,0:T(8,128)S(1)}, f32[1,256,16,128]{3,1,2,0:T(8,128)}, u32[]{:S(2)}) copy-start(f32[1,256,16,128]{3,1,2,0:T(8,128)} %convolution_bitcast_fusion.4) | copy-start | bytes 6291460
  211.4 4.1 %copy-start.10 = (f32[1,256,16,128]{3,1,2,0:T(8,128)S(1)}, f32[1,256,16,128]{3,1,2,0:T(8,128)}, u32[]{:S(2)}) copy-start(f32[1,256,16,128]{3,1,2,0:T(8,128)} %convolution_bitcast_fusion.5) | copy-start | bytes 6291460
  215.5 3.9 %copy-start.98 = (f32[256,16]{0,1:T(8,128)S(1)}, f32[256,16]{0,1:T(8,128)}, u32[]{:S(2)}) copy-start(f32[256,16]{0,1:T(8,128)} %get-tuple-element.225) | copy-start | bytes 49156
  216.8 35.1 %collective-permute-start.13 = (bf16[2,128,16,128]{3,1,2,0:T(8,128)(2,1)}, bf16[2,128,16,128]{3,1,2,0:T(8,128)(2,1)}, u32[]{:S(2)}, u32[]{:S(2)}) collective-permute-start(bf16[2,128,16,128]{3,1,2,0:T(8,128)(2,1)} %select_convert_fusion.1), channel_id=1, source_target_pairs={{0,8},{8,0},{2,10},{10,2},{4,12},{12,4},{6,14},{14,6},{16,24},{24,... | collective-permute-start | bytes 3145736 | tf_op jit(solution)/shard_map/ppermute | solution.py:23
  219.4 36.2 %collective-permute-start.10 = (bf16[2,128,16,128]{3,1,2,0:T(8,128)(2,1)}, bf16[2,128,16,128]{3,1,2,0:T(8,128)(2,1)}, u32[]{:S(2)}, u32[]{:S(2)}) collective-permute-start(bf16[2,128,16,128]{3,1,2,0:T(8,128)(2,1)} %select_convert_fusion.3), channel_id=1, source_target_pairs={{0,2},{2,0},{4,6},{6,4},{8,10},{10,8},{12,14},{14,12},{16,18},{18,... | collective-permute-start | bytes 3145736 | tf_op jit(solution)/shard_map/ppermute | solution.py:23
  238.8 26.3 %collective-permute-start.11 = (bf16[2,128,16,128]{3,1,2,0:T(8,128)(2,1)}, bf16[2,128,16,128]{3,1,2,0:T(8,128)(2,1)}, u32[]{:S(2)}, u32[]{:S(2)}) collective-permute-start(bf16[2,128,16,128]{3,1,2,0:T(8,128)(2,1)} %select_convert_fusion.2), channel_id=1, source_target_pairs={{0,4},{4,0},{2,6},{6,2},{8,12},{12,8},{10,14},{14,10},{16,20},{20,... | collective-permute-start | bytes 3145736 | tf_op jit(solution)/shard_map/ppermute | solution.py:23
  247.6 4.4 %copy-start.12 = (f32[1,256,16,128]{3,1,2,0:T(8,128)S(1)}, f32[1,256,16,128]{3,1,2,0:T(8,128)}, u32[]{:S(2)}) copy-start(f32[1,256,16,128]{3,1,2,0:T(8,128)} %convolution_bitcast_fusion.4) | copy-start | bytes 6291460
  250.2 48.0 %collective-permute-start.16 = (bf16[2,128,16,128]{3,2,1,0:T(8,128)(2,1)S(1)}, bf16[2,128,16,128]{3,2,1,0:T(8,128)(2,1)S(1)}, u32[]{:S(2)}, u32[]{:S(2)}) collective-permute-start(bf16[2,128,16,128]{3,2,1,0:T(8,128)(2,1)S(1)} %select_convert_fusion), channel_id=1, source_target_pairs={{0,16},{16,0},{2,18},{18,2},{4,20},{20,4},{6,22},{22,6},{8,24},{24... | collective-permute-start | bytes 3145736 | tf_op jit(solution)/shard_map/ppermute | solution.py:23
  252.0 3.6 %copy-start.14 = (f32[1,256,16,128]{3,1,2,0:T(8,128)S(1)}, f32[1,256,16,128]{3,1,2,0:T(8,128)}, u32[]{:S(2)}) copy-start(f32[1,256,16,128]{3,1,2,0:T(8,128)} %convolution_bitcast_fusion.1) | copy-start | bytes 6291460
  252.0 3.6 %copy-start.16 = (f32[1,256,16,128]{3,1,2,0:T(8,128)S(1)}, f32[1,256,16,128]{3,1,2,0:T(8,128)}, u32[]{:S(2)}) copy-start(f32[1,256,16,128]{3,1,2,0:T(8,128)} %convolution_bitcast_fusion) | copy-start | bytes 6291460
  254.0 44.7 %collective-permute-start.14 = (bf16[2,64,16,128]{3,1,2,0:T(8,128)(2,1)S(1)}, bf16[2,64,16,128]{3,1,2,0:T(8,128)(2,1)S(1)}, u32[]{:S(2)}, u32[]{:S(2)}) collective-permute-start(bf16[2,64,16,128]{3,1,2,0:T(8,128)(2,1)S(1)} %select_convert_fusion.5), channel_id=1, source_target_pairs={{0,4},{4,0},{2,6},{6,2},{8,12},{12,8},{10,14},{14,10},{16,20},{20,... | collective-permute-start | bytes 1572872 | tf_op jit(solution)/shard_map/ppermute | solution.py:23
  257.7 7.5 %copy-start.18 = (f32[1,256,16,128]{3,1,2,0:T(8,128)S(1)}, f32[1,256,16,128]{3,1,2,0:T(8,128)}, u32[]{:S(2)}) copy-start(f32[1,256,16,128]{3,1,2,0:T(8,128)} %convolution_bitcast_fusion.3) | copy-start | bytes 6291460
  257.7 7.5 %copy-start.20 = (f32[1,256,16,128]{3,1,2,0:T(8,128)S(1)}, f32[1,256,16,128]{3,1,2,0:T(8,128)}, u32[]{:S(2)}) copy-start(f32[1,256,16,128]{3,1,2,0:T(8,128)} %convolution_bitcast_fusion.2) | copy-start | bytes 6291460
  265.2 33.0 %copy-start.21 = (f32[16,128,256]{1,0,2:T(8,128)S(1)}, f32[16,128,256]{1,0,2:T(8,128)}, u32[]{:S(2)}) copy-start(f32[16,128,256]{1,0,2:T(8,128)} %copy.419) | copy-start | bytes 6291460
  265.2 33.0 %copy-start.22 = (f32[16,128,256]{1,0,2:T(8,128)S(1)}, f32[16,128,256]{1,0,2:T(8,128)}, u32[]{:S(2)}) copy-start(f32[16,128,256]{1,0,2:T(8,128)} %copy.421) | copy-start | bytes 6291460
  267.3 46.7 %collective-permute-start.12 = (bf16[2,64,16,128]{3,1,2,0:T(8,128)(2,1)S(1)}, bf16[2,64,16,128]{3,1,2,0:T(8,128)(2,1)S(1)}, u32[]{:S(2)}, u32[]{:S(2)}) collective-permute-start(bf16[2,64,16,128]{3,1,2,0:T(8,128)(2,1)S(1)} %select_convert_fusion.6), channel_id=1, source_target_pairs={{0,2},{2,0},{4,6},{6,4},{8,10},{10,8},{12,14},{14,12},{16,18},{18,... | collective-permute-start | bytes 1572872 | tf_op jit(solution)/shard_map/ppermute | solution.py:23
  298.6 13.7 %collective-permute-start.17 = (bf16[2,64,16,128]{3,2,1,0:T(8,128)(2,1)S(1)}, bf16[2,64,16,128]{3,2,1,0:T(8,128)(2,1)S(1)}, u32[]{:S(2)}, u32[]{:S(2)}) collective-permute-start(bf16[2,64,16,128]{3,2,1,0:T(8,128)(2,1)S(1)} %select_convert_fusion.4), channel_id=1, source_target_pairs={{0,8},{8,0},{2,10},{10,2},{4,12},{12,4},{6,14},{14,6},{16,24},{24,... | collective-permute-start | bytes 1572872 | tf_op jit(solution)/shard_map/ppermute | solution.py:23
  299.1 20.8 %collective-permute-start.15 = (bf16[2,32,16,128]{3,1,2,0:T(8,128)(2,1)S(1)}, bf16[2,32,16,128]{3,1,2,0:T(8,128)(2,1)S(1)}, u32[]{:S(2)}, u32[]{:S(2)}) collective-permute-start(bf16[2,32,16,128]{3,1,2,0:T(8,128)(2,1)S(1)} %select_convert_fusion.8), channel_id=1, source_target_pairs={{0,2},{2,0},{4,6},{6,4},{8,10},{10,8},{12,14},{14,12},{16,18},{18,... | collective-permute-start | bytes 786440 | tf_op jit(solution)/shard_map/ppermute | solution.py:23
  312.5 7.2 %collective-permute-start.18 = (bf16[2,32,16,128]{3,2,1,0:T(8,128)(2,1)S(1)}, bf16[2,32,16,128]{3,2,1,0:T(8,128)(2,1)S(1)}, u32[]{:S(2)}, u32[]{:S(2)}) collective-permute-start(bf16[2,32,16,128]{3,2,1,0:T(8,128)(2,1)S(1)} %select_convert_fusion.7), channel_id=1, source_target_pairs={{0,4},{4,0},{2,6},{6,2},{8,12},{12,8},{10,14},{14,10},{16,20},{20,... | collective-permute-start | bytes 786440 | tf_op jit(solution)/shard_map/ppermute | solution.py:23
  319.8 2.0 collective-permute-start.19
  325.3 3.6 %copy-start.42 = (f32[256,2048]{1,0:T(8,128)S(1)}, f32[256,2048]{1,0:T(8,128)}, u32[]{:S(2)}) copy-start(f32[256,2048]{1,0:T(8,128)} %copy.375) | copy-start | bytes 6291460
  325.3 4.4 %copy-start.43 = (f32[256,2048]{1,0:T(8,128)S(1)}, f32[256,2048]{1,0:T(8,128)}, u32[]{:S(2)}) copy-start(f32[256,2048]{1,0:T(8,128)} %copy.405) | copy-start | bytes 6291460
  329.7 15.7 %copy-start.1 = (s32[4,32]{1,0:T(4,128)S(1)}, s32[4,32]{1,0:T(4,128)}, u32[]{:S(2)}) copy-start(s32[4,32]{1,0:T(4,128)} %param.14) | copy-start | bytes 1540
  (80 other events, 180.2 us)
where the time goes:
time: 353 us; the launch traced here: 346 us
  local copies, waits for them, and re-layouts  92.4 us (26%)
  other arithmetic  90.7 us (26%)
  waiting for transfers between devices  76.6 us (22%)
  matrix products  50.5 us (14%)
  starting transfers between devices  17.9 us (5%)
  blocking collectives  14.9 us (4%)
    ppermute x20, waiting for transfers between devices, from_partner(): return lax.ppermute(block, axis, route)  76.6 us
    broadcast_in_dim x52, local copies, waits for them, and re-layouts, place_rows(): jnp.where(member, piece_rows[:, None], jnp.asarray(filler, piece_rows.dty...  24 us
    ppermute x20, starting transfers between devices, from_partner(): return lax.ppermute(block, axis, route)  17.9 us
    select_n x10, other arithmetic, grow_group(): jnp.where(upper_side(seq_index, section), jnp.concatenate([other, current...  17.5 us
    unnamed x253, local copies, waits for them, and re-layouts  17 us
    add x1, other arithmetic, shards(): grad_value + place_rows(returned[branch - 1][1], stride, offsets_now, 0.0)  15.7 us
    reduce_sum x12, other arithmetic, pick_rows(): jnp.sum(jnp.where(member, shaped, jnp.zeros((), source.dtype)), axis=1)  15.2 us
    psum x3, blocking collectives, width_sum(): return lax.psum(payload, 'head')  14.9 us
  transfers between devices with their start and end apart: 20, of which 7 were waited for; matrix products, arithmetic and copies ran while one was open for 30% of the time, Pallas kernels for 0%

commit v1 on v0

v1 whole, which is shorter than its diff:
```python
import functools
import math
from typing import NamedTuple

import jax
import jax.numpy as jnp
from jax import lax
from jax.experimental import pallas as pl
from jax.experimental.pallas import tpu as pltpu
from jax.sharding import PartitionSpec as P

HEAD_DIM = 128
BRANCHES = 4
FAR = (2, 3, 4)
STAT_ROWS = 8

alpha_res = (2.0 * 24.0) ** 0.25
eps_norm = 1e-05
scaling = HEAD_DIM ** (-0.5)
scaling2 = scaling * math.log2(math.e)

f32 = jnp.float32
bf16 = jnp.bfloat16


def dot_nt(a, b):
    return lax.dot_general(a, b, (((1,), (1,)), ((), ())), preferred_element_type=f32)


def dot_nn(a, b):
    return lax.dot_general(a, b, (((1,), (0,)), ((), ())), preferred_element_type=f32)


def dot_tn(a, b):
    return lax.dot_general(a, b, (((0,), (0,)), ((), ())), preferred_element_type=f32)


def flip(block, axis, mask):
    count = lax.axis_size(axis)
    return lax.ppermute(block, axis, [(i, i ^ mask) for i in range(count)])


def wide(column_block, times):
    return jnp.concatenate([column_block] * times, axis=1)


def attend(query, key, value):
    scores = dot_nt(query, key)
    peak = jnp.max(scores, axis=1, keepdims=True)
    weights = jnp.exp2((scores - peak) * scaling2).astype(bf16)
    both = dot_nn(weights, jnp.concatenate([value, jnp.ones_like(value)], axis=1))
    total = both[:, HEAD_DIM:]
    return both[:, :HEAD_DIM] / total, peak * scaling2 + jnp.log2(total)


def merged(out_a, lse_a, out_b, lse_b):
    peak = jnp.maximum(lse_a, lse_b)
    part_a = jnp.exp2(lse_a - peak)
    part_b = jnp.exp2(lse_b - peak)
    total = part_a + part_b
    return (out_a * part_a + out_b * part_b) / total, peak + jnp.log2(total)


def room(scratch):
    arrays = [x for x in scratch if not isinstance(x, pltpu.SemaphoreType) and hasattr(x, "memory_space")]
    arrays = [x for x in arrays if x.memory_space == pltpu.VMEM]
    return sum(math.prod(x.shape) * jnp.dtype(x.dtype).itemsize for x in arrays) + 4 * 2**20


class Plan:
    def __init__(self, rows, heads_here, meta, offsets):
        self.rows = rows
        self.heads = heads_here // 2
        self.width = self.heads * HEAD_DIM
        self.meta = meta
        self.offsets = offsets

    def taken(self, branch):
        return self.rows >> branch

    def call(
        self,
        body,
        ins,
        outs,
        scratch=(),
        name=None,
        in_place=pltpu.VMEM,
        out_place=pltpu.VMEM,
        aliases=None,
        wait_for=(),
    ):
        given, waited = 2 + len(ins), len(wait_for)

        def without_waited(*refs):
            body(*refs[:given], *refs[given + waited :])

        scalars = pl.BlockSpec(memory_space=pltpu.SMEM)
        return pl.pallas_call(
            without_waited if waited else body,
            out_shape=outs,
            in_specs=[scalars, scalars]
            + [pl.BlockSpec(memory_space=in_place)] * len(ins)
            + [pl.BlockSpec(memory_space=pl.ANY)] * waited,
            out_specs=[
                pl.BlockSpec(memory_space=out_place[i] if isinstance(out_place, list) else out_place)
                for i in range(len(outs))
            ],
            scratch_shapes=list(scratch),
            compiler_params=pltpu.CompilerParams(vmem_limit_bytes=room(scratch)),
            cost_estimate=pl.CostEstimate(flops=0, bytes_accessed=0, transcendentals=0),
            input_output_aliases=aliases or {},
            name=name,
        )(self.meta, self.offsets, *ins, *wait_for)

    def each_head(self, together, body):
        together = min(together, self.heads)
        if together == self.heads:
            for h in range(self.heads):
                body(h, h)
            return

        def step(i, carry):
            for slot in range(together):
                body(i * together + slot, slot)
            return carry

        lax.fori_loop(0, self.heads // together, step, 0)


def lanes(h):
    if isinstance(h, int):
        return slice(h * HEAD_DIM, (h + 1) * HEAD_DIM)
    return pl.ds(pl.multiple_of(h * HEAD_DIM, HEAD_DIM), HEAD_DIM)


def own_lanes(meta, heads, h):
    return pl.ds(pl.multiple_of((meta[0] * heads + h) * HEAD_DIM, HEAD_DIM), HEAD_DIM)


def member_rows(meta, off, heads, branch, h, taken, shift=0):
    start = off[branch - 1, meta[1] + meta[0] * heads + h]
    return pl.ds(start + shift, taken, stride=2**branch)


def halves_body(plan, count, meta, off, *refs):
    ins, out, sems = refs[:count], refs[count], refs[count + 1]
    other = pl.ds(pl.multiple_of((1 - meta[0]) * plan.width, plan.width), plan.width)
    copies = [pltpu.make_async_copy(ref.at[:, other], out.at[i], sems.at[i]) for i, ref in enumerate(ins)]
    for copy in copies:
        copy.start()
    for copy in copies:
        copy.wait()


def halves(plan, blocks):
    count = len(blocks)
    out = jax.ShapeDtypeStruct((count, plan.rows, plan.width), blocks[0].dtype)
    return plan.call(
        functools.partial(halves_body, plan, count),
        [pltpu.with_memory_space_constraint(x, pltpu.HBM) for x in blocks],
        [out],
        [pltpu.SemaphoreType.DMA((count,))],
        name="halves",
        in_place=pltpu.HBM,
    )[0]


def pick_body(plan, count, first, meta, off, *refs):
    owns, got, outs, scratch = refs[:count], refs[count], refs[count + 1 : count + 4], refs[-1]
    heads, rows = plan.heads, plan.rows

    def one(h, slot):
        for i in range(count):
            scratch[slot, 2 * i] = owns[i][:, own_lanes(meta, heads, h)].astype(f32)
            scratch[slot, 2 * i + 1] = got[first + i, :, lanes(h)].astype(f32)
        for branch, out in zip(FAR, outs):
            taken = plan.taken(branch)
            where = member_rows(meta, off, heads, branch, h, taken)
            for i in range(count):
                picked = [scratch[slot, 2 * i + seg, where, :] for seg in range(2)]
                out[0, i, h] = jnp.concatenate(picked, axis=0).astype(bf16)

    plan.each_head(4, one)


def pick(plan, owns, got, first):
    count = len(owns)
    outs = [
        jax.ShapeDtypeStruct((1, count, plan.heads, 2 * plan.taken(b), HEAD_DIM), bf16) for b in FAR
    ]
    return plan.call(
        functools.partial(pick_body, plan, count, first),
        [*owns, got],
        outs,
        [pltpu.VMEM((4, 2 * count, plan.rows, HEAD_DIM), f32)],
        name="pick",
    )


def near_forward_body(plan, together, meta, off, qo, ko, vo, kv_got, q_got, out, lse, wide_in, acc, acc_l):
    heads, rows, taken = plan.heads, plan.rows, plan.taken(1)

    def one(h, slot):
        mine = own_lanes(meta, heads, h)
        seg_in = (
            (qo[:, mine], ko[:, mine], vo[:, mine]),
            (q_got[0, :, lanes(h)], kv_got[0, :, lanes(h)], kv_got[1, :, lanes(h)]),
        )
        for seg in range(2):
            for i in range(3):
                wide_in[slot, 2 * i + seg] = seg_in[seg][i].astype(f32)
        where = member_rows(meta, off, heads, 1, h, taken)
        near = []
        for i in range(3):
            picked = [wide_in[slot, 2 * i + seg, where, :] for seg in range(2)]
            near.append(jnp.concatenate(picked, axis=0).astype(bf16))
        for seg in range(2):
            o, l2 = attend(*seg_in[seg])
            acc[slot, seg] = o
            acc_l[slot, seg] = l2
        o, l2 = attend(*near)
        for seg in range(2):
            part = slice(seg * taken, (seg + 1) * taken)
            new_o, new_l = merged(
                acc[slot, seg, where, :], acc_l[slot, seg, where, :], o[part], l2[part]
            )
            acc[slot, seg, where, :] = new_o
            acc_l[slot, seg, where, :] = new_l
        for seg in range(2):
            part = slice(seg * rows, (seg + 1) * rows)
            out[h, part, :] = acc[slot, seg]
            lse[h, part, :] = acc_l[slot, seg]

    plan.each_head(together, one)


def near_forward(plan, q, k, v, kv_got, q_got):
    rows, heads = plan.rows, plan.heads
    together = 2
    out = jax.ShapeDtypeStruct((heads, 2 * rows, HEAD_DIM), f32)
    pair = pltpu.VMEM((together, 2, rows, HEAD_DIM), f32)
    return plan.call(
        functools.partial(near_forward_body, plan, together),
        [q, k, v, kv_got, q_got],
        [out, out],
        [pltpu.VMEM((together, 6, rows, HEAD_DIM), f32), pair, pair],
        name="near_forward",
    )


class Rows(NamedTuple):
    array: jax.Array
    start: int
    count: int


def whole_rows(array):
    return Rows(array, 0, array.shape[3])


def extents(pieces):
    return [(p.array.shape[0], p.start, p.count) for p in pieces]


def gathered(refs, layout, which, h):
    parts = []
    for ref, (many, start, count) in zip(refs, layout, strict=True):
        for n in range(many):
            parts.append(ref[n, which, h, start : start + count, :])
    return jnp.concatenate(parts, axis=0)


def far_forward_body(plan, layout, meta, off, q, *refs):
    pieces, out, lse = refs[:-2], refs[-2], refs[-1]

    def one(h, slot):
        o, l2 = attend(q[0, 0, h], gathered(pieces, layout, 0, h), gathered(pieces, layout, 1, h))
        out[h] = o
        lse[h] = l2

    plan.each_head(4, one)


def far_forward(plan, branch, q, pieces):
    rows, heads = 2 * plan.taken(branch), plan.heads
    outs = [jax.ShapeDtypeStruct((heads, rows, HEAD_DIM), f32)] * 2
    return plan.call(
        functools.partial(far_forward_body, plan, extents(pieces)),
        [q, *[p.array for p in pieces]],
        outs,
        name=f"far_forward{branch}",
    )


def combine_body(plan, meta, off, *refs):
    near_o, near_l, far, (so, co, sc_got, gain) = refs[0], refs[1], refs[2:8], refs[8:12]
    attn, lse, stats, pre_all, g_all = refs[12:]
    rows, heads = plan.rows, plan.heads

    def one(h, slot):
        mine = own_lanes(meta, heads, h)
        attn[h] = near_o[h]
        lse[h] = near_l[h]
        for i, branch in enumerate(FAR):
            taken = plan.taken(branch)
            for seg in range(2):
                where = member_rows(meta, off, heads, branch, h, taken, seg * rows)
                part = slice(seg * taken, (seg + 1) * taken)
                new_o, new_l = merged(
                    attn[h, where, :], lse[h, where, :], far[2 * i][h, part], far[2 * i + 1][h, part]
                )
                attn[h, where, :] = new_o
                lse[h, where, :] = new_l
        scale = gain[:, mine]
        res = (so[:, mine], sc_got[1, :, lanes(h)])
        cot = (co[:, mine], sc_got[2, :, lanes(h)])
        for seg in range(2):
            part = slice(seg * rows, (seg + 1) * rows)
            pre_all[h, part, :] = alpha_res * res[seg].astype(f32) + attn[h, part, :]
            g_all[h, part, :] = cot[seg].astype(f32) * scale

    plan.each_head(2, one)

    def total(i, acc):
        return acc + pre_all[i]

    for seg in range(2):
        part = slice(seg * rows, (seg + 1) * rows)
        acc = pre_all[0, part, :]
        for i in range(1, heads):
            acc = acc + pre_all[i, part, :]
        pre_sum = jnp.sum(acc, axis=1, keepdims=True)
        centre = pre_sum / (heads * HEAD_DIM)
        second = jnp.zeros((rows, HEAD_DIM), f32)
        g_sum, cross = second, second
        for i in range(heads):
            diff = pre_all[i, part, :] - centre
            g = g_all[i, part, :]
            second, g_sum, cross = second + diff * diff, g_sum + g, cross + g * diff
        lane = lax.broadcasted_iota(jnp.int32, (rows, HEAD_DIM), 1)
        table = jnp.broadcast_to(pre_sum, (rows, HEAD_DIM))
        for i, x in enumerate((second, g_sum, cross)):
            table = jnp.where(lane == i + 1, jnp.sum(x, axis=1, keepdims=True), table)
        stats[:, part] = jnp.transpose(table)[:STAT_ROWS]


def combine(plan, near, far, stream, cot, sc_got, gain):
    rows, heads = plan.rows, plan.heads
    per_head = jax.ShapeDtypeStruct((heads, 2 * rows, HEAD_DIM), f32)
    outs = [per_head, per_head, jax.ShapeDtypeStruct((STAT_ROWS, 2 * rows), f32)]
    return plan.call(
        functools.partial(combine_body, plan),
        [*near, *[x for pair in far for x in pair], stream, cot, sc_got, gain],
        outs,
        [pltpu.VMEM((heads, 2 * rows, HEAD_DIM), f32)] * 2,
        name="combine",
    )


def joined(mine, other, count):
    gap = (mine[0:1] - other[0:1]) / count
    return [
        mine[0:1] + other[0:1],
        mine[1:2] + other[1:2] + gap * gap * (count / 2),
        mine[2:3] + other[2:3],
        mine[3:4] + other[3:4] + gap * 0.5 * (mine[2:3] - other[2:3]),
    ]


def join_body(rows, count, swap, meta, off, mine, other, out):
    theirs = other[...]
    if swap:
        theirs = jnp.concatenate([theirs[:, rows:], theirs[:, :rows]], axis=1)
    for i, row in enumerate(joined(mine[...], theirs, count)):
        out[i : i + 1, :] = row


def join(plan, mine, other, count, swap=False):
    return plan.call(
        functools.partial(join_body, plan.rows, count, swap),
        [mine, other],
        [jax.ShapeDtypeStruct(mine.shape, f32)],
        name="join",
    )[0]


def relay_body(meta, off, three, four, four_far, both, for_z):
    both[0:1] = four[...]
    both[1:2] = four_far[...]
    place = 0
    for ref in (three, four, four_far):
        rows = ref.shape[3]
        for c in range(ref.shape[1]):
            for h in range(ref.shape[2]):
                for_z[0, c, h, place : place + rows, :] = ref[0, c, h]
        place += rows


def relay(plan, three, four, four_far, wait_for):
    _, tensors, heads, rows, width = four.shape
    sd = jax.ShapeDtypeStruct
    outs = [
        sd((2, tensors, heads, rows, width), four.dtype),
        sd((1, tensors, heads, three.shape[3] + 2 * rows, width), four.dtype),
    ]
    return plan.call(relay_body, [three, four, four_far], outs, name="relay", wait_for=wait_for)


def split_rows(lse, delta):
    high = lse.astype(bf16).astype(f32)
    mid = (lse - high).astype(bf16).astype(f32)
    low = lse - high - mid
    delta_high = delta.astype(bf16).astype(f32)
    delta_low = delta - delta_high
    return jnp.concatenate(
        [high, mid, low, delta_high, delta_low] + [jnp.zeros_like(lse)] * (STAT_ROWS - 5), axis=0
    ).astype(bf16)


def norm_body(plan, full_width, together, meta, off, *refs):
    stats, stats_got, attn, lse, so, co, sc_got, gain, bias = refs[:9]
    q_far = refs[9:12]
    n_own, n_send, da_out, delta_out, m2, m3, m4, cols, da_wide, delta_wide = refs[12:]
    rows, heads = plan.rows, plan.heads
    st = joined(stats[...], stats_got[...], full_width // 2)
    centre = st[0] / full_width
    inv = 1.0 / jnp.sqrt(st[1] / full_width + eps_norm)
    for i, row in enumerate((centre, inv, st[2] / full_width, st[3] * inv / full_width)):
        cols[i] = jnp.transpose(jnp.broadcast_to(row, (HEAD_DIM, 2 * rows)))

    def one(h, slot):
        mine = own_lanes(meta, heads, h)
        scale, shift = gain[:, mine], bias[:, mine]
        res = (so[:, mine], sc_got[1, :, lanes(h)])
        cot = (co[:, mine], sc_got[2, :, lanes(h)])
        for seg in range(2):
            part = slice(seg * rows, (seg + 1) * rows)
            att = attn[h, part, :]
            inv_col = cols[1, part, :]
            normed = (alpha_res * res[seg].astype(f32) + att - cols[0, part, :]) * inv_col
            if seg == 0:
                n_own[:, lanes(h)] = (scale * normed + shift).astype(bf16)
            else:
                n_send[h] = (scale * normed + shift).astype(bf16)
            g = cot[seg].astype(f32) * scale
            da = (inv_col * (g - cols[2, part, :] - normed * cols[3, part, :])).astype(bf16)
            da_out[h, part, :] = da
            da_f = da.astype(f32)
            da_wide[slot, part, :] = da_f
            delta = jnp.broadcast_to(jnp.sum(da_f * att, axis=1, keepdims=True), (rows, HEAD_DIM))
            delta_wide[slot, part, :] = delta
            delta_out[h, part, :] = delta
        for branch, msg, q_rows in zip(FAR, (m2, m3, m4), q_far):
            taken = plan.taken(branch)
            where = [member_rows(meta, off, heads, branch, h, taken, seg * rows) for seg in range(2)]
            picked = jnp.concatenate([da_wide[slot, w, :] for w in where], axis=0)
            msg[0, 0, h, : 2 * taken, :] = picked.astype(bf16)
            pad = [jnp.zeros((HEAD_DIM - 2 * taken, HEAD_DIM), f32)] if 2 * taken < HEAD_DIM else []
            lse_rows = jnp.concatenate([lse[h, w, :] for w in where] + pad, axis=0)
            delta_rows = jnp.concatenate([delta_wide[slot, w, :] for w in where] + pad, axis=0)
            msg[0, 0, h, 2 * taken + STAT_ROWS :, :] = q_rows[0, 0, h]
            msg[0, 0, h, 2 * taken : 2 * taken + STAT_ROWS, :] = split_rows(
                jnp.transpose(lse_rows)[0:1], jnp.transpose(delta_rows)[0:1]
            )

    plan.each_head(together, one)


def norm(plan, full_width, stats, stats_got, attn, lse, stream, cot, sc_got, gain, bias, q_far):
    rows, heads = plan.rows, plan.heads
    sd = jax.ShapeDtypeStruct
    together = 2
    outs = [
        sd((rows, plan.width), bf16),
        sd((heads, rows, HEAD_DIM), bf16),
        sd((heads, 2 * rows, HEAD_DIM), bf16),
        sd((heads, 2 * rows, HEAD_DIM), f32),
    ] + [sd((1, 1, heads, 4 * plan.taken(b) + STAT_ROWS, HEAD_DIM), bf16) for b in FAR]
    wide_rows = pltpu.VMEM((together, 2 * rows, HEAD_DIM), f32)
    return plan.call(
        functools.partial(norm_body, plan, full_width, together),
        [stats, stats_got, attn, lse, stream, cot, sc_got, gain, bias, *q_far],
        outs,
        [pltpu.VMEM((4, 2 * rows, HEAD_DIM), f32), wide_rows, wide_rows],
        name="norm",
    )


def dscores(query, key, value, grad, lse, delta):
    reach = key.shape[0] // HEAD_DIM
    probs = jnp.exp2(dot_nt(query, key) * scaling2 - wide(lse, reach))
    dprob = dot_nt(grad, value)
    return probs.astype(bf16), (probs * (dprob - wide(delta, reach))).astype(bf16)


def near_backward_body(plan, layouts, first_head, count, meta, off, *refs):
    counts = [len(x) for x in layouts]
    qo, ko, vo, kv_got, q_got, da, lse, delta = refs[:8]
    pieces = refs[8 : 8 + sum(counts)]
    own, *sends, wide_in, sums = refs[-6:]
    rows, heads = plan.rows, plan.heads

    def one(i, slot):
        h = first_head + i
        mine = own_lanes(meta, heads, h)
        seg_in = (
            (qo[:, mine], ko[:, mine], vo[:, mine], da[h, :rows, :]),
            (q_got[0, :, lanes(h)], kv_got[0, :, lanes(h)], kv_got[1, :, lanes(h)], da[h, rows:, :]),
        )
        for seg in range(2):
            for t in range(4):
                wide_in[slot, 2 * t + seg] = seg_in[seg][t].astype(f32)
        for seg in range(2):
            part = slice(seg * rows, (seg + 1) * rows)
            q, k, v, grad = seg_in[seg]
            probs, ds = dscores(q, k, v, grad, lse[h, part, :], delta[h, part, :])
            sums[slot, 0, part, :] = dot_nn(ds, k)
            sums[slot, 1, part, :] = dot_tn(ds, q)
            sums[slot, 2, part, :] = dot_tn(probs, grad)
        for branch in range(1, BRANCHES + 1):
            taken = plan.taken(branch)
            inside = member_rows(meta, off, heads, branch, h, taken)
            where = [member_rows(meta, off, heads, branch, h, taken, seg * rows) for seg in range(2)]

            def member(t):
                picked = [wide_in[slot, 2 * t + seg, inside, :] for seg in range(2)]
                return jnp.concatenate(picked, axis=0).astype(bf16)

            query, grad = member(0), member(3)
            lse_rows = jnp.concatenate([lse[h, w, :] for w in where], axis=0)
            delta_rows = jnp.concatenate([delta[h, w, :] for w in where], axis=0)
            if branch == 1:
                key, value = member(1), member(2)
            else:
                first = sum(counts[: branch - 2])
                far = pieces[first : first + counts[branch - 2]]
                layout = layouts[branch - 2]
                key, value = gathered(far, layout, 0, h), gathered(far, layout, 1, h)
            probs, ds = dscores(query, key, value, grad, lse_rows, delta_rows)
            grads = [dot_nn(ds, key)]
            if branch == 1:
                grads += [dot_tn(ds, query), dot_tn(probs, grad)]
            for t, rows_new in enumerate(grads):
                for seg in range(2):
                    sums[slot, t, where[seg], :] = (
                        sums[slot, t, where[seg], :] + rows_new[seg * taken : (seg + 1) * taken]
                    )
        for t, scale in enumerate((scaling, scaling, None)):
            both = sums[slot, t]
            both = both if scale is None else both * scale
            own[t, h] = both[:rows]
            sends[t][h] = both[rows:].astype(bf16)

    together = min(2, count)

    def step(i, carry):
        for slot in range(together):
            one(i * together + slot, slot)
        return carry

    lax.fori_loop(0, count // together, step, 0)


def near_backward(plan, first_head, count, ins, pieces, before=(), wait_for=()):
    shape = (plan.heads, plan.rows, HEAD_DIM)
    flat = [*ins, *[x.array for p in pieces for x in p]]
    return plan.call(
        functools.partial(near_backward_body, plan, [extents(p) for p in pieces], first_head, count),
        [*flat, *before],
        [jax.ShapeDtypeStruct((3, *shape), f32)] + [jax.ShapeDtypeStruct(shape, bf16)] * 3,
        [pltpu.VMEM((2, 8, plan.rows, HEAD_DIM), f32), pltpu.VMEM((2, 3, 2 * plan.rows, HEAD_DIM), f32)],
        name=f"near_backward{first_head}",
        aliases={len(flat) + 2 + i: i for i in range(len(before))},
        wait_for=wait_for,
    )


def far_backward_body(plan, branches, layouts, meta, off, *refs):
    counts = [len(x) for x in layouts]
    kvs, msgs, (own, send) = refs[: len(branches)], refs[len(branches) : -2], refs[-2:]

    def one(h, slot):
        row = 0
        for j, branch in enumerate(branches):
            taken = plan.taken(branch)
            grads, queries, halves_of = [], [], [None] * (plan.rows // HEAD_DIM)
            place = 0
            mine = msgs[sum(counts[:j]) : sum(counts[: j + 1])]
            for ref, (many, start, _) in zip(mine, layouts[j], strict=True):
                table_at = start + 2 * taken
                for n in range(many):
                    grads.append(ref[n, 0, h, start:table_at, :])
                    queries.append(ref[n, 0, h, table_at + STAT_ROWS : table_at + STAT_ROWS + 2 * taken, :])
                    terms = ref[n, 0, h, table_at : table_at + STAT_ROWS, :].astype(f32)
                    half, shift = divmod(place, HEAD_DIM)
                    if shift:
                        terms = pltpu.roll(terms, shift, 1)
                    halves_of[half] = terms if halves_of[half] is None else halves_of[half] + terms
                    place += 2 * taken
            grad = jnp.concatenate(grads, axis=0)
            query = jnp.concatenate(queries, axis=0)
            table = jnp.concatenate(halves_of, axis=1)
            lse = table[0:1] + table[1:2] + table[2:3]
            delta = table[3:4] + table[4:5]
            key, value = kvs[j][0, 0, h], kvs[j][0, 1, h]
            probs = jnp.exp2(dot_nt(key, query) * scaling2 - lse)
            ds = (probs * (dot_nt(value, grad) - delta)).astype(bf16)
            dkey = dot_nn(ds, query) * scaling
            dvalue = dot_nn(probs.astype(bf16), grad)
            for i, rows in enumerate((dkey, dvalue)):
                own[i, h, row : row + taken, :] = rows[:taken]
                send[i, h, row : row + taken, :] = rows[taken:].astype(bf16)
            row += taken

    plan.each_head(4, one)


def far_backward(plan, branches, kvs, pieces, wait_for=()):
    shape = (2, plan.heads, sum(plan.taken(b) for b in branches), HEAD_DIM)
    return plan.call(
        functools.partial(far_backward_body, plan, branches, [extents(p) for p in pieces]),
        [*kvs, *[x.array for p in pieces for x in p]],
        [jax.ShapeDtypeStruct(shape, f32), jax.ShapeDtypeStruct(shape, bf16)],
        name=f"far_backward{branches[0]}",
        wait_for=wait_for,
    )


def column_of(plan, meta, slot):
    heads = plan.heads
    core = meta[0] if slot < heads else 1 - meta[0]
    return core * heads + slot % heads


def column_lanes(plan, meta, slot):
    return pl.ds(pl.multiple_of(column_of(plan, meta, slot) * HEAD_DIM, HEAD_DIM), HEAD_DIM)


def finish_q_body(plan, meta, off, own, got, n_own, n_got, dq, normed, mark, wide_got, sems):
    copies = []

    def send(src, dst):
        copy = pltpu.make_async_copy(src, dst, sems.at[len(copies)])
        copy.start()
        copies.append(copy)

    mine = pl.ds(pl.multiple_of(meta[0] * plan.width, plan.width), plan.width)
    send(n_own, normed.at[:, mine])
    for i in range(plan.heads):
        theirs = column_lanes(plan, meta, plan.heads + i)
        send(own.at[0, i], dq.at[:, column_lanes(plan, meta, i)])
        send(n_got.at[i], normed.at[:, theirs])
        wide_got[i] = got[i].astype(f32)
        send(wide_got.at[i], dq.at[:, theirs])
    for copy in copies:
        copy.wait()
    mark[...] = jnp.zeros_like(mark)


def finish_q(plan, own, got, n_own, n_got):
    full = (plan.rows, 2 * plan.width)
    return plan.call(
        functools.partial(finish_q_body, plan),
        [own, got, n_own, n_got],
        [
            jax.ShapeDtypeStruct(full, f32),
            jax.ShapeDtypeStruct(full, bf16),
            jax.ShapeDtypeStruct((8, HEAD_DIM), f32),
        ],
        [
            pltpu.VMEM((plan.heads, plan.rows, HEAD_DIM), f32),
            pltpu.SemaphoreType.DMA((3 * plan.heads + 1,)),
        ],
        name="finish_q",
        out_place=[pltpu.HBM, pltpu.HBM, pltpu.VMEM],
    )


def fold_body(plan, branches, meta, off, *refs):
    own, got, row_refs, sums = refs[0], refs[1:3], refs[3:5], refs[5]
    for slot in range(2 * plan.heads):
        side, h = divmod(slot, plan.heads)
        for t in range(2):
            sums[t, slot] = own[1 + t, h] if side == 0 else got[t][h].astype(f32)
        row = 0
        for branch in branches:
            taken = plan.taken(branch)
            start = off[branch - 1, meta[1] + column_of(plan, meta, slot)]
            where = pl.ds(start, taken, stride=2**branch)
            for t in range(2):
                rows = row_refs[side][t, h, row : row + taken, :].astype(f32)
                sums[t, slot, where, :] = sums[t, slot, where, :] + rows
            row += taken


def fold(plan, branches, own, got, rows_own, rows_got):
    shape = (2, 2 * plan.heads, plan.rows, HEAD_DIM)
    return plan.call(
        functools.partial(fold_body, plan, branches),
        [own, *got, rows_own, rows_got],
        [jax.ShapeDtypeStruct(shape, f32)],
        name="fold",
    )[0]


def finish_kv_body(plan, branch, meta, off, given, own, got, dk, dv, sums, sems):
    copies = []
    for slot in range(2 * plan.heads):
        taken = plan.taken(branch)
        start = off[branch - 1, meta[1] + column_of(plan, meta, slot)]
        where = pl.ds(start, taken, stride=2**branch)
        rows = (own, got)[slot // plan.heads]
        for t, out in enumerate((dk, dv)):
            sums[t, slot] = given[t, slot]
            sums[t, slot, where, :] = given[t, slot, where, :] + rows[t, slot % plan.heads].astype(f32)
            copy = pltpu.make_async_copy(
                sums.at[t, slot], out.at[:, column_lanes(plan, meta, slot)], sems.at[len(copies)]
            )
            copy.start()
            copies.append(copy)
    for copy in copies:
        copy.wait()


def finish_kv(plan, branch, sums, own, got):
    full = jax.ShapeDtypeStruct((plan.rows, 2 * plan.width), f32)
    return plan.call(
        functools.partial(finish_kv_body, plan, branch),
        [sums, own, got],
        [full, full],
        [pltpu.VMEM(sums.shape, f32), pltpu.SemaphoreType.DMA((4 * plan.heads,))],
        name="finish_kv",
        out_place=pltpu.HBM,
    )


def gather(plan, msgs, filler, last_filler=None):
    two, three, four = msgs
    four_far, three_y, three_z = flip(four, "seq", 8), flip(three, "seq", 2), flip(three, "seq", 4)
    two_y = flip(two, "seq", 2)
    both, for_z = relay(plan, three_y, four, four_far, [filler(), three_z])
    four_y, from_z = flip(both, "seq", 2), flip(for_z, "seq", 4)
    four_yz = flip(last_filler(four_y, both) if last_filler else four_y, "seq", 4)
    rows_three, rows_four = three.shape[3], four.shape[3]
    from_z_four = [Rows(from_z, rows_three + i * rows_four, rows_four) for i in range(2)]
    return (
        [whole_rows(x) for x in (two, two_y)],
        [whole_rows(x) for x in (three, three_y, three_z)] + [Rows(from_z, 0, rows_three)],
        [whole_rows(x) for x in (four, four_far, four_y)] + from_z_four + [whole_rows(four_yz)],
    )


def shards(queries, key_rows, value_rows, stream, norm_gain, norm_bias, head_offsets, cotangent):
    rows = queries.shape[0]
    heads_here = queries.shape[1] // HEAD_DIM
    half = queries.shape[1] // 2
    core = lax.axis_index("seq") & 1
    first_head = lax.axis_index("head") * heads_here
    meta = jnp.stack([core, first_head]).astype(jnp.int32)
    plan = Plan(rows, heads_here, meta, head_offsets)
    gain, bias = norm_gain[None, :], norm_bias[None, :]

    kv_got = flip(halves(plan, [key_rows, value_rows]), "seq", 1)
    qsc_got = flip(halves(plan, [queries, stream, cotangent]), "seq", 1)
    kv_far = pick(plan, [key_rows, value_rows], kv_got, 0)
    near = near_forward(plan, queries, key_rows, value_rows, kv_got, qsc_got)
    kv_pieces = gather(plan, kv_far, lambda: near[1])
    q_far = pick(plan, [queries], qsc_got, 0)
    far = [far_forward(plan, b, q_far[b - 2], kv_pieces[b - 2]) for b in FAR]
    attn, lse, stats = combine(plan, near, far, stream, cotangent, qsc_got, gain)

    stats = join(plan, stats, flip(stats, "seq", 1), half, swap=True)
    width, mask = 4 * half, 1
    while 2 * mask < lax.axis_size("head"):
        stats = join(plan, stats, flip(stats, "head", mask), width // 2)
        width, mask = 2 * width, 2 * mask
    n_own, n_send, da, delta, *msgs = norm(
        plan,
        width,
        stats,
        flip(stats, "head", mask),
        attn,
        lse,
        stream,
        cotangent,
        qsc_got,
        gain,
        bias,
        q_far,
    )

    n_got = flip(n_send, "seq", 1)
    ins = [queries, key_rows, value_rows, kv_got, qsc_got, da, lse, delta]
    first = max(1, plan.heads // 4)
    parts = []

    def near_first():
        parts.append(near_backward(plan, 0, first, ins, kv_pieces))
        return parts[-1][0]

    def near_rest(four_y, both):
        own, *sends = near_backward(
            plan, first, plan.heads - first, ins, kv_pieces, parts[-1], wait_for=[both, n_got]
        )
        four_y, own = lax.optimization_barrier((four_y, own))
        parts.append((own, *sends))
        return four_y

    msg_pieces = gather(plan, msgs, near_first, near_rest)
    own, *sends = parts[-1]
    got_q, *got_kv = [flip(send, "seq", 1) for send in sends]
    grad_query, normed_out, mark = finish_q(plan, own, got_q, n_own, n_got)
    rows_own, rows_send = far_backward(plan, FAR[:-1], kv_far[:-1], msg_pieces[:-1], [own])
    sums = fold(plan, FAR[:-1], own, got_kv, rows_own, flip(rows_send, "seq", 1))
    rows_own, rows_send = far_backward(plan, FAR[-1:], kv_far[-1:], msg_pieces[-1:], [mark, sums])
    grad_key, grad_value = finish_kv(plan, FAR[-1], sums, rows_own, flip(rows_send, "seq", 1))
    return normed_out, grad_query, grad_key, grad_value


def solution(mesh):
    return jax.shard_map(
        shards,
        mesh=mesh,
        in_specs=(
            P("seq", "head"),
            P("seq", "head"),
            P("seq", "head"),
            P("seq", "head"),
            P("head"),
            P("head"),
            P(),
            P("seq", "head"),
        ),
        out_specs=(P("seq", "head"), P("seq", "head"), P("seq", "head"), P("seq", "head")),
        check_vma=False,
    )
```

time: 353 us -> 112 us (0.32); the launches traced: 346 us -> 112 us
  local copies, waits for them, and re-layouts: 92.4 us -> 0.73 us
  other arithmetic: 90.7 us -> 0.08 us
  Pallas kernels: 0 us -> 52.1 us
  matrix products: 50.5 us -> 0 us
  waiting for transfers between devices: 76.6 us -> 31 us
  blocking collectives: 14.9 us -> 0 us
  starting transfers between devices: 17.9 us -> 27.1 us
    pallas_call x0 -> x20, Pallas kernels: none -> 52.1 us  [call(): pl.pallas_call(without_waited if waited else body, out_shape=outs, in_spe...]
    dot_general x30 -> x0, matrix products: 50.5 us -> none  [the longest x5 10.8 us: backward_block(): jnp.einsum('qhe,khe->hqk', grad_rows, value_set, preferred_element_type=j...]
    ppermute x20 -> x24, waiting for transfers between devices: 76.6 us -> 31 us  [flip(): return lax.ppermute(block, axis, [(i, i ^ mask) for i in range(count)])]
    reduce_sum x21 -> x0, other arithmetic: 38.6 us -> none  [the longest x12 15.2 us: pick_rows(): jnp.sum(jnp.where(member, shaped, jnp.zeros((), source.dtype)), axis=1)]
    broadcast_in_dim x60 -> x0, local copies, waits for them, and re-layouts: 30.9 us -> none  [the longest x52 24 us: place_rows(): jnp.where(member, piece_rows[:, None], jnp.asarray(filler, piece_rows.dty...]
    add x12 -> x0, other arithmetic: 23.5 us -> none  [the longest x1 15.7 us: shards(): grad_value + place_rows(returned[branch - 1][1], stride, offsets_now, 0.0)]
    select_n x10 -> x0, other arithmetic: 17.5 us -> none  [grow_group(): jnp.where(upper_side(seq_index, section), jnp.concatenate([other, current...]
    unnamed x253 -> x18, local copies, waits for them, and re-layouts: 17 us -> 0.73 us
  transfers between devices with their start and end apart: 20 -> 24, of which waited for: 7 -> 12; matrix products, arithmetic and copies ran while one was open for 30% -> 0% of each run, Pallas kernels for 0% -> 31%
where the time goes in v1:
time: 112 us
  Pallas kernels  52.1 us (47%)
  waiting for transfers between devices  31 us (28%)
  starting transfers between devices  27.1 us (24%)
    pallas_call x20, Pallas kernels, call(): pl.pallas_call(without_waited if waited else body, out_shape=outs, in_spe...  52.1 us
    ppermute x24, waiting for transfers between devices, flip(): return lax.ppermute(block, axis, [(i, i ^ mask) for i in range(count)])  31 us
    ppermute x24, starting transfers between devices, flip(): return lax.ppermute(block, axis, [(i, i ^ mask) for i in range(count)])  27.1 us
  transfers between devices with their start and end apart: 24, of which 12 were waited for; matrix products, arithmetic and copies ran while one was open for 0% of the time, Pallas kernels for 31%

profile of v1, /device:TPU:0, one launch (start us, length us, event | category | flops | bytes accessed | tf_op | source)
XLA Modules:
  0.0 112.2 jit_solution(10401146959110857533)
XLA Ops:
  0.6 0.1 pad_add_fusion.meta.refs_0_
  0.7 0.7 copy-done.5
  1.4 2.0 %halves.3 = bf16[3,256,1024]{2,1,0:T(8,128)(2,1)S(1)} custom-call(s32[2]{0:T(128)S(1)} %pad_add_fusion.meta.refs_0_, s32[4,32]{1,0:T(4,128)S(1)} %copy-done.5, bf16[256,2048]{1,0:T(8,128)(2,1)} %refs_2_.5, bf16[256,2048]{1,0:T(8,128)(2,1)} %refs_4_.2, bf16[256,2048]{1,0:T(8,128)(2,1)} %refs_5_.1), custom_call_target="tpu_custom_call" | custom-call | tf_op jit(solution)/shard_map/halves/pallas_call | solution.py:99
  3.4 0.0 copy-start
  3.4 0.0 copy-start.1
  3.4 0.0 copy-start.6
  3.4 0.6 collective-permute-start.1
  4.0 1.8 %halves.2 = bf16[2,256,1024]{2,1,0:T(8,128)(2,1)S(1)} custom-call(s32[2]{0:T(128)S(1)} %pad_add_fusion.meta.refs_0_, s32[4,32]{1,0:T(4,128)S(1)} %copy-done.5, bf16[256,2048]{1,0:T(8,128)(2,1)} %refs_3_.1, bf16[256,2048]{1,0:T(8,128)(2,1)} %refs_4_.3), custom_call_target="tpu_custom_call" | custom-call | tf_op jit(solution)/shard_map/halves/pallas_call | solution.py:99
  5.7 0.0 copy-start.2
  5.8 0.1 collective-permute-start
  5.8 2.6 %collective-permute-done.kv_got.refs_2_.refs_3_.refs_5_ = bf16[2,256,1024]{2,1,0:T(8,128)(2,1)S(1)} collective-permute-done((bf16[2,256,1024]{2,1,0:T(8,128)(2,1)S(1)}, bf16[2,256,1024]{2,1,0:T(8,128)(2,1)S(1)}, u32[]{:S(2)}, u32[]{:S(2)}) %collective-permute-start) | collective-permute-done | bytes 1048608 | tf_op jit(solution)/shard_map/ppermute | solution.py:40
  8.5 1.6 %pick.3 = (bf16[1,2,8,128,128]{4,3,2,1,0:T(8,128)(2,1)S(1)}, bf16[1,2,8,64,128]{4,3,2,1,0:T(8,128)(2,1)S(1)}, bf16[1,2,8,32,128]{4,3,2,1,0:T(8,128)(2,1)S(1)}) custom-call(s32[2]{0:T(128)S(1)} %pad_add_fusion.meta.refs_0_, s32[4,32]{1,0:T(4,128)S(1)} %copy-done.6, bf16[256,2048]{1,0:T(8,128)(2,1)S(1)} %copy-done, bf16[256,2048]{1,0:T(8,128)(2,1)S(1)} %copy-done.1, ...), custom_call_target="tpu_custom_call" | custom-call | tf_op jit(solution)/shard_map/pick/pallas_call | solution.py:99
  10.1 2.9 %collective-permute-start.3 = (bf16[1,2,8,64,128]{4,3,2,1,0:T(8,128)(2,1)S(1)}, bf16[1,2,8,64,128]{4,3,2,1,0:T(8,128)(2,1)S(1)}, u32[]{:S(2)}, u32[]{:S(2)}) collective-permute-start(bf16[1,2,8,64,128]{4,3,2,1,0:T(8,128)(2,1)S(1)} %get-tuple-element.58.refs_0_.refs_10_.refs_12_.refs_3_), channel_id=1, source_target_pairs={{0,4},{2,6},{4,0},{6,2},{8,12},{10,14},{12,8},{14,10},{16,20},{18,... | collective-permute-start | bytes 786440 | tf_op jit(solution)/shard_map/ppermute | solution.py:40
  13.0 1.6 %collective-permute-start.4 = (bf16[1,2,8,64,128]{4,3,2,1,0:T(8,128)(2,1)S(1)}, bf16[1,2,8,64,128]{4,3,2,1,0:T(8,128)(2,1)S(1)}, u32[]{:S(2)}, u32[]{:S(2)}) collective-permute-start(bf16[1,2,8,64,128]{4,3,2,1,0:T(8,128)(2,1)S(1)} %get-tuple-element.58.refs_0_.refs_10_.refs_12_.refs_3_), channel_id=1, source_target_pairs={{0,8},{2,10},{4,12},{6,14},{8,0},{10,2},{12,4},{14,6},{16,24},{18,... | collective-permute-start | bytes 786440 | tf_op jit(solution)/shard_map/ppermute | solution.py:40
  14.6 2.6 %collective-permute-start.5 = (bf16[1,2,8,32,128]{4,3,2,1,0:T(8,128)(2,1)S(1)}, bf16[1,2,8,32,128]{4,3,2,1,0:T(8,128)(2,1)S(1)}, u32[]{:S(2)}, u32[]{:S(2)}) collective-permute-start(bf16[1,2,8,32,128]{4,3,2,1,0:T(8,128)(2,1)S(1)} %get-tuple-element.59.refs_3_.refs_0_.refs_14_.refs_16_.refs_2_), channel_id=1, source_target_pairs={{0,16},{2,18},{4,20},{6,22},{8,24},{10,26},{12,28},{14,30},{16,0},... | collective-permute-start | bytes 393224 | tf_op jit(solution)/shard_map/ppermute | solution.py:40
  17.2 0.5 collective-permute-start.2
  17.7 4.9 %near_forward.1 = (f32[8,512,128]{2,1,0:T(8,128)S(1)}, f32[8,512,128]{2,1,0:T(8,128)S(1)}) custom-call(s32[2]{0:T(128)S(1)} %pad_add_fusion.meta.refs_0_, s32[4,32]{1,0:T(4,128)S(1)} %copy-done.6, bf16[256,2048]{1,0:T(8,128)(2,1)S(1)} %copy-done.2, bf16[256,2048]{1,0:T(8,128)(2,1)S(1)} %copy-done, bf16[256,2048]{1,0:T(8,128)(2,1)S(1)} %copy-done.1, ...), custom_call_target="tpu_custom_call" | custom-call | tf_op jit(solution)/shard_map/near_forward/pallas_call | solution.py:99
  22.6 0.3 collective-permute-done.5.refs_4_.refs_1_.refs_15_.refs_17_
  23.0 0.9 collective-permute-done.4.refs_6_.refs_2_.refs_12_.refs_14_
  23.9 0.7 relay.2
  24.5 2.7 %collective-permute-start.6 = (bf16[1,2,8,128,128]{4,3,2,1,0:T(8,128)(2,1)S(1)}, bf16[1,2,8,128,128]{4,3,2,1,0:T(8,128)(2,1)S(1)}, u32[]{:S(2)}, u32[]{:S(2)}) collective-permute-start(bf16[1,2,8,128,128]{4,3,2,1,0:T(8,128)(2,1)S(1)} %get-tuple-element.60), channel_id=1, source_target_pairs={{0,8},{2,10},{4,12},{6,14},{8,0},{10,2},{12,4},{14,6},{16,24},{18,... | collective-permute-start | bytes 1572872 | tf_op jit(solution)/shard_map/ppermute | solution.py:40
  27.2 0.5 collective-permute-start.7
  27.7 8.8 %collective-permute-done.7.refs_2_.refs_16_.refs_18_ = bf16[2,2,8,32,128]{4,3,2,1,0:T(8,128)(2,1)S(1)} collective-permute-done((bf16[2,2,8,32,128]{4,3,2,1,0:T(8,128)(2,1)S(1)}, bf16[2,2,8,32,128]{4,3,2,1,0:T(8,128)(2,1)S(1)}, u32[]{:S(2)}, u32[]{:S(2)}) %collective-permute-start.7) | collective-permute-done | bytes 262176 | tf_op jit(solution)/shard_map/ppermute | solution.py:40
  36.5 1.8 %collective-permute-start.8 = (bf16[2,2,8,32,128]{4,3,2,1,0:T(8,128)(2,1)S(1)}, bf16[2,2,8,32,128]{4,3,2,1,0:T(8,128)(2,1)S(1)}, u32[]{:S(2)}, u32[]{:S(2)}) collective-permute-start(bf16[2,2,8,32,128]{4,3,2,1,0:T(8,128)(2,1)S(1)} %collective-permute-done.7.refs_2_.refs_16_.refs_18_), channel_id=1, source_target_pairs={{0,8},{2,10},{4,12},{6,14},{8,0},{10,2},{12,4},{14,6},{16,24},{18,... | collective-permute-start | bytes 786440 | tf_op jit(solution)/shard_map/ppermute | solution.py:40
  38.3 1.1 pick.2
  39.3 0.0 copy-start.3
  39.4 0.0 copy-start.4
  39.4 0.0 copy-start.7
  39.4 1.6 %far_forward2.1 = (f32[8,128,128]{2,1,0:T(8,128)S(1)}, f32[8,128,128]{2,1,0:T(8,128)S(1)}) custom-call(s32[2]{0:T(128)S(1)} %pad_add_fusion.meta.refs_0_, s32[4,32]{1,0:T(4,128)S(1)} %copy-done.6, bf16[1,1,8,128,128]{4,3,2,1,0:T(8,128)(2,1)S(1)} %get-tuple-element.53.q.refs_9_, ...), custom_call_target="tpu_custom_call" | custom-call | tf_op jit(solution)/shard_map/far_forward2/pallas_call | solution.py:99
  41.0 1.6 %far_forward3.1 = (f32[8,64,128]{2,1,0:T(8,128)S(1)}, f32[8,64,128]{2,1,0:T(8,128)S(1)}) custom-call(s32[2]{0:T(128)S(1)} %pad_add_fusion.meta.refs_0_, s32[4,32]{1,0:T(4,128)S(1)} %copy-done.6, bf16[1,1,8,64,128]{4,3,2,1,0:T(8,128)(2,1)S(1)} %get-tuple-element.57.q.refs_10_, ...), custom_call_target="tpu_custom_call" | custom-call | tf_op jit(solution)/shard_map/far_forward3/pallas_call | solution.py:99
  42.5 1.5 %collective-permute-done.8.refs_5_.refs_19_.refs_21_ = bf16[2,2,8,32,128]{4,3,2,1,0:T(8,128)(2,1)S(1)} collective-permute-done((bf16[2,2,8,32,128]{4,3,2,1,0:T(8,128)(2,1)S(1)}, bf16[2,2,8,32,128]{4,3,2,1,0:T(8,128)(2,1)S(1)}, u32[]{:S(2)}, u32[]{:S(2)}) %collective-permute-start.8) | collective-permute-done | bytes 262176 | tf_op jit(solution)/shard_map/ppermute | solution.py:40
  44.0 1.5 %far_forward4.1 = (f32[8,32,128]{2,1,0:T(8,128)S(1)}, f32[8,32,128]{2,1,0:T(8,128)S(1)}) custom-call(s32[2]{0:T(128)S(1)} %pad_add_fusion.meta.refs_0_, s32[4,32]{1,0:T(4,128)S(1)} %copy-done.6, bf16[1,1,8,32,128]{4,3,2,1,0:T(8,128)(2,1)S(1)} %get-tuple-element.63.q.refs_11_, ...), custom_call_target="tpu_custom_call" | custom-call | tf_op jit(solution)/shard_map/far_forward4/pallas_call | solution.py:99
  45.6 0.0 copy-start.8
  45.6 3.6 %combine.1 = (f32[8,512,128]{2,1,0:T(8,128)S(1)}, f32[8,512,128]{2,1,0:T(8,128)S(1)}, f32[8,512]{1,0:T(8,128)S(1)}) custom-call(s32[2]{0:T(128)S(1)} %pad_add_fusion.meta.refs_0_, s32[4,32]{1,0:T(4,128)S(1)} %copy-done.6, f32[8,512,128]{2,1,0:T(8,128)S(1)} %get-tuple-element.51.refs_0_, f32[8,512,128]{2,1,0:T(8,128)S(1)} %get-tuple-element.52.refs_5_.refs_1_, ...), custom_call_target="tpu_custom_call" | custom-call | tf_op jit(solution)/shard_map/combine/pallas_call | solution.py:99
  49.2 0.0 collective-permute-start.9
  49.3 1.2 %collective-permute-done.9.other = f32[8,512]{1,0:T(8,128)S(1)} collective-permute-done((f32[8,512]{1,0:T(8,128)S(1)}, f32[8,512]{1,0:T(8,128)S(1)}, u32[]{:S(2)}, u32[]{:S(2)}) %collective-permute-start.9) | collective-permute-done | bytes 16416 | tf_op jit(solution)/shard_map/ppermute | solution.py:40
  50.4 0.6 join.1.refs_0_
  51.0 1.7 %collective-permute-start.10 = (f32[8,512]{1,0:T(8,128)S(1)}, f32[8,512]{1,0:T(8,128)S(1)}, u32[]{:S(2)}, u32[]{:S(2)}) collective-permute-start(f32[8,512]{1,0:T(8,128)S(1)} %join.1.refs_0_), channel_id=1, source_target_pairs={{0,1},{1,0},{2,3},{3,2},{4,5},{5,4},{6,7},{7,6},{8,9},{9,8},{10,11... | collective-permute-start | bytes 49160 | tf_op jit(solution)/shard_map/ppermute | solution.py:40
  52.7 2.1 %collective-permute-done.10.refs_1_ = f32[8,512]{1,0:T(8,128)S(1)} collective-permute-done((f32[8,512]{1,0:T(8,128)S(1)}, f32[8,512]{1,0:T(8,128)S(1)}, u32[]{:S(2)}, u32[]{:S(2)}) %collective-permute-start.10) | collective-permute-done | bytes 16416 | tf_op jit(solution)/shard_map/ppermute | solution.py:40
  54.8 4.1 %norm.1 = (bf16[256,1024]{1,0:T(8,128)(2,1)S(1)}, bf16[8,256,128]{2,1,0:T(8,128)(2,1)S(1)}, bf16[8,512,128]{2,1,0:T(8,128)(2,1)S(1)}, f32[8,512,128]{2,1,0:T(8,1...) custom-call(s32[2]{0:T(128)S(1)} %pad_add_fusion.meta.refs_0_, ...), custom_call_target="tpu_custom_call" | custom-call | tf_op jit(solution)/shard_map/norm/pallas_call | solution.py:99
  59.0 1.8 %collective-permute-start.11 = (bf16[1,1,8,136,128]{4,3,2,1,0:T(8,128)(2,1)S(1)}, bf16[1,1,8,136,128]{4,3,2,1,0:T(8,128)(2,1)S(1)}, u32[]{:S(2)}, u32[]{:S(2)}) collective-permute-start(bf16[1,1,8,136,128]{4,3,2,1,0:T(8,128)(2,1)S(1)} %get-tuple-element.70.refs_6_), channel_id=1, source_target_pairs={{0,4},{2,6},{4,0},{6,2},{8,12},{10,14},{12,8},{14,10},{16,20},{18,... | collective-permute-start | bytes 835592 | tf_op jit(solution)/shard_map/ppermute | solution.py:40
  60.7 1.6 %collective-permute-start.13 = (bf16[1,1,8,136,128]{4,3,2,1,0:T(8,128)(2,1)S(1)}, bf16[1,1,8,136,128]{4,3,2,1,0:T(8,128)(2,1)S(1)}, u32[]{:S(2)}, u32[]{:S(2)}) collective-permute-start(bf16[1,1,8,136,128]{4,3,2,1,0:T(8,128)(2,1)S(1)} %get-tuple-element.70.refs_6_), channel_id=1, source_target_pairs={{0,8},{2,10},{4,12},{6,14},{8,0},{10,2},{12,4},{14,6},{16,24},{18,... | collective-permute-start | bytes 835592 | tf_op jit(solution)/shard_map/ppermute | solution.py:40
  62.3 2.6 %collective-permute-start.12 = (bf16[1,1,8,72,128]{4,3,2,1,0:T(8,128)(2,1)S(1)}, bf16[1,1,8,72,128]{4,3,2,1,0:T(8,128)(2,1)S(1)}, u32[]{:S(2)}, u32[]{:S(2)}) collective-permute-start(bf16[1,1,8,72,128]{4,3,2,1,0:T(8,128)(2,1)S(1)} %get-tuple-element.71.refs_3_), channel_id=1, source_target_pairs={{0,16},{2,18},{4,20},{6,22},{8,24},{10,26},{12,28},{14,30},{16,0},... | collective-permute-start | bytes 442376 | tf_op jit(solution)/shard_map/ppermute | solution.py:40
  64.9 3.8 %near_backward0.1 = (f32[3,8,256,128]{3,2,1,0:T(8,128)S(1)}, bf16[8,256,128]{2,1,0:T(8,128)(2,1)S(1)}, bf16[8,256,128]{2,1,0:T(8,128)(2,1)S(1)}, bf16[8,256,128]{2,1,0:T(8,128)(2,1)S(1)}) custom-call(s32[2]{0:T(128)S(1)} %pad_add_fusion.meta.refs_0_, s32[4,32]{1,0:T(4,128)S(1)} %copy-done.6, bf16[256,2048]{1,0:T(8,128)(2,1)S(1)} %copy-done.2, ...), custom_call_target="tpu_custom_call" | custom-call | tf_op jit(solution)/shard_map/near_backward0/pallas_call | solution.py:99
  68.7 1.6 %collective-permute-done.12.refs_4_ = bf16[1,1,8,72,128]{4,3,2,1,0:T(8,128)(2,1)S(1)} collective-permute-done((bf16[1,1,8,72,128]{4,3,2,1,0:T(8,128)(2,1)S(1)}, bf16[1,1,8,72,128]{4,3,2,1,0:T(8,128)(2,1)S(1)}, u32[]{:S(2)}, u32[]{:S(2)}) %collective-permute-start.12) | collective-permute-done | bytes 147488 | tf_op jit(solution)/shard_map/ppermute | solution.py:40
  70.3 0.9 collective-permute-done.13.refs_6_.refs_8_
  71.2 0.6 relay.3
  71.8 2.7 %collective-permute-start.20 = (bf16[1,1,8,280,128]{4,3,2,1,0:T(8,128)(2,1)S(1)}, bf16[1,1,8,280,128]{4,3,2,1,0:T(8,128)(2,1)S(1)}, u32[]{:S(2)}, u32[]{:S(2)}) collective-permute-start(bf16[1,1,8,280,128]{4,3,2,1,0:T(8,128)(2,1)S(1)} %get-tuple-element.89), channel_id=1, source_target_pairs={{0,8},{2,10},{4,12},{6,14},{8,0},{10,2},{12,4},{14,6},{16,24},{18,... | collective-permute-start | bytes 1720328 | tf_op jit(solution)/shard_map/ppermute | solution.py:40
  74.5 0.5 collective-permute-start.19
  75.0 1.5 %collective-permute-start.14 = (bf16[2,1,8,72,128]{4,3,2,1,0:T(8,128)(2,1)S(1)}, bf16[2,1,8,72,128]{4,3,2,1,0:T(8,128)(2,1)S(1)}, u32[]{:S(2)}, u32[]{:S(2)}) collective-permute-start(bf16[2,1,8,72,128]{4,3,2,1,0:T(8,128)(2,1)S(1)} %get-tuple-element.75.refs_26_), channel_id=1, source_target_pairs={{0,4},{2,6},{4,0},{6,2},{8,12},{10,14},{12,8},{14,10},{16,20},{18,... | collective-permute-start | bytes 884744 | tf_op jit(solution)/shard_map/ppermute | solution.py:40
  76.5 10.3 %near_backward2.1 = (f32[3,8,256,128]{3,2,1,0:T(8,128)S(1)}, bf16[8,256,128]{2,1,0:T(8,128)(2,1)S(1)}, bf16[8,256,128]{2,1,0:T(8,128)(2,1)S(1)}, bf16[8,256,128]{2,1,0:T(8,128)(2,1)S(1)}) custom-call(s32[2]{0:T(128)S(1)} %pad_add_fusion.meta.refs_0_, ...), custom_call_target="tpu_custom_call", output_to_operand_aliasing={{0}: (22, {}), {1}: (23, {}), {2}: (24, {}), {3}: (25, {})} | custom-call | tf_op jit(solution)/shard_map/near_backward2/pallas_call | solution.py:99
  86.8 0.1 collective-permute-start.16
  86.8 0.5 collective-permute-start.17
  87.3 4.9 %collective-permute-done.14.refs_5_ = bf16[2,1,8,72,128]{4,3,2,1,0:T(8,128)(2,1)S(1)} collective-permute-done((bf16[2,1,8,72,128]{4,3,2,1,0:T(8,128)(2,1)S(1)}, bf16[2,1,8,72,128]{4,3,2,1,0:T(8,128)(2,1)S(1)}, u32[]{:S(2)}, u32[]{:S(2)}) %collective-permute-start.14) | collective-permute-done | bytes 294944 | tf_op jit(solution)/shard_map/ppermute | solution.py:40
  92.3 3.8 %far_backward2.1 = (f32[2,8,96,128]{3,2,1,0:T(8,128)S(1)}, bf16[2,8,96,128]{3,2,1,0:T(8,128)(2,1)S(1)}) custom-call(s32[2]{0:T(128)S(1)} %pad_add_fusion.meta.refs_0_, s32[4,32]{1,0:T(4,128)S(1)} %copy-done.6, bf16[1,2,8,128,128]{4,3,2,1,0:T(8,128)(2,1)S(1)} %get-tuple-element.54.refs_0_.refs_8_.refs_10_.refs_2_, ...), custom_call_target="tpu_custom_call" | custom-call | tf_op jit(solution)/shard_map/far_backward2/pallas_call | solution.py:99
  96.1 0.6 collective-permute-start.21
  96.7 0.4 collective-permute-start.22
  97.1 2.4 %finish_q.1 = (f32[256,2048]{1,0:T(8,128)}, bf16[256,2048]{1,0:T(8,128)(2,1)}, f32[8,128]{1,0:T(8,128)S(1)}) custom-call(s32[2]{0:T(128)S(1)} %pad_add_fusion.meta.refs_0_, s32[4,32]{1,0:T(4,128)S(1)} %copy-done.6, f32[3,8,256,128]{3,2,1,0:T(8,128)S(1)} %get-tuple-element.81.own.refs_10_.refs_0_, bf16[8,256,128]{2,1,0:T(8,128)(2,1)S(1)} %collective-permute-done.16.got, ...), custom_call_target="tpu_custom_call" | custom-call | tf_op jit(solution)/shard_map/finish_q/pallas_call | solution.py:99
  99.5 1.2 %fold.1.refs_10_.given = f32[2,16,256,128]{3,2,1,0:T(8,128)S(1)} custom-call(s32[2]{0:T(128)S(1)} %pad_add_fusion.meta.refs_0_, s32[4,32]{1,0:T(4,128)S(1)} %copy-done.6, f32[3,8,256,128]{3,2,1,0:T(8,128)S(1)} %get-tuple-element.81.own.refs_10_.refs_0_, bf16[8,256,128]{2,1,0:T(8,128)(2,1)S(1)} %collective-permute-done.17.refs_1_, ...), custom_call_target="tpu_custom_call" | custom-call | tf_op jit(solution)/shard_map/fold/pallas_call | solution.py:99
  100.8 4.9 %collective-permute-done.22.refs_8_ = bf16[2,1,8,72,128]{4,3,2,1,0:T(8,128)(2,1)S(1)} collective-permute-done((bf16[2,1,8,72,128]{4,3,2,1,0:T(8,128)(2,1)S(1)}, bf16[2,1,8,72,128]{4,3,2,1,0:T(8,128)(2,1)S(1)}, u32[]{:S(2)}, u32[]{:S(2)}) %collective-permute-start.22) | collective-permute-done | bytes 294944 | tf_op jit(solution)/shard_map/ppermute | solution.py:40
  105.7 2.1 %far_backward4.1 = (f32[2,8,16,128]{3,2,1,0:T(8,128)S(1)}, bf16[2,8,16,128]{3,2,1,0:T(8,128)(2,1)S(1)}) custom-call(s32[2]{0:T(128)S(1)} %pad_add_fusion.meta.refs_0_, s32[4,32]{1,0:T(4,128)S(1)} %copy-done.6, bf16[1,2,8,32,128]{4,3,2,1,0:T(8,128)(2,1)S(1)} %get-tuple-element.59.refs_3_.refs_0_.refs_14_.refs_16_.refs_2_, ...), custom_call_target="tpu_custom_call" | custom-call | tf_op jit(solution)/shard_map/far_backward4/pallas_call | solution.py:99
  107.8 0.1 collective-permute-start.23
  107.9 1.2 %collective-permute-done.23.got = bf16[2,8,16,128]{3,2,1,0:T(8,128)(2,1)S(1)} collective-permute-done((bf16[2,8,16,128]{3,2,1,0:T(8,128)(2,1)S(1)}, bf16[2,8,16,128]{3,2,1,0:T(8,128)(2,1)S(1)}, u32[]{:S(2)}, u32[]{:S(2)}) %collective-permute-start.23) | collective-permute-done | bytes 65568 | tf_op jit(solution)/shard_map/ppermute | solution.py:40
  109.1 2.9 %finish_kv.1 = (f32[256,2048]{1,0:T(8,128)}, f32[256,2048]{1,0:T(8,128)}) custom-call(s32[2]{0:T(128)S(1)} %pad_add_fusion.meta.refs_0_, s32[4,32]{1,0:T(4,128)S(1)} %copy-done.6, f32[2,16,256,128]{3,2,1,0:T(8,128)S(1)} %fold.1.refs_10_.given, f32[2,8,16,128]{3,2,1,0:T(8,128)S(1)} %get-tuple-element.94.own, ...), custom_call_target="tpu_custom_call" | custom-call | tf_op jit(solution)/shard_map/finish_kv/pallas_call | solution.py:99
  (23 shorter events, 0.1 us)
Async XLA Ops:
  0.7 0.7 copy-start.5
  3.4 5.1 %copy-start = (bf16[256,2048]{1,0:T(8,128)(2,1)S(1)}, bf16[256,2048]{1,0:T(8,128)(2,1)}, u32[]{:S(2)}) copy-start(bf16[256,2048]{1,0:T(8,128)(2,1)} %refs_3_.1) | copy-start | bytes 3145732
  3.4 5.1 %copy-start.1 = (bf16[256,2048]{1,0:T(8,128)(2,1)S(1)}, bf16[256,2048]{1,0:T(8,128)(2,1)}, u32[]{:S(2)}) copy-start(bf16[256,2048]{1,0:T(8,128)(2,1)} %refs_4_.3) | copy-start | bytes 3145732
  3.4 5.1 %copy-start.6 = (s32[4,32]{1,0:T(4,128)S(1)}, s32[4,32]{1,0:T(4,128)}, u32[]{:S(2)}) copy-start(s32[4,32]{1,0:T(4,128)} %off.29) | copy-start | bytes 1540
  3.4 14.3 %collective-permute-start.1 = (bf16[3,256,1024]{2,1,0:T(8,128)(2,1)S(1)}, bf16[3,256,1024]{2,1,0:T(8,128)(2,1)S(1)}, u32[]{:S(2)}, u32[]{:S(2)}) collective-permute-start(bf16[3,256,1024]{2,1,0:T(8,128)(2,1)S(1)} %halves.3), channel_id=1, source_target_pairs={{0,2},{2,0},{4,6},{6,4},{8,10},{10,8},{12,14},{14,12},{16,18},{18,... | collective-permute-start | bytes 4718600 | tf_op jit(solution)/shard_map/ppermute | solution.py:40
  5.7 11.9 %copy-start.2 = (bf16[256,2048]{1,0:T(8,128)(2,1)S(1)}, bf16[256,2048]{1,0:T(8,128)(2,1)}, u32[]{:S(2)}) copy-start(bf16[256,2048]{1,0:T(8,128)(2,1)} %refs_2_.5) | copy-start | bytes 3145732
  5.8 2.7 %collective-permute-start = (bf16[2,256,1024]{2,1,0:T(8,128)(2,1)S(1)}, bf16[2,256,1024]{2,1,0:T(8,128)(2,1)S(1)}, u32[]{:S(2)}, u32[]{:S(2)}) collective-permute-start(bf16[2,256,1024]{2,1,0:T(8,128)(2,1)S(1)} %halves.2), channel_id=1, source_target_pairs={{0,2},{2,0},{4,6},{6,4},{8,10},{10,8},{12,14},{14,12},{16,18},{18,... | collective-permute-start | bytes 3145736 | tf_op jit(solution)/shard_map/ppermute | solution.py:40
  10.1 12.9 %collective-permute-start.3 = (bf16[1,2,8,64,128]{4,3,2,1,0:T(8,128)(2,1)S(1)}, bf16[1,2,8,64,128]{4,3,2,1,0:T(8,128)(2,1)S(1)}, u32[]{:S(2)}, u32[]{:S(2)}) collective-permute-start(bf16[1,2,8,64,128]{4,3,2,1,0:T(8,128)(2,1)S(1)} %get-tuple-element.58.refs_0_.refs_10_.refs_12_.refs_3_), channel_id=1, source_target_pairs={{0,4},{2,6},{4,0},{6,2},{8,12},{10,14},{12,8},{14,10},{16,20},{18,... | collective-permute-start | bytes 786440 | tf_op jit(solution)/shard_map/ppermute | solution.py:40
  13.0 10.9 %collective-permute-start.4 = (bf16[1,2,8,64,128]{4,3,2,1,0:T(8,128)(2,1)S(1)}, bf16[1,2,8,64,128]{4,3,2,1,0:T(8,128)(2,1)S(1)}, u32[]{:S(2)}, u32[]{:S(2)}) collective-permute-start(bf16[1,2,8,64,128]{4,3,2,1,0:T(8,128)(2,1)S(1)} %get-tuple-element.58.refs_0_.refs_10_.refs_12_.refs_3_), channel_id=1, source_target_pairs={{0,8},{2,10},{4,12},{6,14},{8,0},{10,2},{12,4},{14,6},{16,24},{18,... | collective-permute-start | bytes 786440 | tf_op jit(solution)/shard_map/ppermute | solution.py:40
  14.6 8.4 %collective-permute-start.5 = (bf16[1,2,8,32,128]{4,3,2,1,0:T(8,128)(2,1)S(1)}, bf16[1,2,8,32,128]{4,3,2,1,0:T(8,128)(2,1)S(1)}, u32[]{:S(2)}, u32[]{:S(2)}) collective-permute-start(bf16[1,2,8,32,128]{4,3,2,1,0:T(8,128)(2,1)S(1)} %get-tuple-element.59.refs_3_.refs_0_.refs_14_.refs_16_.refs_2_), channel_id=1, source_target_pairs={{0,16},{2,18},{4,20},{6,22},{8,24},{10,26},{12,28},{14,30},{16,0},... | collective-permute-start | bytes 393224 | tf_op jit(solution)/shard_map/ppermute | solution.py:40
  17.2 22.2 %collective-permute-start.2 = (bf16[1,2,8,128,128]{4,3,2,1,0:T(8,128)(2,1)S(1)}, bf16[1,2,8,128,128]{4,3,2,1,0:T(8,128)(2,1)S(1)}, u32[]{:S(2)}, u32[]{:S(2)}) collective-permute-start(bf16[1,2,8,128,128]{4,3,2,1,0:T(8,128)(2,1)S(1)} %get-tuple-element.54.refs_0_.refs_8_.refs_10_.refs_2_), channel_id=1, source_target_pairs={{0,4},{2,6},{4,0},{6,2},{8,12},{10,14},{12,8},{14,10},{16,20},{18,... | collective-permute-start | bytes 1572872 | tf_op jit(solution)/shard_map/ppermute | solution.py:40
  24.5 16.4 %collective-permute-start.6 = (bf16[1,2,8,128,128]{4,3,2,1,0:T(8,128)(2,1)S(1)}, bf16[1,2,8,128,128]{4,3,2,1,0:T(8,128)(2,1)S(1)}, u32[]{:S(2)}, u32[]{:S(2)}) collective-permute-start(bf16[1,2,8,128,128]{4,3,2,1,0:T(8,128)(2,1)S(1)} %get-tuple-element.60), channel_id=1, source_target_pairs={{0,8},{2,10},{4,12},{6,14},{8,0},{10,2},{12,4},{14,6},{16,24},{18,... | collective-permute-start | bytes 1572872 | tf_op jit(solution)/shard_map/ppermute | solution.py:40
  27.2 9.3 %collective-permute-start.7 = (bf16[2,2,8,32,128]{4,3,2,1,0:T(8,128)(2,1)S(1)}, bf16[2,2,8,32,128]{4,3,2,1,0:T(8,128)(2,1)S(1)}, u32[]{:S(2)}, u32[]{:S(2)}) collective-permute-start(bf16[2,2,8,32,128]{4,3,2,1,0:T(8,128)(2,1)S(1)} %get-tuple-element.64), channel_id=1, source_target_pairs={{0,4},{2,6},{4,0},{6,2},{8,12},{10,14},{12,8},{14,10},{16,20},{18,... | collective-permute-start | bytes 786440 | tf_op jit(solution)/shard_map/ppermute | solution.py:40
  36.5 7.5 %collective-permute-start.8 = (bf16[2,2,8,32,128]{4,3,2,1,0:T(8,128)(2,1)S(1)}, bf16[2,2,8,32,128]{4,3,2,1,0:T(8,128)(2,1)S(1)}, u32[]{:S(2)}, u32[]{:S(2)}) collective-permute-start(bf16[2,2,8,32,128]{4,3,2,1,0:T(8,128)(2,1)S(1)} %collective-permute-done.7.refs_2_.refs_16_.refs_18_), channel_id=1, source_target_pairs={{0,8},{2,10},{4,12},{6,14},{8,0},{10,2},{12,4},{14,6},{16,24},{18,... | collective-permute-start | bytes 786440 | tf_op jit(solution)/shard_map/ppermute | solution.py:40
  39.3 6.2 %copy-start.3 = (bf16[256,2048]{1,0:T(8,128)(2,1)S(1)}, bf16[256,2048]{1,0:T(8,128)(2,1)}, u32[]{:S(2)}) copy-start(bf16[256,2048]{1,0:T(8,128)(2,1)} %refs_4_.2) | copy-start | bytes 3145732
  39.4 6.2 %copy-start.4 = (bf16[256,2048]{1,0:T(8,128)(2,1)S(1)}, bf16[256,2048]{1,0:T(8,128)(2,1)}, u32[]{:S(2)}) copy-start(bf16[256,2048]{1,0:T(8,128)(2,1)} %refs_5_.1) | copy-start | bytes 3145732
  39.4 6.2 %copy-start.7 = (f32[2048]{0:T(1024)S(1)}, f32[2048]{0:T(1024)}, u32[]{:S(2)}) copy-start(f32[2048]{0:T(1024)} %param.12) | copy-start | bytes 24580
  45.6 9.3 %copy-start.8 = (f32[2048]{0:T(1024)S(1)}, f32[2048]{0:T(1024)}, u32[]{:S(2)}) copy-start(f32[2048]{0:T(1024)} %param.13) | copy-start | bytes 24580
  49.2 1.2 %collective-permute-start.9 = (f32[8,512]{1,0:T(8,128)S(1)}, f32[8,512]{1,0:T(8,128)S(1)}, u32[]{:S(2)}, u32[]{:S(2)}) collective-permute-start(f32[8,512]{1,0:T(8,128)S(1)} %get-tuple-element.67.mine), channel_id=1, source_target_pairs={{0,2},{2,0},{4,6},{6,4},{8,10},{10,8},{12,14},{14,12},{16,18},{18,... | collective-permute-start | bytes 49160 | tf_op jit(solution)/shard_map/ppermute | solution.py:40
  51.0 3.8 %collective-permute-start.10 = (f32[8,512]{1,0:T(8,128)S(1)}, f32[8,512]{1,0:T(8,128)S(1)}, u32[]{:S(2)}, u32[]{:S(2)}) collective-permute-start(f32[8,512]{1,0:T(8,128)S(1)} %join.1.refs_0_), channel_id=1, source_target_pairs={{0,1},{1,0},{2,3},{3,2},{4,5},{5,4},{6,7},{7,6},{8,9},{9,8},{10,11... | collective-permute-start | bytes 49160 | tf_op jit(solution)/shard_map/ppermute | solution.py:40
  59.0 11.3 %collective-permute-start.11 = (bf16[1,1,8,136,128]{4,3,2,1,0:T(8,128)(2,1)S(1)}, bf16[1,1,8,136,128]{4,3,2,1,0:T(8,128)(2,1)S(1)}, u32[]{:S(2)}, u32[]{:S(2)}) collective-permute-start(bf16[1,1,8,136,128]{4,3,2,1,0:T(8,128)(2,1)S(1)} %get-tuple-element.70.refs_6_), channel_id=1, source_target_pairs={{0,4},{2,6},{4,0},{6,2},{8,12},{10,14},{12,8},{14,10},{16,20},{18,... | collective-permute-start | bytes 835592 | tf_op jit(solution)/shard_map/ppermute | solution.py:40
  60.7 10.4 %collective-permute-start.13 = (bf16[1,1,8,136,128]{4,3,2,1,0:T(8,128)(2,1)S(1)}, bf16[1,1,8,136,128]{4,3,2,1,0:T(8,128)(2,1)S(1)}, u32[]{:S(2)}, u32[]{:S(2)}) collective-permute-start(bf16[1,1,8,136,128]{4,3,2,1,0:T(8,128)(2,1)S(1)} %get-tuple-element.70.refs_6_), channel_id=1, source_target_pairs={{0,8},{2,10},{4,12},{6,14},{8,0},{10,2},{12,4},{14,6},{16,24},{18,... | collective-permute-start | bytes 835592 | tf_op jit(solution)/shard_map/ppermute | solution.py:40
  62.3 8.0 %collective-permute-start.12 = (bf16[1,1,8,72,128]{4,3,2,1,0:T(8,128)(2,1)S(1)}, bf16[1,1,8,72,128]{4,3,2,1,0:T(8,128)(2,1)S(1)}, u32[]{:S(2)}, u32[]{:S(2)}) collective-permute-start(bf16[1,1,8,72,128]{4,3,2,1,0:T(8,128)(2,1)S(1)} %get-tuple-element.71.refs_3_), channel_id=1, source_target_pairs={{0,16},{2,18},{4,20},{6,22},{8,24},{10,26},{12,28},{14,30},{16,0},... | collective-permute-start | bytes 442376 | tf_op jit(solution)/shard_map/ppermute | solution.py:40
  64.9 11.6 %collective-permute-start.15 = (bf16[8,256,128]{2,1,0:T(8,128)(2,1)S(1)}, bf16[8,256,128]{2,1,0:T(8,128)(2,1)S(1)}, u32[]{:S(2)}, u32[]{:S(2)}) collective-permute-start(bf16[8,256,128]{2,1,0:T(8,128)(2,1)S(1)} %get-tuple-element.79), channel_id=1, source_target_pairs={{0,2},{2,0},{4,6},{6,4},{8,10},{10,8},{12,14},{14,12},{16,18},{18,... | collective-permute-start | bytes 1572872 | tf_op jit(solution)/shard_map/ppermute | solution.py:40
  71.8 20.5 %collective-permute-start.20 = (bf16[1,1,8,280,128]{4,3,2,1,0:T(8,128)(2,1)S(1)}, bf16[1,1,8,280,128]{4,3,2,1,0:T(8,128)(2,1)S(1)}, u32[]{:S(2)}, u32[]{:S(2)}) collective-permute-start(bf16[1,1,8,280,128]{4,3,2,1,0:T(8,128)(2,1)S(1)} %get-tuple-element.89), channel_id=1, source_target_pairs={{0,8},{2,10},{4,12},{6,14},{8,0},{10,2},{12,4},{14,6},{16,24},{18,... | collective-permute-start | bytes 1720328 | tf_op jit(solution)/shard_map/ppermute | solution.py:40
  74.5 17.8 %collective-permute-start.19 = (bf16[1,1,8,264,128]{4,3,2,1,0:T(8,128)(2,1)S(1)}, bf16[1,1,8,264,128]{4,3,2,1,0:T(8,128)(2,1)S(1)}, u32[]{:S(2)}, u32[]{:S(2)}) collective-permute-start(bf16[1,1,8,264,128]{4,3,2,1,0:T(8,128)(2,1)S(1)} %get-tuple-element.88.refs_4_), channel_id=1, source_target_pairs={{0,4},{2,6},{4,0},{6,2},{8,12},{10,14},{12,8},{14,10},{16,20},{18,... | collective-permute-start | bytes 1622024 | tf_op jit(solution)/shard_map/ppermute | solution.py:40
  75.0 17.3 %collective-permute-start.14 = (bf16[2,1,8,72,128]{4,3,2,1,0:T(8,128)(2,1)S(1)}, bf16[2,1,8,72,128]{4,3,2,1,0:T(8,128)(2,1)S(1)}, u32[]{:S(2)}, u32[]{:S(2)}) collective-permute-start(bf16[2,1,8,72,128]{4,3,2,1,0:T(8,128)(2,1)S(1)} %get-tuple-element.75.refs_26_), channel_id=1, source_target_pairs={{0,4},{2,6},{4,0},{6,2},{8,12},{10,14},{12,8},{14,10},{16,20},{18,... | collective-permute-start | bytes 884744 | tf_op jit(solution)/shard_map/ppermute | solution.py:40
  86.8 10.3 %collective-permute-start.16 = (bf16[8,256,128]{2,1,0:T(8,128)(2,1)S(1)}, bf16[8,256,128]{2,1,0:T(8,128)(2,1)S(1)}, u32[]{:S(2)}, u32[]{:S(2)}) collective-permute-start(bf16[8,256,128]{2,1,0:T(8,128)(2,1)S(1)} %get-tuple-element.82), channel_id=1, source_target_pairs={{0,2},{2,0},{4,6},{6,4},{8,10},{10,8},{12,14},{14,12},{16,18},{18,... | collective-permute-start | bytes 1572872 | tf_op jit(solution)/shard_map/ppermute | solution.py:40
  86.8 12.7 %collective-permute-start.17 = (bf16[8,256,128]{2,1,0:T(8,128)(2,1)S(1)}, bf16[8,256,128]{2,1,0:T(8,128)(2,1)S(1)}, u32[]{:S(2)}, u32[]{:S(2)}) collective-permute-start(bf16[8,256,128]{2,1,0:T(8,128)(2,1)S(1)} %get-tuple-element.86), channel_id=1, source_target_pairs={{0,2},{2,0},{4,6},{6,4},{8,10},{10,8},{12,14},{14,12},{16,18},{18,... | collective-permute-start | bytes 1572872 | tf_op jit(solution)/shard_map/ppermute | solution.py:40
  92.2 7.3 %collective-permute-start.18 = (bf16[8,256,128]{2,1,0:T(8,128)(2,1)S(1)}, bf16[8,256,128]{2,1,0:T(8,128)(2,1)S(1)}, u32[]{:S(2)}, u32[]{:S(2)}) collective-permute-start(bf16[8,256,128]{2,1,0:T(8,128)(2,1)S(1)} %get-tuple-element.87), channel_id=1, source_target_pairs={{0,2},{2,0},{4,6},{6,4},{8,10},{10,8},{12,14},{14,12},{16,18},{18,... | collective-permute-start | bytes 1572872 | tf_op jit(solution)/shard_map/ppermute | solution.py:40
  96.1 3.4 %collective-permute-start.21 = (bf16[2,8,96,128]{3,2,1,0:T(8,128)(2,1)S(1)}, bf16[2,8,96,128]{3,2,1,0:T(8,128)(2,1)S(1)}, u32[]{:S(2)}, u32[]{:S(2)}) collective-permute-start(bf16[2,8,96,128]{3,2,1,0:T(8,128)(2,1)S(1)} %get-tuple-element.91), channel_id=1, source_target_pairs={{0,2},{2,0},{4,6},{6,4},{8,10},{10,8},{12,14},{14,12},{16,18},{18,... | collective-permute-start | bytes 1179656 | tf_op jit(solution)/shard_map/ppermute | solution.py:40
  96.7 9.0 %collective-permute-start.22 = (bf16[2,1,8,72,128]{4,3,2,1,0:T(8,128)(2,1)S(1)}, bf16[2,1,8,72,128]{4,3,2,1,0:T(8,128)(2,1)S(1)}, u32[]{:S(2)}, u32[]{:S(2)}) collective-permute-start(bf16[2,1,8,72,128]{4,3,2,1,0:T(8,128)(2,1)S(1)} %collective-permute-done.14.refs_5_), channel_id=1, source_target_pairs={{0,8},{2,10},{4,12},{6,14},{8,0},{10,2},{12,4},{14,6},{16,24},{18,... | collective-permute-start | bytes 884744 | tf_op jit(solution)/shard_map/ppermute | solution.py:40
  107.8 1.3 %collective-permute-start.23 = (bf16[2,8,16,128]{3,2,1,0:T(8,128)(2,1)S(1)}, bf16[2,8,16,128]{3,2,1,0:T(8,128)(2,1)S(1)}, u32[]{:S(2)}, u32[]{:S(2)}) collective-permute-start(bf16[2,8,16,128]{3,2,1,0:T(8,128)(2,1)S(1)} %get-tuple-element.95), channel_id=1, source_target_pairs={{0,2},{2,0},{4,6},{6,4},{8,10},{10,8},{12,14},{14,12},{16,18},{18,... | collective-permute-start | bytes 196616 | tf_op jit(solution)/shard_map/ppermute | solution.py:40

commit v2 on v1

--- a/solution.py
+++ b/solution.py
@@ -12,7 +12,9 @@
 HEAD_DIM = 128
 BRANCHES = 4
 FAR = (2, 3, 4)
+GROUPS = ((2, 3), (4,))
 STAT_ROWS = 8
+COPIES = 4
 
 alpha_res = (2.0 * 24.0) ** 0.25
 eps_norm = 1e-05
@@ -146,22 +148,29 @@
 def halves_body(plan, count, meta, off, *refs):
     ins, out, sems = refs[:count], refs[count], refs[count + 1]
     other = pl.ds(pl.multiple_of((1 - meta[0]) * plan.width, plan.width), plan.width)
-    copies = [pltpu.make_async_copy(ref.at[:, other], out.at[i], sems.at[i]) for i, ref in enumerate(ins)]
+    step = plan.rows // COPIES
+    copies = []
+    for i, ref in enumerate(ins):
+        for j in range(COPIES):
+            rows = slice(j * step, (j + 1) * step)
+            sem = sems.at[i * COPIES + j]
+            copies.append(pltpu.make_async_copy(ref.at[rows, other], out.at[i, rows], sem))
     for copy in copies:
         copy.start()
     for copy in copies:
         copy.wait()
 
 
-def halves(plan, blocks):
+def halves(plan, blocks, wait_for=()):
     count = len(blocks)
     out = jax.ShapeDtypeStruct((count, plan.rows, plan.width), blocks[0].dtype)
     return plan.call(
         functools.partial(halves_body, plan, count),
         [pltpu.with_memory_space_constraint(x, pltpu.HBM) for x in blocks],
         [out],
-        [pltpu.SemaphoreType.DMA((count,))],
+        [pltpu.SemaphoreType.DMA((count * COPIES,))],
         name="halves",
+        wait_for=wait_for,
         in_place=pltpu.HBM,
     )[0]
 
@@ -420,8 +429,8 @@
 
 def norm_body(plan, full_width, together, meta, off, *refs):
     stats, stats_got, attn, lse, so, co, sc_got, gain, bias = refs[:9]
-    q_far = refs[9:12]
-    n_own, n_send, da_out, delta_out, m2, m3, m4, cols, da_wide, delta_wide = refs[12:]
+    q_far = (None, *refs[9:11])
+    n_own, n_send, da_out, delta_out, m2, m3, m4, cols, da_wide, delta_wide = refs[11:]
     rows, heads = plan.rows, plan.heads
     st = joined(stats[...], stats_got[...], full_width // 2)
     centre = st[0] / full_width
@@ -459,7 +468,8 @@
             pad = [jnp.zeros((HEAD_DIM - 2 * taken, HEAD_DIM), f32)] if 2 * taken < HEAD_DIM else []
             lse_rows = jnp.concatenate([lse[h, w, :] for w in where] + pad, axis=0)
             delta_rows = jnp.concatenate([delta_wide[slot, w, :] for w in where] + pad, axis=0)
-            msg[0, 0, h, 2 * taken + STAT_ROWS :, :] = q_rows[0, 0, h]
+            if q_rows is not None:
+                msg[0, 0, h, 2 * taken + STAT_ROWS :, :] = q_rows[0, 0, h]
             msg[0, 0, h, 2 * taken : 2 * taken + STAT_ROWS, :] = split_rows(
                 jnp.transpose(lse_rows)[0:1], jnp.transpose(delta_rows)[0:1]
             )
@@ -467,7 +477,7 @@
     plan.each_head(together, one)
 
 
-def norm(plan, full_width, stats, stats_got, attn, lse, stream, cot, sc_got, gain, bias, q_far):
+def norm(plan, full_width, stats, stats_got, attn, lse, stream, cot, sc_got, gain, bias, q_far, wait_for):
     rows, heads = plan.rows, plan.heads
     sd = jax.ShapeDtypeStruct
     together = 2
@@ -476,7 +486,7 @@
         sd((heads, rows, HEAD_DIM), bf16),
         sd((heads, 2 * rows, HEAD_DIM), bf16),
         sd((heads, 2 * rows, HEAD_DIM), f32),
-    ] + [sd((1, 1, heads, 4 * plan.taken(b) + STAT_ROWS, HEAD_DIM), bf16) for b in FAR]
+    ] + [sd((1, 1, heads, (2 if b == 2 else 4) * plan.taken(b) + STAT_ROWS, HEAD_DIM), bf16) for b in FAR]
     wide_rows = pltpu.VMEM((together, 2 * rows, HEAD_DIM), f32)
     return plan.call(
         functools.partial(norm_body, plan, full_width, together),
@@ -484,13 +494,13 @@
         outs,
         [pltpu.VMEM((4, 2 * rows, HEAD_DIM), f32), wide_rows, wide_rows],
         name="norm",
-    )
-
-
-def dscores(query, key, value, grad, lse, delta):
-    reach = key.shape[0] // HEAD_DIM
-    probs = jnp.exp2(dot_nt(query, key) * scaling2 - wide(lse, reach))
-    dprob = dot_nt(grad, value)
+        wait_for=wait_for,
+    )
+
+
+def probs_and_ds(scores, dprob, lse, delta):
+    reach = scores.shape[1] // HEAD_DIM
+    probs = jnp.exp2(scores * scaling2 - wide(lse, reach))
     return probs.astype(bf16), (probs * (dprob - wide(delta, reach))).astype(bf16)
 
 
@@ -501,8 +511,7 @@
     own, *sends, wide_in, sums = refs[-6:]
     rows, heads = plan.rows, plan.heads
 
-    def one(i, slot):
-        h = first_head + i
+    def load(h, slot):
         mine = own_lanes(meta, heads, h)
         seg_in = (
             (qo[:, mine], ko[:, mine], vo[:, mine], da[h, :rows, :]),
@@ -511,41 +520,45 @@
         for seg in range(2):
             for t in range(4):
                 wide_in[slot, 2 * t + seg] = seg_in[seg][t].astype(f32)
-        for seg in range(2):
-            part = slice(seg * rows, (seg + 1) * rows)
-            q, k, v, grad = seg_in[seg]
-            probs, ds = dscores(q, k, v, grad, lse[h, part, :], delta[h, part, :])
-            sums[slot, 0, part, :] = dot_nn(ds, k)
-            sums[slot, 1, part, :] = dot_tn(ds, q)
-            sums[slot, 2, part, :] = dot_tn(probs, grad)
-        for branch in range(1, BRANCHES + 1):
-            taken = plan.taken(branch)
-            inside = member_rows(meta, off, heads, branch, h, taken)
-            where = [member_rows(meta, off, heads, branch, h, taken, seg * rows) for seg in range(2)]
+        return seg_in
+
+    def begin(h, slot, seg_in, branch, seg):
+        if branch == 0:
+            query, key, value, grad = seg_in[seg]
+        else:
+            inside = member_rows(meta, off, heads, branch, h, plan.taken(branch))
 
             def member(t):
-                picked = [wide_in[slot, 2 * t + seg, inside, :] for seg in range(2)]
+                picked = [wide_in[slot, 2 * t + s, inside, :] for s in range(2)]
                 return jnp.concatenate(picked, axis=0).astype(bf16)
 
             query, grad = member(0), member(3)
-            lse_rows = jnp.concatenate([lse[h, w, :] for w in where], axis=0)
-            delta_rows = jnp.concatenate([delta[h, w, :] for w in where], axis=0)
             if branch == 1:
                 key, value = member(1), member(2)
             else:
-                first = sum(counts[: branch - 2])
+                first, layout = sum(counts[: branch - 2]), layouts[branch - 2]
                 far = pieces[first : first + counts[branch - 2]]
-                layout = layouts[branch - 2]
                 key, value = gathered(far, layout, 0, h), gathered(far, layout, 1, h)
-            probs, ds = dscores(query, key, value, grad, lse_rows, delta_rows)
-            grads = [dot_nn(ds, key)]
-            if branch == 1:
-                grads += [dot_tn(ds, query), dot_tn(probs, grad)]
-            for t, rows_new in enumerate(grads):
-                for seg in range(2):
-                    sums[slot, t, where[seg], :] = (
-                        sums[slot, t, where[seg], :] + rows_new[seg * taken : (seg + 1) * taken]
-                    )
+        return (h, slot, branch, seg, query, key, grad, dot_nt(query, key), dot_nt(grad, value))
+
+    def end(h, slot, branch, seg, query, key, grad, scores, dprob):
+        taken = plan.taken(branch)
+        if branch == 0:
+            where = [slice(seg * rows, (seg + 1) * rows)]
+        else:
+            where = [member_rows(meta, off, heads, branch, h, taken, s * rows) for s in range(2)]
+        lse_rows = jnp.concatenate([lse[h, w, :] for w in where], axis=0)
+        delta_rows = jnp.concatenate([delta[h, w, :] for w in where], axis=0)
+        probs, ds = probs_and_ds(scores, dprob, lse_rows, delta_rows)
+        grads = [dot_nn(ds, key)]
+        if branch <= 1:
+            grads += [dot_tn(ds, query), dot_tn(probs, grad)]
+        for t, rows_new in enumerate(grads):
+            for s, w in enumerate(where):
+                part = rows_new[s * taken : (s + 1) * taken]
+                sums[slot, t, w, :] = part if branch == 0 else sums[slot, t, w, :] + part
+
+    def store(h, slot):
         for t, scale in enumerate((scaling, scaling, None)):
             both = sums[slot, t]
             both = both if scale is None else both * scale
@@ -553,10 +566,21 @@
             sends[t][h] = both[rows:].astype(bf16)
 
     together = min(2, count)
+    order = [(0, 0), (0, 1)] + [(branch, 0) for branch in range(1, BRANCHES + 1)]
 
     def step(i, carry):
-        for slot in range(together):
-            one(i * together + slot, slot)
+        hs = [first_head + i * together + slot for slot in range(together)]
+        seg_ins = [load(h, slot) for slot, h in enumerate(hs)]
+        waiting = []
+        for branch, seg in order:
+            for slot, h in enumerate(hs):
+                waiting.append(begin(h, slot, seg_ins[slot], branch, seg))
+                if len(waiting) > 2:
+                    end(*waiting.pop(0))
+        for item in waiting:
+            end(*item)
+        for slot, h in enumerate(hs):
+            store(h, slot)
         return carry
 
     lax.fori_loop(0, count // together, step, 0)
@@ -576,12 +600,13 @@
     )
 
 
-def far_backward_body(plan, branches, layouts, meta, off, *refs):
+def far_backward_body(plan, branches, layouts, first_row, meta, off, *refs):
     counts = [len(x) for x in layouts]
     kvs, msgs, (own, send) = refs[: len(branches)], refs[len(branches) : -2], refs[-2:]
+    msgs, q_two = msgs[: sum(counts)], msgs[sum(counts) : sum(counts) + 2]
 
     def one(h, slot):
-        row = 0
+        row = first_row
         for j, branch in enumerate(branches):
             taken = plan.taken(branch)
             grads, queries, halves_of = [], [], [None] * (plan.rows // HEAD_DIM)
@@ -591,13 +616,16 @@
                 table_at = start + 2 * taken
                 for n in range(many):
                     grads.append(ref[n, 0, h, start:table_at, :])
-                    queries.append(ref[n, 0, h, table_at + STAT_ROWS : table_at + STAT_ROWS + 2 * taken, :])
+                    if branch != 2:
+                        queries.append(ref[n, 0, h, table_at + STAT_ROWS : table_at + STAT_ROWS + 2 * taken, :])
                     terms = ref[n, 0, h, table_at : table_at + STAT_ROWS, :].astype(f32)
                     half, shift = divmod(place, HEAD_DIM)
                     if shift:
                         terms = pltpu.roll(terms, shift, 1)
                     halves_of[half] = terms if halves_of[half] is None else halves_of[half] + terms
                     place += 2 * taken
+            if branch == 2:
+                queries = [ref[0, 0, h] for ref in q_two]
             grad = jnp.concatenate(grads, axis=0)
             query = jnp.concatenate(queries, axis=0)
             table = jnp.concatenate(halves_of, axis=1)
@@ -616,13 +644,16 @@
     plan.each_head(4, one)
 
 
-def far_backward(plan, branches, kvs, pieces, wait_for=()):
-    shape = (2, plan.heads, sum(plan.taken(b) for b in branches), HEAD_DIM)
-    return plan.call(
-        functools.partial(far_backward_body, plan, branches, [extents(p) for p in pieces]),
-        [*kvs, *[x.array for p in pieces for x in p]],
+def far_backward(plan, branches, kvs, pieces, q_two, wait_for, before=()):
+    shape = (2, plan.heads, sum(plan.taken(b) for b in FAR), HEAD_DIM)
+    first_row = sum(plan.taken(b) for b in FAR if b < branches[0])
+    flat = [*kvs, *[x.array for p in pieces for x in p], *q_two]
+    return plan.call(
+        functools.partial(far_backward_body, plan, branches, [extents(p) for p in pieces], first_row),
+        [*flat, *before],
         [jax.ShapeDtypeStruct(shape, f32), jax.ShapeDtypeStruct(shape, bf16)],
         name=f"far_backward{branches[0]}",
+        aliases={len(flat) + 2 + i: i for i in range(len(before))},
         wait_for=wait_for,
     )
 
@@ -677,14 +708,32 @@
     )
 
 
-def fold_body(plan, branches, meta, off, *refs):
-    own, got, row_refs, sums = refs[0], refs[1:3], refs[3:5], refs[5]
+def fold_body(plan, meta, off, own, got_k, got_v, sums):
+    for h in range(plan.heads):
+        for t, got in enumerate((got_k, got_v)):
+            sums[t, h] = own[1 + t, h]
+            sums[t, plan.heads + h] = got[h].astype(f32)
+
+
+def fold(plan, own, got):
+    shape = (2, 2 * plan.heads, plan.rows, HEAD_DIM)
+    return plan.call(
+        functools.partial(fold_body, plan),
+        [own, *got],
+        [jax.ShapeDtypeStruct(shape, f32)],
+        name="fold",
+    )[0]
+
+
+def finish_kv_body(plan, meta, off, given, *refs):
+    row_refs, (dk, dv, sums, sems) = refs[:-4], refs[-4:]
+    copies = []
     for slot in range(2 * plan.heads):
         side, h = divmod(slot, plan.heads)
         for t in range(2):
-            sums[t, slot] = own[1 + t, h] if side == 0 else got[t][h].astype(f32)
+            sums[t, slot] = given[t, slot]
         row = 0
-        for branch in branches:
+        for branch in FAR:
             taken = plan.taken(branch)
             start = off[branch - 1, meta[1] + column_of(plan, meta, slot)]
             where = pl.ds(start, taken, stride=2**branch)
@@ -692,28 +741,7 @@
                 rows = row_refs[side][t, h, row : row + taken, :].astype(f32)
                 sums[t, slot, where, :] = sums[t, slot, where, :] + rows
             row += taken
-
-
-def fold(plan, branches, own, got, rows_own, rows_got):
-    shape = (2, 2 * plan.heads, plan.rows, HEAD_DIM)
-    return plan.call(
-        functools.partial(fold_body, plan, branches),
-        [own, *got, rows_own, rows_got],
-        [jax.ShapeDtypeStruct(shape, f32)],
-        name="fold",
-    )[0]
-
-
-def finish_kv_body(plan, branch, meta, off, given, own, got, dk, dv, sums, sems):
-    copies = []
-    for slot in range(2 * plan.heads):
-        taken = plan.taken(branch)
-        start = off[branch - 1, meta[1] + column_of(plan, meta, slot)]
-        where = pl.ds(start, taken, stride=2**branch)
-        rows = (own, got)[slot // plan.heads]
         for t, out in enumerate((dk, dv)):
-            sums[t, slot] = given[t, slot]
-            sums[t, slot, where, :] = given[t, slot, where, :] + rows[t, slot % plan.heads].astype(f32)
             copy = pltpu.make_async_copy(
                 sums.at[t, slot], out.at[:, column_lanes(plan, meta, slot)], sems.at[len(copies)]
             )
@@ -723,10 +751,10 @@
         copy.wait()
 
 
-def finish_kv(plan, branch, sums, own, got):
+def finish_kv(plan, sums, own, got):
     full = jax.ShapeDtypeStruct((plan.rows, 2 * plan.width), f32)
     return plan.call(
-        functools.partial(finish_kv_body, plan, branch),
+        functools.partial(finish_kv_body, plan),
         [sums, own, got],
         [full, full],
         [pltpu.VMEM(sums.shape, f32), pltpu.SemaphoreType.DMA((4 * plan.heads,))],
@@ -741,7 +769,7 @@
     two_y = flip(two, "seq", 2)
     both, for_z = relay(plan, three_y, four, four_far, [filler(), three_z])
     four_y, from_z = flip(both, "seq", 2), flip(for_z, "seq", 4)
-    four_yz = flip(last_filler(four_y, both) if last_filler else four_y, "seq", 4)
+    four_yz = flip(last_filler(four_y, both, two_y) if last_filler else four_y, "seq", 4)
     rows_three, rows_four = three.shape[3], four.shape[3]
     from_z_four = [Rows(from_z, rows_three + i * rows_four, rows_four) for i in range(2)]
     return (
@@ -761,13 +789,15 @@
     plan = Plan(rows, heads_here, meta, head_offsets)
     gain, bias = norm_gain[None, :], norm_bias[None, :]
 
-    kv_got = flip(halves(plan, [key_rows, value_rows]), "seq", 1)
+    kv_sent = halves(plan, [key_rows, value_rows])
+    kv_got = flip(kv_sent, "seq", 1)
     qsc_got = flip(halves(plan, [queries, stream, cotangent]), "seq", 1)
     kv_far = pick(plan, [key_rows, value_rows], kv_got, 0)
     near = near_forward(plan, queries, key_rows, value_rows, kv_got, qsc_got)
     kv_pieces = gather(plan, kv_far, lambda: near[1])
     q_far = pick(plan, [queries], qsc_got, 0)
     far = [far_forward(plan, b, q_far[b - 2], kv_pieces[b - 2]) for b in FAR]
+    q_two_y = flip(q_far[0], "seq", 2)
     attn, lse, stats = combine(plan, near, far, stream, cotangent, qsc_got, gain)
 
     stats = join(plan, stats, flip(stats, "seq", 1), half, swap=True)
@@ -787,7 +817,8 @@
         qsc_got,
         gain,
         bias,
-        q_far,
+        q_far[1:],
+        [q_two_y],
     )
 
     n_got = flip(n_send, "seq", 1)
@@ -799,9 +830,9 @@
         parts.append(near_backward(plan, 0, first, ins, kv_pieces))
         return parts[-1][0]
 
-    def near_rest(four_y, both):
+    def near_rest(four_y, *ready):
         own, *sends = near_backward(
-            plan, first, plan.heads - first, ins, kv_pieces, parts[-1], wait_for=[both, n_got]
+            plan, first, plan.heads - first, ins, kv_pieces, parts[-1], wait_for=[*ready, n_got]
         )
         four_y, own = lax.optimization_barrier((four_y, own))
         parts.append((own, *sends))
@@ -811,10 +842,14 @@
     own, *sends = parts[-1]
     got_q, *got_kv = [flip(send, "seq", 1) for send in sends]
     grad_query, normed_out, mark = finish_q(plan, own, got_q, n_own, n_got)
-    rows_own, rows_send = far_backward(plan, FAR[:-1], kv_far[:-1], msg_pieces[:-1], [own])
-    sums = fold(plan, FAR[:-1], own, got_kv, rows_own, flip(rows_send, "seq", 1))
-    rows_own, rows_send = far_backward(plan, FAR[-1:], kv_far[-1:], msg_pieces[-1:], [mark, sums])
-    grad_key, grad_value = finish_kv(plan, FAR[-1], sums, rows_own, flip(rows_send, "seq", 1))
+    sums = fold(plan, own, got_kv)
+    rows, done = (), [own]
+    for group in GROUPS:
+        low, high = group[0] - 2, group[-1] - 1
+        q_two = [q_far[0], q_two_y] if group[0] == 2 else []
+        rows = far_backward(plan, group, kv_far[low:high], msg_pieces[low:high], q_two, done, rows)
+        done = [mark, sums]
+    grad_key, grad_value = finish_kv(plan, sums, rows[0], flip(rows[1], "seq", 1))
     return normed_out, grad_query, grad_key, grad_value
 
 

time: 112 us -> 106 us (0.946)
  Pallas kernels: 52.1 us -> 46.3 us
    pallas_call x20, Pallas kernels: 52.1 us -> 46.3 us  [call(): pl.pallas_call(without_waited if waited else body, out_shape=outs, in_spe...]
  transfers between devices with their start and end apart: 24 -> 24, of which waited for: 12 -> 9; matrix products, arithmetic and copies ran while one was open for 0% -> 0% of each run, Pallas kernels for 31% -> 33%
where the time goes in v2:
time: 106 us; the launch traced here: 105 us
  Pallas kernels  46.3 us (44%)
  waiting for transfers between devices  30.9 us (29%)
  starting transfers between devices  26.5 us (25%)
    pallas_call x20, Pallas kernels, call(): pl.pallas_call(without_waited if waited else body, out_shape=outs, in_spe...  46.3 us
    ppermute x24, waiting for transfers between devices, flip(): return lax.ppermute(block, axis, [(i, i ^ mask) for i in range(count)])  30.9 us
    ppermute x24, starting transfers between devices, flip(): return lax.ppermute(block, axis, [(i, i ^ mask) for i in range(count)])  26.5 us
  transfers between devices with their start and end apart: 24, of which 9 were waited for; matrix products, arithmetic and copies ran while one was open for 0% of the time, Pallas kernels for 33%

profile of v2, /device:TPU:0, one launch (start us, length us, event | category | flops | bytes accessed | tf_op | source)
XLA Modules:
  0.0 105.4 jit_solution(314107281584724756)
XLA Ops:
  0.6 0.1 pad_add_fusion.meta.refs_0_
  0.7 0.7 copy-done.5
  1.4 2.1 %halves.3 = bf16[3,256,1024]{2,1,0:T(8,128)(2,1)S(1)} custom-call(s32[2]{0:T(128)S(1)} %pad_add_fusion.meta.refs_0_, s32[4,32]{1,0:T(4,128)S(1)} %copy-done.5, bf16[256,2048]{1,0:T(8,128)(2,1)} %refs_2_.5, bf16[256,2048]{1,0:T(8,128)(2,1)} %refs_6_.1, bf16[256,2048]{1,0:T(8,128)(2,1)} %refs_7_.1), custom_call_target="tpu_custom_call" | custom-call | tf_op jit(solution)/shard_map/halves/pallas_call | solution.py:101
  3.5 0.0 copy-start
  3.5 0.0 copy-start.1
  3.5 0.0 copy-start.6
  3.6 0.6 collective-permute-start.1
  4.1 1.9 %halves.2 = bf16[2,256,1024]{2,1,0:T(8,128)(2,1)S(1)} custom-call(s32[2]{0:T(128)S(1)} %pad_add_fusion.meta.refs_0_, s32[4,32]{1,0:T(4,128)S(1)} %copy-done.5, bf16[256,2048]{1,0:T(8,128)(2,1)} %refs_3_.1, bf16[256,2048]{1,0:T(8,128)(2,1)} %refs_4_.1), custom_call_target="tpu_custom_call" | custom-call | tf_op jit(solution)/shard_map/halves/pallas_call | solution.py:101
  6.0 0.0 copy-start.2
  6.1 0.1 collective-permute-start
  6.1 2.6 %collective-permute-done.kv_got.refs_2_.refs_3_.refs_5_ = bf16[2,256,1024]{2,1,0:T(8,128)(2,1)S(1)} collective-permute-done((bf16[2,256,1024]{2,1,0:T(8,128)(2,1)S(1)}, bf16[2,256,1024]{2,1,0:T(8,128)(2,1)S(1)}, u32[]{:S(2)}, u32[]{:S(2)}) %collective-permute-start) | collective-permute-done | bytes 1048608 | tf_op jit(solution)/shard_map/ppermute | solution.py:42
  8.8 1.6 %pick.3 = (bf16[1,2,8,128,128]{4,3,2,1,0:T(8,128)(2,1)S(1)}, bf16[1,2,8,64,128]{4,3,2,1,0:T(8,128)(2,1)S(1)}, bf16[1,2,8,32,128]{4,3,2,1,0:T(8,128)(2,1)S(1)}) custom-call(s32[2]{0:T(128)S(1)} %pad_add_fusion.meta.refs_0_, s32[4,32]{1,0:T(4,128)S(1)} %copy-done.6, bf16[256,2048]{1,0:T(8,128)(2,1)S(1)} %copy-done, bf16[256,2048]{1,0:T(8,128)(2,1)S(1)} %copy-done.1, ...), custom_call_target="tpu_custom_call" | custom-call | tf_op jit(solution)/shard_map/pick/pallas_call | solution.py:101
  10.4 2.9 %collective-permute-start.4 = (bf16[1,2,8,64,128]{4,3,2,1,0:T(8,128)(2,1)S(1)}, bf16[1,2,8,64,128]{4,3,2,1,0:T(8,128)(2,1)S(1)}, u32[]{:S(2)}, u32[]{:S(2)}) collective-permute-start(bf16[1,2,8,64,128]{4,3,2,1,0:T(8,128)(2,1)S(1)} %get-tuple-element.58.refs_0_.refs_10_.refs_12_.refs_3_), channel_id=1, source_target_pairs={{0,8},{2,10},{4,12},{6,14},{8,0},{10,2},{12,4},{14,6},{16,24},{18,... | collective-permute-start | bytes 786440 | tf_op jit(solution)/shard_map/ppermute | solution.py:42
  13.2 1.5 %collective-permute-start.3 = (bf16[1,2,8,64,128]{4,3,2,1,0:T(8,128)(2,1)S(1)}, bf16[1,2,8,64,128]{4,3,2,1,0:T(8,128)(2,1)S(1)}, u32[]{:S(2)}, u32[]{:S(2)}) collective-permute-start(bf16[1,2,8,64,128]{4,3,2,1,0:T(8,128)(2,1)S(1)} %get-tuple-element.58.refs_0_.refs_10_.refs_12_.refs_3_), channel_id=1, source_target_pairs={{0,4},{2,6},{4,0},{6,2},{8,12},{10,14},{12,8},{14,10},{16,20},{18,... | collective-permute-start | bytes 786440 | tf_op jit(solution)/shard_map/ppermute | solution.py:42
  14.7 2.6 %collective-permute-start.5 = (bf16[1,2,8,32,128]{4,3,2,1,0:T(8,128)(2,1)S(1)}, bf16[1,2,8,32,128]{4,3,2,1,0:T(8,128)(2,1)S(1)}, u32[]{:S(2)}, u32[]{:S(2)}) collective-permute-start(bf16[1,2,8,32,128]{4,3,2,1,0:T(8,128)(2,1)S(1)} %get-tuple-element.59.refs_3_.refs_0_.refs_14_.refs_16_.refs_2_), channel_id=1, source_target_pairs={{0,16},{2,18},{4,20},{6,22},{8,24},{10,26},{12,28},{14,30},{16,0},... | collective-permute-start | bytes 393224 | tf_op jit(solution)/shard_map/ppermute | solution.py:42
  17.3 0.5 collective-permute-start.2
  17.8 4.9 %near_forward.1 = (f32[8,512,128]{2,1,0:T(8,128)S(1)}, f32[8,512,128]{2,1,0:T(8,128)S(1)}) custom-call(s32[2]{0:T(128)S(1)} %pad_add_fusion.meta.refs_0_, s32[4,32]{1,0:T(4,128)S(1)} %copy-done.6, bf16[256,2048]{1,0:T(8,128)(2,1)S(1)} %copy-done.2, bf16[256,2048]{1,0:T(8,128)(2,1)S(1)} %copy-done, bf16[256,2048]{1,0:T(8,128)(2,1)S(1)} %copy-done.1, ...), custom_call_target="tpu_custom_call" | custom-call | tf_op jit(solution)/shard_map/near_forward/pallas_call | solution.py:101
  22.8 0.0 collective-permute-done.5.refs_4_.refs_1_.refs_15_.refs_17_
  22.8 0.7 relay.2
  23.5 2.8 %collective-permute-start.6 = (bf16[1,2,8,128,128]{4,3,2,1,0:T(8,128)(2,1)S(1)}, bf16[1,2,8,128,128]{4,3,2,1,0:T(8,128)(2,1)S(1)}, u32[]{:S(2)}, u32[]{:S(2)}) collective-permute-start(bf16[1,2,8,128,128]{4,3,2,1,0:T(8,128)(2,1)S(1)} %get-tuple-element.60), channel_id=1, source_target_pairs={{0,8},{2,10},{4,12},{6,14},{8,0},{10,2},{12,4},{14,6},{16,24},{18,... | collective-permute-start | bytes 1572872 | tf_op jit(solution)/shard_map/ppermute | solution.py:42
  26.3 1.5 %collective-permute-start.7 = (bf16[2,2,8,32,128]{4,3,2,1,0:T(8,128)(2,1)S(1)}, bf16[2,2,8,32,128]{4,3,2,1,0:T(8,128)(2,1)S(1)}, u32[]{:S(2)}, u32[]{:S(2)}) collective-permute-start(bf16[2,2,8,32,128]{4,3,2,1,0:T(8,128)(2,1)S(1)} %get-tuple-element.64), channel_id=1, source_target_pairs={{0,4},{2,6},{4,0},{6,2},{8,12},{10,14},{12,8},{14,10},{16,20},{18,... | collective-permute-start | bytes 786440 | tf_op jit(solution)/shard_map/ppermute | solution.py:42
  27.8 10.5 %collective-permute-done.7.refs_2_.refs_16_.refs_18_ = bf16[2,2,8,32,128]{4,3,2,1,0:T(8,128)(2,1)S(1)} collective-permute-done((bf16[2,2,8,32,128]{4,3,2,1,0:T(8,128)(2,1)S(1)}, bf16[2,2,8,32,128]{4,3,2,1,0:T(8,128)(2,1)S(1)}, u32[]{:S(2)}, u32[]{:S(2)}) %collective-permute-start.7) | collective-permute-done | bytes 262176 | tf_op jit(solution)/shard_map/ppermute | solution.py:42
  38.3 0.4 collective-permute-start.8
  38.6 1.1 %pick.2 = (bf16[1,1,8,128,128]{4,3,2,1,0:T(8,128)(2,1)S(1)}, bf16[1,1,8,64,128]{4,3,2,1,0:T(8,128)(2,1)S(1)}, bf16[1,1,8,32,128]{4,3,2,1,0:T(8,128)(2,1)S(1)}) custom-call(s32[2]{0:T(128)S(1)} %pad_add_fusion.meta.refs_0_, s32[4,32]{1,0:T(4,128)S(1)} %copy-done.6, bf16[256,2048]{1,0:T(8,128)(2,1)S(1)} %copy-done.2, ...), custom_call_target="tpu_custom_call" | custom-call | tf_op jit(solution)/shard_map/pick/pallas_call | solution.py:101
  39.7 0.0 copy-start.3
  39.7 0.0 copy-start.4
  39.7 0.0 copy-start.7
  39.7 1.7 %collective-permute-start.11 = (bf16[1,1,8,128,128]{4,3,2,1,0:T(8,128)(2,1)S(1)}, bf16[1,1,8,128,128]{4,3,2,1,0:T(8,128)(2,1)S(1)}, u32[]{:S(2)}, u32[]{:S(2)}) collective-permute-start(bf16[1,1,8,128,128]{4,3,2,1,0:T(8,128)(2,1)S(1)} %get-tuple-element.53.q.refs_10_), channel_id=1, source_target_pairs={{0,4},{2,6},{4,0},{6,2},{8,12},{10,14},{12,8},{14,10},{16,20},{18,... | collective-permute-start | bytes 786440 | tf_op jit(solution)/shard_map/ppermute | solution.py:42
  41.4 1.6 %far_forward2.1 = (f32[8,128,128]{2,1,0:T(8,128)S(1)}, f32[8,128,128]{2,1,0:T(8,128)S(1)}) custom-call(s32[2]{0:T(128)S(1)} %pad_add_fusion.meta.refs_0_, s32[4,32]{1,0:T(4,128)S(1)} %copy-done.6, bf16[1,1,8,128,128]{4,3,2,1,0:T(8,128)(2,1)S(1)} %get-tuple-element.53.q.refs_10_, ...), custom_call_target="tpu_custom_call" | custom-call | tf_op jit(solution)/shard_map/far_forward2/pallas_call | solution.py:101
  43.0 1.6 %far_forward3.1 = (f32[8,64,128]{2,1,0:T(8,128)S(1)}, f32[8,64,128]{2,1,0:T(8,128)S(1)}) custom-call(s32[2]{0:T(128)S(1)} %pad_add_fusion.meta.refs_0_, s32[4,32]{1,0:T(4,128)S(1)} %copy-done.6, bf16[1,1,8,64,128]{4,3,2,1,0:T(8,128)(2,1)S(1)} %get-tuple-element.57.q.refs_11_, ...), custom_call_target="tpu_custom_call" | custom-call | tf_op jit(solution)/shard_map/far_forward3/pallas_call | solution.py:101
  44.6 1.0 collective-permute-done.8.refs_5_.refs_19_.refs_21_
  45.6 1.5 %far_forward4.1 = (f32[8,32,128]{2,1,0:T(8,128)S(1)}, f32[8,32,128]{2,1,0:T(8,128)S(1)}) custom-call(s32[2]{0:T(128)S(1)} %pad_add_fusion.meta.refs_0_, s32[4,32]{1,0:T(4,128)S(1)} %copy-done.6, bf16[1,1,8,32,128]{4,3,2,1,0:T(8,128)(2,1)S(1)} %get-tuple-element.63.q.refs_12_, ...), custom_call_target="tpu_custom_call" | custom-call | tf_op jit(solution)/shard_map/far_forward4/pallas_call | solution.py:101
  47.2 0.0 copy-start.8
  47.2 3.6 %combine.1 = (f32[8,512,128]{2,1,0:T(8,128)S(1)}, f32[8,512,128]{2,1,0:T(8,128)S(1)}, f32[8,512]{1,0:T(8,128)S(1)}) custom-call(s32[2]{0:T(128)S(1)} %pad_add_fusion.meta.refs_0_, s32[4,32]{1,0:T(4,128)S(1)} %copy-done.6, f32[8,512,128]{2,1,0:T(8,128)S(1)} %get-tuple-element.51.refs_0_, f32[8,512,128]{2,1,0:T(8,128)S(1)} %get-tuple-element.52.refs_5_.refs_1_, ...), custom_call_target="tpu_custom_call" | custom-call | tf_op jit(solution)/shard_map/combine/pallas_call | solution.py:101
  50.8 0.0 collective-permute-start.9
  50.9 1.2 %collective-permute-done.9.other = f32[8,512]{1,0:T(8,128)S(1)} collective-permute-done((f32[8,512]{1,0:T(8,128)S(1)}, f32[8,512]{1,0:T(8,128)S(1)}, u32[]{:S(2)}, u32[]{:S(2)}) %collective-permute-start.9) | collective-permute-done | bytes 16416 | tf_op jit(solution)/shard_map/ppermute | solution.py:42
  52.0 0.6 join.1.refs_2_
  52.6 1.6 %collective-permute-start.10 = (f32[8,512]{1,0:T(8,128)S(1)}, f32[8,512]{1,0:T(8,128)S(1)}, u32[]{:S(2)}, u32[]{:S(2)}) collective-permute-start(f32[8,512]{1,0:T(8,128)S(1)} %join.1.refs_2_), channel_id=1, source_target_pairs={{0,1},{1,0},{2,3},{3,2},{4,5},{5,4},{6,7},{7,6},{8,9},{9,8},{10,11... | collective-permute-start | bytes 49160 | tf_op jit(solution)/shard_map/ppermute | solution.py:42
  54.2 2.2 %collective-permute-done.10.refs_3_ = f32[8,512]{1,0:T(8,128)S(1)} collective-permute-done((f32[8,512]{1,0:T(8,128)S(1)}, f32[8,512]{1,0:T(8,128)S(1)}, u32[]{:S(2)}, u32[]{:S(2)}) %collective-permute-start.10) | collective-permute-done | bytes 16416 | tf_op jit(solution)/shard_map/ppermute | solution.py:42
  56.4 4.1 %norm.1 = (bf16[256,1024]{1,0:T(8,128)(2,1)S(1)}, bf16[8,256,128]{2,1,0:T(8,128)(2,1)S(1)}, bf16[8,512,128]{2,1,0:T(8,128)(2,1)S(1)}, f32[8,512,128]{2,1,0:T(8,1...) custom-call(s32[2]{0:T(128)S(1)} %pad_add_fusion.meta.refs_0_, ...), custom_call_target="tpu_custom_call" | custom-call | tf_op jit(solution)/shard_map/norm/pallas_call | solution.py:101
  60.5 0.1 collective-permute-start.17
  60.6 0.7 collective-permute-start.14
  61.3 1.3 %collective-permute-start.12 = (bf16[1,1,8,136,128]{4,3,2,1,0:T(8,128)(2,1)S(1)}, bf16[1,1,8,136,128]{4,3,2,1,0:T(8,128)(2,1)S(1)}, u32[]{:S(2)}, u32[]{:S(2)}) collective-permute-start(bf16[1,1,8,136,128]{4,3,2,1,0:T(8,128)(2,1)S(1)} %get-tuple-element.70.refs_6_), channel_id=1, source_target_pairs={{0,4},{2,6},{4,0},{6,2},{8,12},{10,14},{12,8},{14,10},{16,20},{18,... | collective-permute-start | bytes 835592 | tf_op jit(solution)/shard_map/ppermute | solution.py:42
  62.7 0.7 collective-permute-start.16
  63.4 2.5 %collective-permute-start.13 = (bf16[1,1,8,72,128]{4,3,2,1,0:T(8,128)(2,1)S(1)}, bf16[1,1,8,72,128]{4,3,2,1,0:T(8,128)(2,1)S(1)}, u32[]{:S(2)}, u32[]{:S(2)}) collective-permute-start(bf16[1,1,8,72,128]{4,3,2,1,0:T(8,128)(2,1)S(1)} %get-tuple-element.71.refs_3_), channel_id=1, source_target_pairs={{0,16},{2,18},{4,20},{6,22},{8,24},{10,26},{12,28},{14,30},{16,0},... | collective-permute-start | bytes 442376 | tf_op jit(solution)/shard_map/ppermute | solution.py:42
  65.8 2.4 %near_backward0.1 = (f32[3,8,256,128]{3,2,1,0:T(8,128)S(1)}, bf16[8,256,128]{2,1,0:T(8,128)(2,1)S(1)}, bf16[8,256,128]{2,1,0:T(8,128)(2,1)S(1)}, bf16[8,256,128]{2,1,0:T(8,128)(2,1)S(1)}) custom-call(s32[2]{0:T(128)S(1)} %pad_add_fusion.meta.refs_0_, s32[4,32]{1,0:T(4,128)S(1)} %copy-done.6, bf16[256,2048]{1,0:T(8,128)(2,1)S(1)} %copy-done.2, ...), custom_call_target="tpu_custom_call" | custom-call | tf_op jit(solution)/shard_map/near_backward0/pallas_call | solution.py:101
  68.2 2.8 %collective-permute-done.13.refs_4_ = bf16[1,1,8,72,128]{4,3,2,1,0:T(8,128)(2,1)S(1)} collective-permute-done((bf16[1,1,8,72,128]{4,3,2,1,0:T(8,128)(2,1)S(1)}, bf16[1,1,8,72,128]{4,3,2,1,0:T(8,128)(2,1)S(1)}, u32[]{:S(2)}, u32[]{:S(2)}) %collective-permute-start.13) | collective-permute-done | bytes 147488 | tf_op jit(solution)/shard_map/ppermute | solution.py:42
  71.0 1.8 %collective-permute-done.14.refs_6_.refs_8_ = bf16[1,1,8,136,128]{4,3,2,1,0:T(8,128)(2,1)S(1)} collective-permute-done((bf16[1,1,8,136,128]{4,3,2,1,0:T(8,128)(2,1)S(1)}, bf16[1,1,8,136,128]{4,3,2,1,0:T(8,128)(2,1)S(1)}, u32[]{:S(2)}, u32[]{:S(2)}) %collective-permute-start.14) | collective-permute-done | bytes 278560 | tf_op jit(solution)/shard_map/ppermute | solution.py:42
  72.8 0.6 relay.3
  73.5 1.6 %collective-permute-start.15 = (bf16[2,1,8,72,128]{4,3,2,1,0:T(8,128)(2,1)S(1)}, bf16[2,1,8,72,128]{4,3,2,1,0:T(8,128)(2,1)S(1)}, u32[]{:S(2)}, u32[]{:S(2)}) collective-permute-start(bf16[2,1,8,72,128]{4,3,2,1,0:T(8,128)(2,1)S(1)} %get-tuple-element.75.refs_26_), channel_id=1, source_target_pairs={{0,4},{2,6},{4,0},{6,2},{8,12},{10,14},{12,8},{14,10},{16,20},{18,... | collective-permute-start | bytes 884744 | tf_op jit(solution)/shard_map/ppermute | solution.py:42
  75.1 2.6 %collective-permute-start.21 = (bf16[1,1,8,280,128]{4,3,2,1,0:T(8,128)(2,1)S(1)}, bf16[1,1,8,280,128]{4,3,2,1,0:T(8,128)(2,1)S(1)}, u32[]{:S(2)}, u32[]{:S(2)}) collective-permute-start(bf16[1,1,8,280,128]{4,3,2,1,0:T(8,128)(2,1)S(1)} %get-tuple-element.89), channel_id=1, source_target_pairs={{0,8},{2,10},{4,12},{6,14},{8,0},{10,2},{12,4},{14,6},{16,24},{18,... | collective-permute-start | bytes 1720328 | tf_op jit(solution)/shard_map/ppermute | solution.py:42
  77.7 6.0 %near_backward2.1 = (f32[3,8,256,128]{3,2,1,0:T(8,128)S(1)}, bf16[8,256,128]{2,1,0:T(8,128)(2,1)S(1)}, bf16[8,256,128]{2,1,0:T(8,128)(2,1)S(1)}, bf16[8,256,128]{2,1,0:T(8,128)(2,1)S(1)}) custom-call(s32[2]{0:T(128)S(1)} %pad_add_fusion.meta.refs_0_, ...), custom_call_target="tpu_custom_call", output_to_operand_aliasing={{0}: (22, {}), {1}: (23, {}), {2}: (24, {}), {3}: (25, {})} | custom-call | tf_op jit(solution)/shard_map/near_backward2/pallas_call | solution.py:101
  83.7 0.1 collective-permute-start.18
  83.8 0.5 collective-permute-start.19
  84.3 0.1 collective-permute-start.20
  84.4 0.3 collective-permute-start.22
  84.6 6.9 %collective-permute-done.21.refs_9_.refs_6_.refs_7_ = bf16[1,1,8,280,128]{4,3,2,1,0:T(8,128)(2,1)S(1)} collective-permute-done((bf16[1,1,8,280,128]{4,3,2,1,0:T(8,128)(2,1)S(1)}, bf16[1,1,8,280,128]{4,3,2,1,0:T(8,128)(2,1)S(1)}, u32[]{:S(2)}, u32[]{:S(2)}) %collective-permute-start.21) | collective-permute-done | bytes 573472 | tf_op jit(solution)/shard_map/ppermute | solution.py:42
  91.5 3.7 %far_backward2.1 = (f32[2,8,112,128]{3,2,1,0:T(8,128)S(1)}, bf16[2,8,112,128]{3,2,1,0:T(8,128)(2,1)S(1)}) custom-call(s32[2]{0:T(128)S(1)} %pad_add_fusion.meta.refs_0_, s32[4,32]{1,0:T(4,128)S(1)} %copy-done.6, bf16[1,2,8,128,128]{4,3,2,1,0:T(8,128)(2,1)S(1)} %get-tuple-element.54.refs_0_.refs_8_.refs_10_.refs_2_, ...), custom_call_target="tpu_custom_call" | custom-call | tf_op jit(solution)/shard_map/far_backward2/pallas_call | solution.py:101
  95.2 2.4 %finish_q.1 = (f32[256,2048]{1,0:T(8,128)}, bf16[256,2048]{1,0:T(8,128)(2,1)}, f32[8,128]{1,0:T(8,128)S(1)}) custom-call(s32[2]{0:T(128)S(1)} %pad_add_fusion.meta.refs_0_, s32[4,32]{1,0:T(4,128)S(1)} %copy-done.6, f32[3,8,256,128]{3,2,1,0:T(8,128)S(1)} %get-tuple-element.82.own.refs_12_, bf16[8,256,128]{2,1,0:T(8,128)(2,1)S(1)} %collective-permute-done.18.got, ...), custom_call_target="tpu_custom_call" | custom-call | tf_op jit(solution)/shard_map/finish_q/pallas_call | solution.py:101
  97.6 0.8 fold.1.refs_12_.given
  98.5 2.2 %far_backward4.1 = (f32[2,8,112,128]{3,2,1,0:T(8,128)S(1)}, bf16[2,8,112,128]{3,2,1,0:T(8,128)(2,1)S(1)}) custom-call(s32[2]{0:T(128)S(1)} %pad_add_fusion.meta.refs_0_, s32[4,32]{1,0:T(4,128)S(1)} %copy-done.6, ...), custom_call_target="tpu_custom_call", output_to_operand_aliasing={{0}: (9, {}), {1}: (10, {})} | custom-call | tf_op jit(solution)/shard_map/far_backward4/pallas_call | solution.py:101
  100.7 0.1 collective-permute-start.23
  100.7 1.8 %collective-permute-done.23.refs_1_ = bf16[2,8,112,128]{3,2,1,0:T(8,128)(2,1)S(1)} collective-permute-done((bf16[2,8,112,128]{3,2,1,0:T(8,128)(2,1)S(1)}, bf16[2,8,112,128]{3,2,1,0:T(8,128)(2,1)S(1)}, u32[]{:S(2)}, u32[]{:S(2)}) %collective-permute-start.23) | collective-permute-done | bytes 458784 | tf_op jit(solution)/shard_map/ppermute | solution.py:42
  102.5 2.9 %finish_kv.1 = (f32[256,2048]{1,0:T(8,128)}, f32[256,2048]{1,0:T(8,128)}) custom-call(s32[2]{0:T(128)S(1)} %pad_add_fusion.meta.refs_0_, s32[4,32]{1,0:T(4,128)S(1)} %copy-done.6, f32[2,16,256,128]{3,2,1,0:T(8,128)S(1)} %fold.1.refs_12_.given, f32[2,8,112,128]{3,2,1,0:T(8,128)S(1)} %get-tuple-element.94.refs_0_, ...), custom_call_target="tpu_custom_call" | custom-call | tf_op jit(solution)/shard_map/finish_kv/pallas_call | solution.py:101
  (23 shorter events, 0.1 us)
Async XLA Ops:
  0.7 0.7 copy-start.5
  3.5 5.3 %copy-start = (bf16[256,2048]{1,0:T(8,128)(2,1)S(1)}, bf16[256,2048]{1,0:T(8,128)(2,1)}, u32[]{:S(2)}) copy-start(bf16[256,2048]{1,0:T(8,128)(2,1)} %refs_3_.1) | copy-start | bytes 3145732
  3.5 5.3 %copy-start.1 = (bf16[256,2048]{1,0:T(8,128)(2,1)S(1)}, bf16[256,2048]{1,0:T(8,128)(2,1)}, u32[]{:S(2)}) copy-start(bf16[256,2048]{1,0:T(8,128)(2,1)} %refs_4_.1) | copy-start | bytes 3145732
  3.5 5.2 %copy-start.6 = (s32[4,32]{1,0:T(4,128)S(1)}, s32[4,32]{1,0:T(4,128)}, u32[]{:S(2)}) copy-start(s32[4,32]{1,0:T(4,128)} %off.27) | copy-start | bytes 1540
  3.6 14.3 %collective-permute-start.1 = (bf16[3,256,1024]{2,1,0:T(8,128)(2,1)S(1)}, bf16[3,256,1024]{2,1,0:T(8,128)(2,1)S(1)}, u32[]{:S(2)}, u32[]{:S(2)}) collective-permute-start(bf16[3,256,1024]{2,1,0:T(8,128)(2,1)S(1)} %halves.3), channel_id=1, source_target_pairs={{0,2},{2,0},{4,6},{6,4},{8,10},{10,8},{12,14},{14,12},{16,18},{18,... | collective-permute-start | bytes 4718600 | tf_op jit(solution)/shard_map/ppermute | solution.py:42
  6.0 11.8 %copy-start.2 = (bf16[256,2048]{1,0:T(8,128)(2,1)S(1)}, bf16[256,2048]{1,0:T(8,128)(2,1)}, u32[]{:S(2)}) copy-start(bf16[256,2048]{1,0:T(8,128)(2,1)} %refs_2_.5) | copy-start | bytes 3145732
  6.1 2.7 %collective-permute-start = (bf16[2,256,1024]{2,1,0:T(8,128)(2,1)S(1)}, bf16[2,256,1024]{2,1,0:T(8,128)(2,1)S(1)}, u32[]{:S(2)}, u32[]{:S(2)}) collective-permute-start(bf16[2,256,1024]{2,1,0:T(8,128)(2,1)S(1)} %halves.2), channel_id=1, source_target_pairs={{0,2},{2,0},{4,6},{6,4},{8,10},{10,8},{12,14},{14,12},{16,18},{18,... | collective-permute-start | bytes 3145736 | tf_op jit(solution)/shard_map/ppermute | solution.py:42
  10.4 12.4 %collective-permute-start.4 = (bf16[1,2,8,64,128]{4,3,2,1,0:T(8,128)(2,1)S(1)}, bf16[1,2,8,64,128]{4,3,2,1,0:T(8,128)(2,1)S(1)}, u32[]{:S(2)}, u32[]{:S(2)}) collective-permute-start(bf16[1,2,8,64,128]{4,3,2,1,0:T(8,128)(2,1)S(1)} %get-tuple-element.58.refs_0_.refs_10_.refs_12_.refs_3_), channel_id=1, source_target_pairs={{0,8},{2,10},{4,12},{6,14},{8,0},{10,2},{12,4},{14,6},{16,24},{18,... | collective-permute-start | bytes 786440 | tf_op jit(solution)/shard_map/ppermute | solution.py:42
  13.2 9.6 %collective-permute-start.3 = (bf16[1,2,8,64,128]{4,3,2,1,0:T(8,128)(2,1)S(1)}, bf16[1,2,8,64,128]{4,3,2,1,0:T(8,128)(2,1)S(1)}, u32[]{:S(2)}, u32[]{:S(2)}) collective-permute-start(bf16[1,2,8,64,128]{4,3,2,1,0:T(8,128)(2,1)S(1)} %get-tuple-element.58.refs_0_.refs_10_.refs_12_.refs_3_), channel_id=1, source_target_pairs={{0,4},{2,6},{4,0},{6,2},{8,12},{10,14},{12,8},{14,10},{16,20},{18,... | collective-permute-start | bytes 786440 | tf_op jit(solution)/shard_map/ppermute | solution.py:42
  14.7 8.0 %collective-permute-start.5 = (bf16[1,2,8,32,128]{4,3,2,1,0:T(8,128)(2,1)S(1)}, bf16[1,2,8,32,128]{4,3,2,1,0:T(8,128)(2,1)S(1)}, u32[]{:S(2)}, u32[]{:S(2)}) collective-permute-start(bf16[1,2,8,32,128]{4,3,2,1,0:T(8,128)(2,1)S(1)} %get-tuple-element.59.refs_3_.refs_0_.refs_14_.refs_16_.refs_2_), channel_id=1, source_target_pairs={{0,16},{2,18},{4,20},{6,22},{8,24},{10,26},{12,28},{14,30},{16,0},... | collective-permute-start | bytes 393224 | tf_op jit(solution)/shard_map/ppermute | solution.py:42
  17.3 24.1 %collective-permute-start.2 = (bf16[1,2,8,128,128]{4,3,2,1,0:T(8,128)(2,1)S(1)}, bf16[1,2,8,128,128]{4,3,2,1,0:T(8,128)(2,1)S(1)}, u32[]{:S(2)}, u32[]{:S(2)}) collective-permute-start(bf16[1,2,8,128,128]{4,3,2,1,0:T(8,128)(2,1)S(1)} %get-tuple-element.54.refs_0_.refs_8_.refs_10_.refs_2_), channel_id=1, source_target_pairs={{0,4},{2,6},{4,0},{6,2},{8,12},{10,14},{12,8},{14,10},{16,20},{18,... | collective-permute-start | bytes 1572872 | tf_op jit(solution)/shard_map/ppermute | solution.py:42
  23.5 19.5 %collective-permute-start.6 = (bf16[1,2,8,128,128]{4,3,2,1,0:T(8,128)(2,1)S(1)}, bf16[1,2,8,128,128]{4,3,2,1,0:T(8,128)(2,1)S(1)}, u32[]{:S(2)}, u32[]{:S(2)}) collective-permute-start(bf16[1,2,8,128,128]{4,3,2,1,0:T(8,128)(2,1)S(1)} %get-tuple-element.60), channel_id=1, source_target_pairs={{0,8},{2,10},{4,12},{6,14},{8,0},{10,2},{12,4},{14,6},{16,24},{18,... | collective-permute-start | bytes 1572872 | tf_op jit(solution)/shard_map/ppermute | solution.py:42
  26.3 12.0 %collective-permute-start.7 = (bf16[2,2,8,32,128]{4,3,2,1,0:T(8,128)(2,1)S(1)}, bf16[2,2,8,32,128]{4,3,2,1,0:T(8,128)(2,1)S(1)}, u32[]{:S(2)}, u32[]{:S(2)}) collective-permute-start(bf16[2,2,8,32,128]{4,3,2,1,0:T(8,128)(2,1)S(1)} %get-tuple-element.64), channel_id=1, source_target_pairs={{0,4},{2,6},{4,0},{6,2},{8,12},{10,14},{12,8},{14,10},{16,20},{18,... | collective-permute-start | bytes 786440 | tf_op jit(solution)/shard_map/ppermute | solution.py:42
  38.3 7.3 %collective-permute-start.8 = (bf16[2,2,8,32,128]{4,3,2,1,0:T(8,128)(2,1)S(1)}, bf16[2,2,8,32,128]{4,3,2,1,0:T(8,128)(2,1)S(1)}, u32[]{:S(2)}, u32[]{:S(2)}) collective-permute-start(bf16[2,2,8,32,128]{4,3,2,1,0:T(8,128)(2,1)S(1)} %collective-permute-done.7.refs_2_.refs_16_.refs_18_), channel_id=1, source_target_pairs={{0,8},{2,10},{4,12},{6,14},{8,0},{10,2},{12,4},{14,6},{16,24},{18,... | collective-permute-start | bytes 786440 | tf_op jit(solution)/shard_map/ppermute | solution.py:42
  39.7 7.4 %copy-start.3 = (bf16[256,2048]{1,0:T(8,128)(2,1)S(1)}, bf16[256,2048]{1,0:T(8,128)(2,1)}, u32[]{:S(2)}) copy-start(bf16[256,2048]{1,0:T(8,128)(2,1)} %refs_6_.1) | copy-start | bytes 3145732
  39.7 7.4 %copy-start.4 = (bf16[256,2048]{1,0:T(8,128)(2,1)S(1)}, bf16[256,2048]{1,0:T(8,128)(2,1)}, u32[]{:S(2)}) copy-start(bf16[256,2048]{1,0:T(8,128)(2,1)} %refs_7_.1) | copy-start | bytes 3145732
  39.7 7.4 %copy-start.7 = (f32[2048]{0:T(1024)S(1)}, f32[2048]{0:T(1024)}, u32[]{:S(2)}) copy-start(f32[2048]{0:T(1024)} %param.12) | copy-start | bytes 24580
  39.7 14.4 %collective-permute-start.11 = (bf16[1,1,8,128,128]{4,3,2,1,0:T(8,128)(2,1)S(1)}, bf16[1,1,8,128,128]{4,3,2,1,0:T(8,128)(2,1)S(1)}, u32[]{:S(2)}, u32[]{:S(2)}) collective-permute-start(bf16[1,1,8,128,128]{4,3,2,1,0:T(8,128)(2,1)S(1)} %get-tuple-element.53.q.refs_10_), channel_id=1, source_target_pairs={{0,4},{2,6},{4,0},{6,2},{8,12},{10,14},{12,8},{14,10},{16,20},{18,... | collective-permute-start | bytes 786440 | tf_op jit(solution)/shard_map/ppermute | solution.py:42
  47.2 9.3 %copy-start.8 = (f32[2048]{0:T(1024)S(1)}, f32[2048]{0:T(1024)}, u32[]{:S(2)}) copy-start(f32[2048]{0:T(1024)} %param.13) | copy-start | bytes 24580
  50.8 1.2 %collective-permute-start.9 = (f32[8,512]{1,0:T(8,128)S(1)}, f32[8,512]{1,0:T(8,128)S(1)}, u32[]{:S(2)}, u32[]{:S(2)}) collective-permute-start(f32[8,512]{1,0:T(8,128)S(1)} %get-tuple-element.67.mine), channel_id=1, source_target_pairs={{0,2},{2,0},{4,6},{6,4},{8,10},{10,8},{12,14},{14,12},{16,18},{18,... | collective-permute-start | bytes 49160 | tf_op jit(solution)/shard_map/ppermute | solution.py:42
  52.6 3.8 %collective-permute-start.10 = (f32[8,512]{1,0:T(8,128)S(1)}, f32[8,512]{1,0:T(8,128)S(1)}, u32[]{:S(2)}, u32[]{:S(2)}) collective-permute-start(f32[8,512]{1,0:T(8,128)S(1)} %join.1.refs_2_), channel_id=1, source_target_pairs={{0,1},{1,0},{2,3},{3,2},{4,5},{5,4},{6,7},{7,6},{8,9},{9,8},{10,11... | collective-permute-start | bytes 49160 | tf_op jit(solution)/shard_map/ppermute | solution.py:42
  60.5 17.1 %collective-permute-start.17 = (bf16[8,256,128]{2,1,0:T(8,128)(2,1)S(1)}, bf16[8,256,128]{2,1,0:T(8,128)(2,1)S(1)}, u32[]{:S(2)}, u32[]{:S(2)}) collective-permute-start(bf16[8,256,128]{2,1,0:T(8,128)(2,1)S(1)} %get-tuple-element.80), channel_id=1, source_target_pairs={{0,2},{2,0},{4,6},{6,4},{8,10},{10,8},{12,14},{14,12},{16,18},{18,... | collective-permute-start | bytes 1572872 | tf_op jit(solution)/shard_map/ppermute | solution.py:42
  60.6 12.2 %collective-permute-start.14 = (bf16[1,1,8,136,128]{4,3,2,1,0:T(8,128)(2,1)S(1)}, bf16[1,1,8,136,128]{4,3,2,1,0:T(8,128)(2,1)S(1)}, u32[]{:S(2)}, u32[]{:S(2)}) collective-permute-start(bf16[1,1,8,136,128]{4,3,2,1,0:T(8,128)(2,1)S(1)} %get-tuple-element.70.refs_6_), channel_id=1, source_target_pairs={{0,8},{2,10},{4,12},{6,14},{8,0},{10,2},{12,4},{14,6},{16,24},{18,... | collective-permute-start | bytes 835592 | tf_op jit(solution)/shard_map/ppermute | solution.py:42
  61.3 11.5 %collective-permute-start.12 = (bf16[1,1,8,136,128]{4,3,2,1,0:T(8,128)(2,1)S(1)}, bf16[1,1,8,136,128]{4,3,2,1,0:T(8,128)(2,1)S(1)}, u32[]{:S(2)}, u32[]{:S(2)}) collective-permute-start(bf16[1,1,8,136,128]{4,3,2,1,0:T(8,128)(2,1)S(1)} %get-tuple-element.70.refs_6_), channel_id=1, source_target_pairs={{0,4},{2,6},{4,0},{6,2},{8,12},{10,14},{12,8},{14,10},{16,20},{18,... | collective-permute-start | bytes 835592 | tf_op jit(solution)/shard_map/ppermute | solution.py:42
  62.7 15.0 %collective-permute-start.16 = (bf16[1,1,8,136,128]{4,3,2,1,0:T(8,128)(2,1)S(1)}, bf16[1,1,8,136,128]{4,3,2,1,0:T(8,128)(2,1)S(1)}, u32[]{:S(2)}, u32[]{:S(2)}) collective-permute-start(bf16[1,1,8,136,128]{4,3,2,1,0:T(8,128)(2,1)S(1)} %get-tuple-element.79.refs_4_), channel_id=1, source_target_pairs={{0,4},{2,6},{4,0},{6,2},{8,12},{10,14},{12,8},{14,10},{16,20},{18,... | collective-permute-start | bytes 835592 | tf_op jit(solution)/shard_map/ppermute | solution.py:42
  63.4 7.7 %collective-permute-start.13 = (bf16[1,1,8,72,128]{4,3,2,1,0:T(8,128)(2,1)S(1)}, bf16[1,1,8,72,128]{4,3,2,1,0:T(8,128)(2,1)S(1)}, u32[]{:S(2)}, u32[]{:S(2)}) collective-permute-start(bf16[1,1,8,72,128]{4,3,2,1,0:T(8,128)(2,1)S(1)} %get-tuple-element.71.refs_3_), channel_id=1, source_target_pairs={{0,16},{2,18},{4,20},{6,22},{8,24},{10,26},{12,28},{14,30},{16,0},... | collective-permute-start | bytes 442376 | tf_op jit(solution)/shard_map/ppermute | solution.py:42
  73.5 10.9 %collective-permute-start.15 = (bf16[2,1,8,72,128]{4,3,2,1,0:T(8,128)(2,1)S(1)}, bf16[2,1,8,72,128]{4,3,2,1,0:T(8,128)(2,1)S(1)}, u32[]{:S(2)}, u32[]{:S(2)}) collective-permute-start(bf16[2,1,8,72,128]{4,3,2,1,0:T(8,128)(2,1)S(1)} %get-tuple-element.75.refs_26_), channel_id=1, source_target_pairs={{0,4},{2,6},{4,0},{6,2},{8,12},{10,14},{12,8},{14,10},{16,20},{18,... | collective-permute-start | bytes 884744 | tf_op jit(solution)/shard_map/ppermute | solution.py:42
  75.1 16.4 %collective-permute-start.21 = (bf16[1,1,8,280,128]{4,3,2,1,0:T(8,128)(2,1)S(1)}, bf16[1,1,8,280,128]{4,3,2,1,0:T(8,128)(2,1)S(1)}, u32[]{:S(2)}, u32[]{:S(2)}) collective-permute-start(bf16[1,1,8,280,128]{4,3,2,1,0:T(8,128)(2,1)S(1)} %get-tuple-element.89), channel_id=1, source_target_pairs={{0,8},{2,10},{4,12},{6,14},{8,0},{10,2},{12,4},{14,6},{16,24},{18,... | collective-permute-start | bytes 1720328 | tf_op jit(solution)/shard_map/ppermute | solution.py:42
  83.7 11.5 %collective-permute-start.18 = (bf16[8,256,128]{2,1,0:T(8,128)(2,1)S(1)}, bf16[8,256,128]{2,1,0:T(8,128)(2,1)S(1)}, u32[]{:S(2)}, u32[]{:S(2)}) collective-permute-start(bf16[8,256,128]{2,1,0:T(8,128)(2,1)S(1)} %get-tuple-element.83), channel_id=1, source_target_pairs={{0,2},{2,0},{4,6},{6,4},{8,10},{10,8},{12,14},{14,12},{16,18},{18,... | collective-permute-start | bytes 1572872 | tf_op jit(solution)/shard_map/ppermute | solution.py:42
  83.8 13.8 %collective-permute-start.19 = (bf16[8,256,128]{2,1,0:T(8,128)(2,1)S(1)}, bf16[8,256,128]{2,1,0:T(8,128)(2,1)S(1)}, u32[]{:S(2)}, u32[]{:S(2)}) collective-permute-start(bf16[8,256,128]{2,1,0:T(8,128)(2,1)S(1)} %get-tuple-element.87), channel_id=1, source_target_pairs={{0,2},{2,0},{4,6},{6,4},{8,10},{10,8},{12,14},{14,12},{16,18},{18,... | collective-permute-start | bytes 1572872 | tf_op jit(solution)/shard_map/ppermute | solution.py:42
  84.3 13.3 %collective-permute-start.20 = (bf16[8,256,128]{2,1,0:T(8,128)(2,1)S(1)}, bf16[8,256,128]{2,1,0:T(8,128)(2,1)S(1)}, u32[]{:S(2)}, u32[]{:S(2)}) collective-permute-start(bf16[8,256,128]{2,1,0:T(8,128)(2,1)S(1)} %get-tuple-element.88), channel_id=1, source_target_pairs={{0,2},{2,0},{4,6},{6,4},{8,10},{10,8},{12,14},{14,12},{16,18},{18,... | collective-permute-start | bytes 1572872 | tf_op jit(solution)/shard_map/ppermute | solution.py:42
  84.4 14.1 %collective-permute-start.22 = (bf16[2,1,8,72,128]{4,3,2,1,0:T(8,128)(2,1)S(1)}, bf16[2,1,8,72,128]{4,3,2,1,0:T(8,128)(2,1)S(1)}, u32[]{:S(2)}, u32[]{:S(2)}) collective-permute-start(bf16[2,1,8,72,128]{4,3,2,1,0:T(8,128)(2,1)S(1)} %collective-permute-done.15.refs_5_), channel_id=1, source_target_pairs={{0,8},{2,10},{4,12},{6,14},{8,0},{10,2},{12,4},{14,6},{16,24},{18,... | collective-permute-start | bytes 884744 | tf_op jit(solution)/shard_map/ppermute | solution.py:42
  100.7 1.9 %collective-permute-start.23 = (bf16[2,8,112,128]{3,2,1,0:T(8,128)(2,1)S(1)}, bf16[2,8,112,128]{3,2,1,0:T(8,128)(2,1)S(1)}, u32[]{:S(2)}, u32[]{:S(2)}) collective-permute-start(bf16[2,8,112,128]{3,2,1,0:T(8,128)(2,1)S(1)} %get-tuple-element.95), channel_id=1, source_target_pairs={{0,2},{2,0},{4,6},{6,4},{8,10},{10,8},{12,14},{14,12},{16,18},{18,... | collective-permute-start | bytes 1376264 | tf_op jit(solution)/shard_map/ppermute | solution.py:42

commit v3 on v2

--- a/solution.py
+++ b/solution.py
@@ -46,13 +46,26 @@
     return jnp.concatenate([column_block] * times, axis=1)
 
 
-def attend(query, key, value):
-    scores = dot_nt(query, key)
+def attended(scores, value):
     peak = jnp.max(scores, axis=1, keepdims=True)
     weights = jnp.exp2((scores - peak) * scaling2).astype(bf16)
     both = dot_nn(weights, jnp.concatenate([value, jnp.ones_like(value)], axis=1))
     total = both[:, HEAD_DIM:]
     return both[:, :HEAD_DIM] / total, peak * scaling2 + jnp.log2(total)
+
+
+def attend(query, key, value):
+    return attended(dot_nt(query, key), value)
+
+
+def staggered(items, begin, end, depth=2):
+    waiting = []
+    for item in items:
+        waiting.append(begin(*item))
+        if len(waiting) > depth:
+            end(*waiting.pop(0))
+    for item in waiting:
+        end(*item)
 
 
 def merged(out_a, lse_a, out_b, lse_b):
@@ -128,6 +141,19 @@
             return carry
 
         lax.fori_loop(0, self.heads // together, step, 0)
+
+
+def head_groups(heads, together, body):
+    together = min(together, heads)
+
+    def step(i, carry):
+        body([i * together + slot for slot in range(together)])
+        return carry
+
+    if together == heads:
+        body(list(range(heads)))
+    else:
+        lax.fori_loop(0, heads // together, step, 0)
 
 
 def lanes(h):
@@ -283,12 +309,13 @@
 def far_forward_body(plan, layout, meta, off, q, *refs):
     pieces, out, lse = refs[:-2], refs[-2], refs[-1]
 
-    def one(h, slot):
-        o, l2 = attend(q[0, 0, h], gathered(pieces, layout, 0, h), gathered(pieces, layout, 1, h))
-        out[h] = o
-        lse[h] = l2
-
-    plan.each_head(4, one)
+    def begin(h):
+        return h, dot_nt(q[0, 0, h], gathered(pieces, layout, 0, h))
+
+    def end(h, scores):
+        out[h], lse[h] = attended(scores, gathered(pieces, layout, 1, h))
+
+    head_groups(plan.heads, 8, lambda hs: staggered([(h,) for h in hs], begin, end))
 
 
 def far_forward(plan, branch, q, pieces):
@@ -605,43 +632,48 @@
     kvs, msgs, (own, send) = refs[: len(branches)], refs[len(branches) : -2], refs[-2:]
     msgs, q_two = msgs[: sum(counts)], msgs[sum(counts) : sum(counts) + 2]
 
-    def one(h, slot):
-        row = first_row
-        for j, branch in enumerate(branches):
-            taken = plan.taken(branch)
-            grads, queries, halves_of = [], [], [None] * (plan.rows // HEAD_DIM)
-            place = 0
-            mine = msgs[sum(counts[:j]) : sum(counts[: j + 1])]
-            for ref, (many, start, _) in zip(mine, layouts[j], strict=True):
-                table_at = start + 2 * taken
-                for n in range(many):
-                    grads.append(ref[n, 0, h, start:table_at, :])
-                    if branch != 2:
-                        queries.append(ref[n, 0, h, table_at + STAT_ROWS : table_at + STAT_ROWS + 2 * taken, :])
-                    terms = ref[n, 0, h, table_at : table_at + STAT_ROWS, :].astype(f32)
-                    half, shift = divmod(place, HEAD_DIM)
-                    if shift:
-                        terms = pltpu.roll(terms, shift, 1)
-                    halves_of[half] = terms if halves_of[half] is None else halves_of[half] + terms
-                    place += 2 * taken
-            if branch == 2:
-                queries = [ref[0, 0, h] for ref in q_two]
-            grad = jnp.concatenate(grads, axis=0)
-            query = jnp.concatenate(queries, axis=0)
-            table = jnp.concatenate(halves_of, axis=1)
-            lse = table[0:1] + table[1:2] + table[2:3]
-            delta = table[3:4] + table[4:5]
-            key, value = kvs[j][0, 0, h], kvs[j][0, 1, h]
-            probs = jnp.exp2(dot_nt(key, query) * scaling2 - lse)
-            ds = (probs * (dot_nt(value, grad) - delta)).astype(bf16)
-            dkey = dot_nn(ds, query) * scaling
-            dvalue = dot_nn(probs.astype(bf16), grad)
-            for i, rows in enumerate((dkey, dvalue)):
-                own[i, h, row : row + taken, :] = rows[:taken]
-                send[i, h, row : row + taken, :] = rows[taken:].astype(bf16)
-            row += taken
-
-    plan.each_head(4, one)
+    def begin(h, j, branch):
+        taken = plan.taken(branch)
+        grads, queries, halves_of = [], [], [None] * (plan.rows // HEAD_DIM)
+        place = 0
+        mine = msgs[sum(counts[:j]) : sum(counts[: j + 1])]
+        for ref, (many, start, _) in zip(mine, layouts[j], strict=True):
+            table_at = start + 2 * taken
+            for n in range(many):
+                grads.append(ref[n, 0, h, start:table_at, :])
+                if branch != 2:
+                    queries.append(ref[n, 0, h, table_at + STAT_ROWS : table_at + STAT_ROWS + 2 * taken, :])
+                terms = ref[n, 0, h, table_at : table_at + STAT_ROWS, :].astype(f32)
+                half, shift = divmod(place, HEAD_DIM)
+                if shift:
+                    terms = pltpu.roll(terms, shift, 1)
+                halves_of[half] = terms if halves_of[half] is None else halves_of[half] + terms
+                place += 2 * taken
+        if branch == 2:
+            queries = [ref[0, 0, h] for ref in q_two]
+        grad = jnp.concatenate(grads, axis=0)
+        query = jnp.concatenate(queries, axis=0)
+        table = jnp.concatenate(halves_of, axis=1)
+        lse = table[0:1] + table[1:2] + table[2:3]
+        delta = table[3:4] + table[4:5]
+        key, value = kvs[j][0, 0, h], kvs[j][0, 1, h]
+        return h, branch, query, grad, lse, delta, dot_nt(key, query), dot_nt(value, grad)
+
+    def end(h, branch, query, grad, lse, delta, scores, dprob):
+        taken = plan.taken(branch)
+        row = first_row + sum(plan.taken(b) for b in branches if b < branch)
+        probs = jnp.exp2(scores * scaling2 - lse)
+        ds = (probs * (dprob - delta)).astype(bf16)
+        dkey = dot_nn(ds, query) * scaling
+        dvalue = dot_nn(probs.astype(bf16), grad)
+        for i, rows in enumerate((dkey, dvalue)):
+            own[i, h, row : row + taken, :] = rows[:taken]
+            send[i, h, row : row + taken, :] = rows[taken:].astype(bf16)
+
+    def group(hs):
+        staggered([(h, j, b) for j, b in enumerate(branches) for h in hs], begin, end)
+
+    head_groups(plan.heads, 4, group)
 
 
 def far_backward(plan, branches, kvs, pieces, q_two, wait_for, before=()):

time: 106 us -> 103 us (0.972)
  Pallas kernels: 46.3 us -> 42.9 us
    pallas_call x20, Pallas kernels: 46.3 us -> 42.9 us  [call(): pl.pallas_call(without_waited if waited else body, out_shape=outs, in_spe...]
  transfers between devices with their start and end apart: 24 -> 24, of which waited for: 9 -> 9; matrix products, arithmetic and copies ran while one was open for 0% -> 0% of each run, Pallas kernels for 33% -> 31%
where the time goes in v3:
time: 103 us
  Pallas kernels  42.9 us (42%)
  waiting for transfers between devices  31.7 us (31%)
  starting transfers between devices  26.4 us (26%)
    pallas_call x20, Pallas kernels, call(): pl.pallas_call(without_waited if waited else body, out_shape=outs, in_spe...  42.9 us
    ppermute x24, waiting for transfers between devices, flip(): return lax.ppermute(block, axis, [(i, i ^ mask) for i in range(count)])  31.7 us
    ppermute x24, starting transfers between devices, flip(): return lax.ppermute(block, axis, [(i, i ^ mask) for i in range(count)])  26.4 us
  transfers between devices with their start and end apart: 24, of which 9 were waited for; matrix products, arithmetic and copies ran while one was open for 0% of the time, Pallas kernels for 31%

profile of v3, /device:TPU:0, one launch (start us, length us, event | category | flops | bytes accessed | tf_op | source)
XLA Modules:
  0.0 102.8 jit_solution(2536917217229001077)
XLA Ops:
  0.6 0.1 pad_add_fusion.meta.refs_0_
  0.7 0.7 copy-done.5
  1.4 2.1 %halves.3 = bf16[3,256,1024]{2,1,0:T(8,128)(2,1)S(1)} custom-call(s32[2]{0:T(128)S(1)} %pad_add_fusion.meta.refs_0_, s32[4,32]{1,0:T(4,128)S(1)} %copy-done.5, bf16[256,2048]{1,0:T(8,128)(2,1)} %refs_2_.5, bf16[256,2048]{1,0:T(8,128)(2,1)} %refs_6_.1, bf16[256,2048]{1,0:T(8,128)(2,1)} %refs_7_.1), custom_call_target="tpu_custom_call" | custom-call | tf_op jit(solution)/shard_map/halves/pallas_call | solution.py:114
  3.5 0.0 copy-start
  3.5 0.0 copy-start.1
  3.5 0.0 copy-start.6
  3.6 0.6 collective-permute-start.1
  4.1 1.9 %halves.2 = bf16[2,256,1024]{2,1,0:T(8,128)(2,1)S(1)} custom-call(s32[2]{0:T(128)S(1)} %pad_add_fusion.meta.refs_0_, s32[4,32]{1,0:T(4,128)S(1)} %copy-done.5, bf16[256,2048]{1,0:T(8,128)(2,1)} %refs_3_.1, bf16[256,2048]{1,0:T(8,128)(2,1)} %refs_4_.1), custom_call_target="tpu_custom_call" | custom-call | tf_op jit(solution)/shard_map/halves/pallas_call | solution.py:114
  6.0 0.0 copy-start.2
  6.1 0.1 collective-permute-start
  6.1 2.6 %collective-permute-done.kv_got.refs_2_.refs_3_.refs_5_ = bf16[2,256,1024]{2,1,0:T(8,128)(2,1)S(1)} collective-permute-done((bf16[2,256,1024]{2,1,0:T(8,128)(2,1)S(1)}, bf16[2,256,1024]{2,1,0:T(8,128)(2,1)S(1)}, u32[]{:S(2)}, u32[]{:S(2)}) %collective-permute-start) | collective-permute-done | bytes 1048608 | tf_op jit(solution)/shard_map/ppermute | solution.py:42
  8.8 1.6 %pick.3 = (bf16[1,2,8,128,128]{4,3,2,1,0:T(8,128)(2,1)S(1)}, bf16[1,2,8,64,128]{4,3,2,1,0:T(8,128)(2,1)S(1)}, bf16[1,2,8,32,128]{4,3,2,1,0:T(8,128)(2,1)S(1)}) custom-call(s32[2]{0:T(128)S(1)} %pad_add_fusion.meta.refs_0_, s32[4,32]{1,0:T(4,128)S(1)} %copy-done.6, bf16[256,2048]{1,0:T(8,128)(2,1)S(1)} %copy-done, bf16[256,2048]{1,0:T(8,128)(2,1)S(1)} %copy-done.1, ...), custom_call_target="tpu_custom_call" | custom-call | tf_op jit(solution)/shard_map/pick/pallas_call | solution.py:114
  10.4 2.9 %collective-permute-start.4 = (bf16[1,2,8,64,128]{4,3,2,1,0:T(8,128)(2,1)S(1)}, bf16[1,2,8,64,128]{4,3,2,1,0:T(8,128)(2,1)S(1)}, u32[]{:S(2)}, u32[]{:S(2)}) collective-permute-start(bf16[1,2,8,64,128]{4,3,2,1,0:T(8,128)(2,1)S(1)} %get-tuple-element.58.refs_0_.refs_10_.refs_12_.refs_3_), channel_id=1, source_target_pairs={{0,8},{2,10},{4,12},{6,14},{8,0},{10,2},{12,4},{14,6},{16,24},{18,... | collective-permute-start | bytes 786440 | tf_op jit(solution)/shard_map/ppermute | solution.py:42
  13.2 1.5 %collective-permute-start.3 = (bf16[1,2,8,64,128]{4,3,2,1,0:T(8,128)(2,1)S(1)}, bf16[1,2,8,64,128]{4,3,2,1,0:T(8,128)(2,1)S(1)}, u32[]{:S(2)}, u32[]{:S(2)}) collective-permute-start(bf16[1,2,8,64,128]{4,3,2,1,0:T(8,128)(2,1)S(1)} %get-tuple-element.58.refs_0_.refs_10_.refs_12_.refs_3_), channel_id=1, source_target_pairs={{0,4},{2,6},{4,0},{6,2},{8,12},{10,14},{12,8},{14,10},{16,20},{18,... | collective-permute-start | bytes 786440 | tf_op jit(solution)/shard_map/ppermute | solution.py:42
  14.7 2.6 %collective-permute-start.5 = (bf16[1,2,8,32,128]{4,3,2,1,0:T(8,128)(2,1)S(1)}, bf16[1,2,8,32,128]{4,3,2,1,0:T(8,128)(2,1)S(1)}, u32[]{:S(2)}, u32[]{:S(2)}) collective-permute-start(bf16[1,2,8,32,128]{4,3,2,1,0:T(8,128)(2,1)S(1)} %get-tuple-element.59.refs_3_.refs_0_.refs_14_.refs_16_.refs_2_), channel_id=1, source_target_pairs={{0,16},{2,18},{4,20},{6,22},{8,24},{10,26},{12,28},{14,30},{16,0},... | collective-permute-start | bytes 393224 | tf_op jit(solution)/shard_map/ppermute | solution.py:42
  17.3 0.5 collective-permute-start.2
  17.8 4.9 %near_forward.1 = (f32[8,512,128]{2,1,0:T(8,128)S(1)}, f32[8,512,128]{2,1,0:T(8,128)S(1)}) custom-call(s32[2]{0:T(128)S(1)} %pad_add_fusion.meta.refs_0_, s32[4,32]{1,0:T(4,128)S(1)} %copy-done.6, bf16[256,2048]{1,0:T(8,128)(2,1)S(1)} %copy-done.2, bf16[256,2048]{1,0:T(8,128)(2,1)S(1)} %copy-done, bf16[256,2048]{1,0:T(8,128)(2,1)S(1)} %copy-done.1, ...), custom_call_target="tpu_custom_call" | custom-call | tf_op jit(solution)/shard_map/near_forward/pallas_call | solution.py:114
  22.8 0.0 collective-permute-done.3.refs_2_.refs_1_.refs_11_.refs_13_
  22.8 0.7 relay.2
  23.5 2.8 %collective-permute-start.6 = (bf16[1,2,8,128,128]{4,3,2,1,0:T(8,128)(2,1)S(1)}, bf16[1,2,8,128,128]{4,3,2,1,0:T(8,128)(2,1)S(1)}, u32[]{:S(2)}, u32[]{:S(2)}) collective-permute-start(bf16[1,2,8,128,128]{4,3,2,1,0:T(8,128)(2,1)S(1)} %get-tuple-element.60), channel_id=1, source_target_pairs={{0,8},{2,10},{4,12},{6,14},{8,0},{10,2},{12,4},{14,6},{16,24},{18,... | collective-permute-start | bytes 1572872 | tf_op jit(solution)/shard_map/ppermute | solution.py:42
  26.3 1.5 %collective-permute-start.7 = (bf16[2,2,8,32,128]{4,3,2,1,0:T(8,128)(2,1)S(1)}, bf16[2,2,8,32,128]{4,3,2,1,0:T(8,128)(2,1)S(1)}, u32[]{:S(2)}, u32[]{:S(2)}) collective-permute-start(bf16[2,2,8,32,128]{4,3,2,1,0:T(8,128)(2,1)S(1)} %get-tuple-element.64), channel_id=1, source_target_pairs={{0,4},{2,6},{4,0},{6,2},{8,12},{10,14},{12,8},{14,10},{16,20},{18,... | collective-permute-start | bytes 786440 | tf_op jit(solution)/shard_map/ppermute | solution.py:42
  27.8 10.5 %collective-permute-done.7.refs_2_.refs_16_.refs_18_ = bf16[2,2,8,32,128]{4,3,2,1,0:T(8,128)(2,1)S(1)} collective-permute-done((bf16[2,2,8,32,128]{4,3,2,1,0:T(8,128)(2,1)S(1)}, bf16[2,2,8,32,128]{4,3,2,1,0:T(8,128)(2,1)S(1)}, u32[]{:S(2)}, u32[]{:S(2)}) %collective-permute-start.7) | collective-permute-done | bytes 262176 | tf_op jit(solution)/shard_map/ppermute | solution.py:42
  38.3 0.4 collective-permute-start.8
  38.6 1.1 %pick.2 = (bf16[1,1,8,128,128]{4,3,2,1,0:T(8,128)(2,1)S(1)}, bf16[1,1,8,64,128]{4,3,2,1,0:T(8,128)(2,1)S(1)}, bf16[1,1,8,32,128]{4,3,2,1,0:T(8,128)(2,1)S(1)}) custom-call(s32[2]{0:T(128)S(1)} %pad_add_fusion.meta.refs_0_, s32[4,32]{1,0:T(4,128)S(1)} %copy-done.6, bf16[256,2048]{1,0:T(8,128)(2,1)S(1)} %copy-done.2, ...), custom_call_target="tpu_custom_call" | custom-call | tf_op jit(solution)/shard_map/pick/pallas_call | solution.py:114
  39.7 0.0 copy-start.3
  39.7 0.0 copy-start.4
  39.7 0.0 copy-start.7
  39.7 1.7 %collective-permute-start.11 = (bf16[1,1,8,128,128]{4,3,2,1,0:T(8,128)(2,1)S(1)}, bf16[1,1,8,128,128]{4,3,2,1,0:T(8,128)(2,1)S(1)}, u32[]{:S(2)}, u32[]{:S(2)}) collective-permute-start(bf16[1,1,8,128,128]{4,3,2,1,0:T(8,128)(2,1)S(1)} %get-tuple-element.53.q.refs_10_), channel_id=1, source_target_pairs={{0,4},{2,6},{4,0},{6,2},{8,12},{10,14},{12,8},{14,10},{16,20},{18,... | collective-permute-start | bytes 786440 | tf_op jit(solution)/shard_map/ppermute | solution.py:42
  41.4 1.2 %far_forward2.1 = (f32[8,128,128]{2,1,0:T(8,128)S(1)}, f32[8,128,128]{2,1,0:T(8,128)S(1)}) custom-call(s32[2]{0:T(128)S(1)} %pad_add_fusion.meta.refs_0_, s32[4,32]{1,0:T(4,128)S(1)} %copy-done.6, bf16[1,1,8,128,128]{4,3,2,1,0:T(8,128)(2,1)S(1)} %get-tuple-element.53.q.refs_10_, ...), custom_call_target="tpu_custom_call" | custom-call | tf_op jit(solution)/shard_map/far_forward2/pallas_call | solution.py:114
  42.6 1.2 %far_forward3.1 = (f32[8,64,128]{2,1,0:T(8,128)S(1)}, f32[8,64,128]{2,1,0:T(8,128)S(1)}) custom-call(s32[2]{0:T(128)S(1)} %pad_add_fusion.meta.refs_0_, s32[4,32]{1,0:T(4,128)S(1)} %copy-done.6, bf16[1,1,8,64,128]{4,3,2,1,0:T(8,128)(2,1)S(1)} %get-tuple-element.57.q.refs_11_, ...), custom_call_target="tpu_custom_call" | custom-call | tf_op jit(solution)/shard_map/far_forward3/pallas_call | solution.py:114
  43.9 1.8 %collective-permute-done.8.refs_5_.refs_19_.refs_21_ = bf16[2,2,8,32,128]{4,3,2,1,0:T(8,128)(2,1)S(1)} collective-permute-done((bf16[2,2,8,32,128]{4,3,2,1,0:T(8,128)(2,1)S(1)}, bf16[2,2,8,32,128]{4,3,2,1,0:T(8,128)(2,1)S(1)}, u32[]{:S(2)}, u32[]{:S(2)}) %collective-permute-start.8) | collective-permute-done | bytes 262176 | tf_op jit(solution)/shard_map/ppermute | solution.py:42
  45.6 1.2 %far_forward4.1 = (f32[8,32,128]{2,1,0:T(8,128)S(1)}, f32[8,32,128]{2,1,0:T(8,128)S(1)}) custom-call(s32[2]{0:T(128)S(1)} %pad_add_fusion.meta.refs_0_, s32[4,32]{1,0:T(4,128)S(1)} %copy-done.6, bf16[1,1,8,32,128]{4,3,2,1,0:T(8,128)(2,1)S(1)} %get-tuple-element.63.q.refs_12_, ...), custom_call_target="tpu_custom_call" | custom-call | tf_op jit(solution)/shard_map/far_forward4/pallas_call | solution.py:114
  46.8 0.0 copy-start.8
  46.8 3.6 %combine.1 = (f32[8,512,128]{2,1,0:T(8,128)S(1)}, f32[8,512,128]{2,1,0:T(8,128)S(1)}, f32[8,512]{1,0:T(8,128)S(1)}) custom-call(s32[2]{0:T(128)S(1)} %pad_add_fusion.meta.refs_0_, s32[4,32]{1,0:T(4,128)S(1)} %copy-done.6, f32[8,512,128]{2,1,0:T(8,128)S(1)} %get-tuple-element.51.refs_0_, f32[8,512,128]{2,1,0:T(8,128)S(1)} %get-tuple-element.52.refs_5_.refs_1_, ...), custom_call_target="tpu_custom_call" | custom-call | tf_op jit(solution)/shard_map/combine/pallas_call | solution.py:114
  50.5 0.0 collective-permute-start.9
  50.5 1.2 %collective-permute-done.9.other = f32[8,512]{1,0:T(8,128)S(1)} collective-permute-done((f32[8,512]{1,0:T(8,128)S(1)}, f32[8,512]{1,0:T(8,128)S(1)}, u32[]{:S(2)}, u32[]{:S(2)}) %collective-permute-start.9) | collective-permute-done | bytes 16416 | tf_op jit(solution)/shard_map/ppermute | solution.py:42
  51.7 0.6 join.1.refs_2_
  52.3 1.6 %collective-permute-start.10 = (f32[8,512]{1,0:T(8,128)S(1)}, f32[8,512]{1,0:T(8,128)S(1)}, u32[]{:S(2)}, u32[]{:S(2)}) collective-permute-start(f32[8,512]{1,0:T(8,128)S(1)} %join.1.refs_2_), channel_id=1, source_target_pairs={{0,1},{1,0},{2,3},{3,2},{4,5},{5,4},{6,7},{7,6},{8,9},{9,8},{10,11... | collective-permute-start | bytes 49160 | tf_op jit(solution)/shard_map/ppermute | solution.py:42
  53.8 2.2 %collective-permute-done.10.refs_3_ = f32[8,512]{1,0:T(8,128)S(1)} collective-permute-done((f32[8,512]{1,0:T(8,128)S(1)}, f32[8,512]{1,0:T(8,128)S(1)}, u32[]{:S(2)}, u32[]{:S(2)}) %collective-permute-start.10) | collective-permute-done | bytes 16416 | tf_op jit(solution)/shard_map/ppermute | solution.py:42
  56.1 4.1 %norm.1 = (bf16[256,1024]{1,0:T(8,128)(2,1)S(1)}, bf16[8,256,128]{2,1,0:T(8,128)(2,1)S(1)}, bf16[8,512,128]{2,1,0:T(8,128)(2,1)S(1)}, f32[8,512,128]{2,1,0:T(8,1...) custom-call(s32[2]{0:T(128)S(1)} %pad_add_fusion.meta.refs_0_, ...), custom_call_target="tpu_custom_call" | custom-call | tf_op jit(solution)/shard_map/norm/pallas_call | solution.py:114
  60.2 0.1 collective-permute-start.17
  60.3 0.7 collective-permute-start.14
  61.0 1.3 %collective-permute-start.12 = (bf16[1,1,8,136,128]{4,3,2,1,0:T(8,128)(2,1)S(1)}, bf16[1,1,8,136,128]{4,3,2,1,0:T(8,128)(2,1)S(1)}, u32[]{:S(2)}, u32[]{:S(2)}) collective-permute-start(bf16[1,1,8,136,128]{4,3,2,1,0:T(8,128)(2,1)S(1)} %get-tuple-element.70.refs_6_), channel_id=1, source_target_pairs={{0,4},{2,6},{4,0},{6,2},{8,12},{10,14},{12,8},{14,10},{16,20},{18,... | collective-permute-start | bytes 835592 | tf_op jit(solution)/shard_map/ppermute | solution.py:42
  62.3 0.7 collective-permute-start.16
  63.0 2.4 %collective-permute-start.13 = (bf16[1,1,8,72,128]{4,3,2,1,0:T(8,128)(2,1)S(1)}, bf16[1,1,8,72,128]{4,3,2,1,0:T(8,128)(2,1)S(1)}, u32[]{:S(2)}, u32[]{:S(2)}) collective-permute-start(bf16[1,1,8,72,128]{4,3,2,1,0:T(8,128)(2,1)S(1)} %get-tuple-element.71.refs_3_), channel_id=1, source_target_pairs={{0,16},{2,18},{4,20},{6,22},{8,24},{10,26},{12,28},{14,30},{16,0},... | collective-permute-start | bytes 442376 | tf_op jit(solution)/shard_map/ppermute | solution.py:42
  65.4 2.4 %near_backward0.1 = (f32[3,8,256,128]{3,2,1,0:T(8,128)S(1)}, bf16[8,256,128]{2,1,0:T(8,128)(2,1)S(1)}, bf16[8,256,128]{2,1,0:T(8,128)(2,1)S(1)}, bf16[8,256,128]{2,1,0:T(8,128)(2,1)S(1)}) custom-call(s32[2]{0:T(128)S(1)} %pad_add_fusion.meta.refs_0_, s32[4,32]{1,0:T(4,128)S(1)} %copy-done.6, bf16[256,2048]{1,0:T(8,128)(2,1)S(1)} %copy-done.2, ...), custom_call_target="tpu_custom_call" | custom-call | tf_op jit(solution)/shard_map/near_backward0/pallas_call | solution.py:114
  67.8 2.9 %collective-permute-done.13.refs_4_ = bf16[1,1,8,72,128]{4,3,2,1,0:T(8,128)(2,1)S(1)} collective-permute-done((bf16[1,1,8,72,128]{4,3,2,1,0:T(8,128)(2,1)S(1)}, bf16[1,1,8,72,128]{4,3,2,1,0:T(8,128)(2,1)S(1)}, u32[]{:S(2)}, u32[]{:S(2)}) %collective-permute-start.13) | collective-permute-done | bytes 147488 | tf_op jit(solution)/shard_map/ppermute | solution.py:42
  70.7 1.8 %collective-permute-done.14.refs_6_.refs_8_ = bf16[1,1,8,136,128]{4,3,2,1,0:T(8,128)(2,1)S(1)} collective-permute-done((bf16[1,1,8,136,128]{4,3,2,1,0:T(8,128)(2,1)S(1)}, bf16[1,1,8,136,128]{4,3,2,1,0:T(8,128)(2,1)S(1)}, u32[]{:S(2)}, u32[]{:S(2)}) %collective-permute-start.14) | collective-permute-done | bytes 278560 | tf_op jit(solution)/shard_map/ppermute | solution.py:42
  72.5 0.6 relay.3
  73.1 1.6 %collective-permute-start.15 = (bf16[2,1,8,72,128]{4,3,2,1,0:T(8,128)(2,1)S(1)}, bf16[2,1,8,72,128]{4,3,2,1,0:T(8,128)(2,1)S(1)}, u32[]{:S(2)}, u32[]{:S(2)}) collective-permute-start(bf16[2,1,8,72,128]{4,3,2,1,0:T(8,128)(2,1)S(1)} %get-tuple-element.75.refs_26_), channel_id=1, source_target_pairs={{0,4},{2,6},{4,0},{6,2},{8,12},{10,14},{12,8},{14,10},{16,20},{18,... | collective-permute-start | bytes 884744 | tf_op jit(solution)/shard_map/ppermute | solution.py:42
  74.7 2.6 %collective-permute-start.21 = (bf16[1,1,8,280,128]{4,3,2,1,0:T(8,128)(2,1)S(1)}, bf16[1,1,8,280,128]{4,3,2,1,0:T(8,128)(2,1)S(1)}, u32[]{:S(2)}, u32[]{:S(2)}) collective-permute-start(bf16[1,1,8,280,128]{4,3,2,1,0:T(8,128)(2,1)S(1)} %get-tuple-element.89), channel_id=1, source_target_pairs={{0,8},{2,10},{4,12},{6,14},{8,0},{10,2},{12,4},{14,6},{16,24},{18,... | collective-permute-start | bytes 1720328 | tf_op jit(solution)/shard_map/ppermute | solution.py:42
  77.3 6.0 %near_backward2.1 = (f32[3,8,256,128]{3,2,1,0:T(8,128)S(1)}, bf16[8,256,128]{2,1,0:T(8,128)(2,1)S(1)}, bf16[8,256,128]{2,1,0:T(8,128)(2,1)S(1)}, bf16[8,256,128]{2,1,0:T(8,128)(2,1)S(1)}) custom-call(s32[2]{0:T(128)S(1)} %pad_add_fusion.meta.refs_0_, ...), custom_call_target="tpu_custom_call", output_to_operand_aliasing={{0}: (22, {}), {1}: (23, {}), {2}: (24, {}), {3}: (25, {})} | custom-call | tf_op jit(solution)/shard_map/near_backward2/pallas_call | solution.py:114
  83.4 0.1 collective-permute-start.18
  83.4 0.5 collective-permute-start.19
  83.9 0.1 collective-permute-start.20
  84.0 0.2 collective-permute-start.22
  84.3 6.9 %collective-permute-done.21.refs_9_.refs_6_.refs_7_ = bf16[1,1,8,280,128]{4,3,2,1,0:T(8,128)(2,1)S(1)} collective-permute-done((bf16[1,1,8,280,128]{4,3,2,1,0:T(8,128)(2,1)S(1)}, bf16[1,1,8,280,128]{4,3,2,1,0:T(8,128)(2,1)S(1)}, u32[]{:S(2)}, u32[]{:S(2)}) %collective-permute-start.21) | collective-permute-done | bytes 573472 | tf_op jit(solution)/shard_map/ppermute | solution.py:42
  91.1 2.0 %far_backward2.1 = (f32[2,8,112,128]{3,2,1,0:T(8,128)S(1)}, bf16[2,8,112,128]{3,2,1,0:T(8,128)(2,1)S(1)}) custom-call(s32[2]{0:T(128)S(1)} %pad_add_fusion.meta.refs_0_, s32[4,32]{1,0:T(4,128)S(1)} %copy-done.6, bf16[1,2,8,128,128]{4,3,2,1,0:T(8,128)(2,1)S(1)} %get-tuple-element.54.refs_0_.refs_8_.refs_10_.refs_2_, ...), custom_call_target="tpu_custom_call" | custom-call | tf_op jit(solution)/shard_map/far_backward2/pallas_call | solution.py:114
  93.2 2.4 %finish_q.1 = (f32[256,2048]{1,0:T(8,128)}, bf16[256,2048]{1,0:T(8,128)(2,1)}, f32[8,128]{1,0:T(8,128)S(1)}) custom-call(s32[2]{0:T(128)S(1)} %pad_add_fusion.meta.refs_0_, s32[4,32]{1,0:T(4,128)S(1)} %copy-done.6, f32[3,8,256,128]{3,2,1,0:T(8,128)S(1)} %get-tuple-element.82.own.refs_12_, bf16[8,256,128]{2,1,0:T(8,128)(2,1)S(1)} %collective-permute-done.18.got, ...), custom_call_target="tpu_custom_call" | custom-call | tf_op jit(solution)/shard_map/finish_q/pallas_call | solution.py:114
  95.6 0.8 fold.1.refs_12_.given
  96.5 1.5 %far_backward4.1 = (f32[2,8,112,128]{3,2,1,0:T(8,128)S(1)}, bf16[2,8,112,128]{3,2,1,0:T(8,128)(2,1)S(1)}) custom-call(s32[2]{0:T(128)S(1)} %pad_add_fusion.meta.refs_0_, s32[4,32]{1,0:T(4,128)S(1)} %copy-done.6, ...), custom_call_target="tpu_custom_call", output_to_operand_aliasing={{0}: (9, {}), {1}: (10, {})} | custom-call | tf_op jit(solution)/shard_map/far_backward4/pallas_call | solution.py:114
  98.0 0.1 collective-permute-start.23
  98.1 1.8 %collective-permute-done.23.refs_1_ = bf16[2,8,112,128]{3,2,1,0:T(8,128)(2,1)S(1)} collective-permute-done((bf16[2,8,112,128]{3,2,1,0:T(8,128)(2,1)S(1)}, bf16[2,8,112,128]{3,2,1,0:T(8,128)(2,1)S(1)}, u32[]{:S(2)}, u32[]{:S(2)}) %collective-permute-start.23) | collective-permute-done | bytes 458784 | tf_op jit(solution)/shard_map/ppermute | solution.py:42
  99.9 2.9 %finish_kv.1 = (f32[256,2048]{1,0:T(8,128)}, f32[256,2048]{1,0:T(8,128)}) custom-call(s32[2]{0:T(128)S(1)} %pad_add_fusion.meta.refs_0_, s32[4,32]{1,0:T(4,128)S(1)} %copy-done.6, f32[2,16,256,128]{3,2,1,0:T(8,128)S(1)} %fold.1.refs_12_.given, f32[2,8,112,128]{3,2,1,0:T(8,128)S(1)} %get-tuple-element.94.refs_0_, ...), custom_call_target="tpu_custom_call" | custom-call | tf_op jit(solution)/shard_map/finish_kv/pallas_call | solution.py:114
  (23 shorter events, 0.1 us)
Async XLA Ops:
  0.7 0.7 copy-start.5
  3.5 5.3 %copy-start = (bf16[256,2048]{1,0:T(8,128)(2,1)S(1)}, bf16[256,2048]{1,0:T(8,128)(2,1)}, u32[]{:S(2)}) copy-start(bf16[256,2048]{1,0:T(8,128)(2,1)} %refs_3_.1) | copy-start | bytes 3145732
  3.5 5.3 %copy-start.1 = (bf16[256,2048]{1,0:T(8,128)(2,1)S(1)}, bf16[256,2048]{1,0:T(8,128)(2,1)}, u32[]{:S(2)}) copy-start(bf16[256,2048]{1,0:T(8,128)(2,1)} %refs_4_.1) | copy-start | bytes 3145732
  3.5 5.2 %copy-start.6 = (s32[4,32]{1,0:T(4,128)S(1)}, s32[4,32]{1,0:T(4,128)}, u32[]{:S(2)}) copy-start(s32[4,32]{1,0:T(4,128)} %off.27) | copy-start | bytes 1540
  3.6 14.3 %collective-permute-start.1 = (bf16[3,256,1024]{2,1,0:T(8,128)(2,1)S(1)}, bf16[3,256,1024]{2,1,0:T(8,128)(2,1)S(1)}, u32[]{:S(2)}, u32[]{:S(2)}) collective-permute-start(bf16[3,256,1024]{2,1,0:T(8,128)(2,1)S(1)} %halves.3), channel_id=1, source_target_pairs={{0,2},{2,0},{4,6},{6,4},{8,10},{10,8},{12,14},{14,12},{16,18},{18,... | collective-permute-start | bytes 4718600 | tf_op jit(solution)/shard_map/ppermute | solution.py:42
  6.0 11.8 %copy-start.2 = (bf16[256,2048]{1,0:T(8,128)(2,1)S(1)}, bf16[256,2048]{1,0:T(8,128)(2,1)}, u32[]{:S(2)}) copy-start(bf16[256,2048]{1,0:T(8,128)(2,1)} %refs_2_.5) | copy-start | bytes 3145732
  6.1 2.7 %collective-permute-start = (bf16[2,256,1024]{2,1,0:T(8,128)(2,1)S(1)}, bf16[2,256,1024]{2,1,0:T(8,128)(2,1)S(1)}, u32[]{:S(2)}, u32[]{:S(2)}) collective-permute-start(bf16[2,256,1024]{2,1,0:T(8,128)(2,1)S(1)} %halves.2), channel_id=1, source_target_pairs={{0,2},{2,0},{4,6},{6,4},{8,10},{10,8},{12,14},{14,12},{16,18},{18,... | collective-permute-start | bytes 3145736 | tf_op jit(solution)/shard_map/ppermute | solution.py:42
  10.4 12.4 %collective-permute-start.4 = (bf16[1,2,8,64,128]{4,3,2,1,0:T(8,128)(2,1)S(1)}, bf16[1,2,8,64,128]{4,3,2,1,0:T(8,128)(2,1)S(1)}, u32[]{:S(2)}, u32[]{:S(2)}) collective-permute-start(bf16[1,2,8,64,128]{4,3,2,1,0:T(8,128)(2,1)S(1)} %get-tuple-element.58.refs_0_.refs_10_.refs_12_.refs_3_), channel_id=1, source_target_pairs={{0,8},{2,10},{4,12},{6,14},{8,0},{10,2},{12,4},{14,6},{16,24},{18,... | collective-permute-start | bytes 786440 | tf_op jit(solution)/shard_map/ppermute | solution.py:42
  13.2 9.6 %collective-permute-start.3 = (bf16[1,2,8,64,128]{4,3,2,1,0:T(8,128)(2,1)S(1)}, bf16[1,2,8,64,128]{4,3,2,1,0:T(8,128)(2,1)S(1)}, u32[]{:S(2)}, u32[]{:S(2)}) collective-permute-start(bf16[1,2,8,64,128]{4,3,2,1,0:T(8,128)(2,1)S(1)} %get-tuple-element.58.refs_0_.refs_10_.refs_12_.refs_3_), channel_id=1, source_target_pairs={{0,4},{2,6},{4,0},{6,2},{8,12},{10,14},{12,8},{14,10},{16,20},{18,... | collective-permute-start | bytes 786440 | tf_op jit(solution)/shard_map/ppermute | solution.py:42
  14.7 8.0 %collective-permute-start.5 = (bf16[1,2,8,32,128]{4,3,2,1,0:T(8,128)(2,1)S(1)}, bf16[1,2,8,32,128]{4,3,2,1,0:T(8,128)(2,1)S(1)}, u32[]{:S(2)}, u32[]{:S(2)}) collective-permute-start(bf16[1,2,8,32,128]{4,3,2,1,0:T(8,128)(2,1)S(1)} %get-tuple-element.59.refs_3_.refs_0_.refs_14_.refs_16_.refs_2_), channel_id=1, source_target_pairs={{0,16},{2,18},{4,20},{6,22},{8,24},{10,26},{12,28},{14,30},{16,0},... | collective-permute-start | bytes 393224 | tf_op jit(solution)/shard_map/ppermute | solution.py:42
  17.3 24.1 %collective-permute-start.2 = (bf16[1,2,8,128,128]{4,3,2,1,0:T(8,128)(2,1)S(1)}, bf16[1,2,8,128,128]{4,3,2,1,0:T(8,128)(2,1)S(1)}, u32[]{:S(2)}, u32[]{:S(2)}) collective-permute-start(bf16[1,2,8,128,128]{4,3,2,1,0:T(8,128)(2,1)S(1)} %get-tuple-element.54.refs_0_.refs_8_.refs_10_.refs_2_), channel_id=1, source_target_pairs={{0,4},{2,6},{4,0},{6,2},{8,12},{10,14},{12,8},{14,10},{16,20},{18,... | collective-permute-start | bytes 1572872 | tf_op jit(solution)/shard_map/ppermute | solution.py:42
  23.5 19.1 %collective-permute-start.6 = (bf16[1,2,8,128,128]{4,3,2,1,0:T(8,128)(2,1)S(1)}, bf16[1,2,8,128,128]{4,3,2,1,0:T(8,128)(2,1)S(1)}, u32[]{:S(2)}, u32[]{:S(2)}) collective-permute-start(bf16[1,2,8,128,128]{4,3,2,1,0:T(8,128)(2,1)S(1)} %get-tuple-element.60), channel_id=1, source_target_pairs={{0,8},{2,10},{4,12},{6,14},{8,0},{10,2},{12,4},{14,6},{16,24},{18,... | collective-permute-start | bytes 1572872 | tf_op jit(solution)/shard_map/ppermute | solution.py:42
  26.3 12.0 %collective-permute-start.7 = (bf16[2,2,8,32,128]{4,3,2,1,0:T(8,128)(2,1)S(1)}, bf16[2,2,8,32,128]{4,3,2,1,0:T(8,128)(2,1)S(1)}, u32[]{:S(2)}, u32[]{:S(2)}) collective-permute-start(bf16[2,2,8,32,128]{4,3,2,1,0:T(8,128)(2,1)S(1)} %get-tuple-element.64), channel_id=1, source_target_pairs={{0,4},{2,6},{4,0},{6,2},{8,12},{10,14},{12,8},{14,10},{16,20},{18,... | collective-permute-start | bytes 786440 | tf_op jit(solution)/shard_map/ppermute | solution.py:42
  38.3 7.3 %collective-permute-start.8 = (bf16[2,2,8,32,128]{4,3,2,1,0:T(8,128)(2,1)S(1)}, bf16[2,2,8,32,128]{4,3,2,1,0:T(8,128)(2,1)S(1)}, u32[]{:S(2)}, u32[]{:S(2)}) collective-permute-start(bf16[2,2,8,32,128]{4,3,2,1,0:T(8,128)(2,1)S(1)} %collective-permute-done.7.refs_2_.refs_16_.refs_18_), channel_id=1, source_target_pairs={{0,8},{2,10},{4,12},{6,14},{8,0},{10,2},{12,4},{14,6},{16,24},{18,... | collective-permute-start | bytes 786440 | tf_op jit(solution)/shard_map/ppermute | solution.py:42
  39.7 7.1 %copy-start.3 = (bf16[256,2048]{1,0:T(8,128)(2,1)S(1)}, bf16[256,2048]{1,0:T(8,128)(2,1)}, u32[]{:S(2)}) copy-start(bf16[256,2048]{1,0:T(8,128)(2,1)} %refs_6_.1) | copy-start | bytes 3145732
  39.7 7.1 %copy-start.4 = (bf16[256,2048]{1,0:T(8,128)(2,1)S(1)}, bf16[256,2048]{1,0:T(8,128)(2,1)}, u32[]{:S(2)}) copy-start(bf16[256,2048]{1,0:T(8,128)(2,1)} %refs_7_.1) | copy-start | bytes 3145732
  39.7 7.1 %copy-start.7 = (f32[2048]{0:T(1024)S(1)}, f32[2048]{0:T(1024)}, u32[]{:S(2)}) copy-start(f32[2048]{0:T(1024)} %param.12) | copy-start | bytes 24580
  39.7 14.1 %collective-permute-start.11 = (bf16[1,1,8,128,128]{4,3,2,1,0:T(8,128)(2,1)S(1)}, bf16[1,1,8,128,128]{4,3,2,1,0:T(8,128)(2,1)S(1)}, u32[]{:S(2)}, u32[]{:S(2)}) collective-permute-start(bf16[1,1,8,128,128]{4,3,2,1,0:T(8,128)(2,1)S(1)} %get-tuple-element.53.q.refs_10_), channel_id=1, source_target_pairs={{0,4},{2,6},{4,0},{6,2},{8,12},{10,14},{12,8},{14,10},{16,20},{18,... | collective-permute-start | bytes 786440 | tf_op jit(solution)/shard_map/ppermute | solution.py:42
  46.8 9.3 %copy-start.8 = (f32[2048]{0:T(1024)S(1)}, f32[2048]{0:T(1024)}, u32[]{:S(2)}) copy-start(f32[2048]{0:T(1024)} %param.13) | copy-start | bytes 24580
  50.5 1.2 %collective-permute-start.9 = (f32[8,512]{1,0:T(8,128)S(1)}, f32[8,512]{1,0:T(8,128)S(1)}, u32[]{:S(2)}, u32[]{:S(2)}) collective-permute-start(f32[8,512]{1,0:T(8,128)S(1)} %get-tuple-element.67.mine), channel_id=1, source_target_pairs={{0,2},{2,0},{4,6},{6,4},{8,10},{10,8},{12,14},{14,12},{16,18},{18,... | collective-permute-start | bytes 49160 | tf_op jit(solution)/shard_map/ppermute | solution.py:42
  52.3 3.8 %collective-permute-start.10 = (f32[8,512]{1,0:T(8,128)S(1)}, f32[8,512]{1,0:T(8,128)S(1)}, u32[]{:S(2)}, u32[]{:S(2)}) collective-permute-start(f32[8,512]{1,0:T(8,128)S(1)} %join.1.refs_2_), channel_id=1, source_target_pairs={{0,1},{1,0},{2,3},{3,2},{4,5},{5,4},{6,7},{7,6},{8,9},{9,8},{10,11... | collective-permute-start | bytes 49160 | tf_op jit(solution)/shard_map/ppermute | solution.py:42
  60.2 17.1 %collective-permute-start.17 = (bf16[8,256,128]{2,1,0:T(8,128)(2,1)S(1)}, bf16[8,256,128]{2,1,0:T(8,128)(2,1)S(1)}, u32[]{:S(2)}, u32[]{:S(2)}) collective-permute-start(bf16[8,256,128]{2,1,0:T(8,128)(2,1)S(1)} %get-tuple-element.80), channel_id=1, source_target_pairs={{0,2},{2,0},{4,6},{6,4},{8,10},{10,8},{12,14},{14,12},{16,18},{18,... | collective-permute-start | bytes 1572872 | tf_op jit(solution)/shard_map/ppermute | solution.py:42
  60.3 12.2 %collective-permute-start.14 = (bf16[1,1,8,136,128]{4,3,2,1,0:T(8,128)(2,1)S(1)}, bf16[1,1,8,136,128]{4,3,2,1,0:T(8,128)(2,1)S(1)}, u32[]{:S(2)}, u32[]{:S(2)}) collective-permute-start(bf16[1,1,8,136,128]{4,3,2,1,0:T(8,128)(2,1)S(1)} %get-tuple-element.70.refs_6_), channel_id=1, source_target_pairs={{0,8},{2,10},{4,12},{6,14},{8,0},{10,2},{12,4},{14,6},{16,24},{18,... | collective-permute-start | bytes 835592 | tf_op jit(solution)/shard_map/ppermute | solution.py:42
  61.0 11.5 %collective-permute-start.12 = (bf16[1,1,8,136,128]{4,3,2,1,0:T(8,128)(2,1)S(1)}, bf16[1,1,8,136,128]{4,3,2,1,0:T(8,128)(2,1)S(1)}, u32[]{:S(2)}, u32[]{:S(2)}) collective-permute-start(bf16[1,1,8,136,128]{4,3,2,1,0:T(8,128)(2,1)S(1)} %get-tuple-element.70.refs_6_), channel_id=1, source_target_pairs={{0,4},{2,6},{4,0},{6,2},{8,12},{10,14},{12,8},{14,10},{16,20},{18,... | collective-permute-start | bytes 835592 | tf_op jit(solution)/shard_map/ppermute | solution.py:42
  62.3 15.0 %collective-permute-start.16 = (bf16[1,1,8,136,128]{4,3,2,1,0:T(8,128)(2,1)S(1)}, bf16[1,1,8,136,128]{4,3,2,1,0:T(8,128)(2,1)S(1)}, u32[]{:S(2)}, u32[]{:S(2)}) collective-permute-start(bf16[1,1,8,136,128]{4,3,2,1,0:T(8,128)(2,1)S(1)} %get-tuple-element.79.refs_4_), channel_id=1, source_target_pairs={{0,4},{2,6},{4,0},{6,2},{8,12},{10,14},{12,8},{14,10},{16,20},{18,... | collective-permute-start | bytes 835592 | tf_op jit(solution)/shard_map/ppermute | solution.py:42
  63.0 7.7 %collective-permute-start.13 = (bf16[1,1,8,72,128]{4,3,2,1,0:T(8,128)(2,1)S(1)}, bf16[1,1,8,72,128]{4,3,2,1,0:T(8,128)(2,1)S(1)}, u32[]{:S(2)}, u32[]{:S(2)}) collective-permute-start(bf16[1,1,8,72,128]{4,3,2,1,0:T(8,128)(2,1)S(1)} %get-tuple-element.71.refs_3_), channel_id=1, source_target_pairs={{0,16},{2,18},{4,20},{6,22},{8,24},{10,26},{12,28},{14,30},{16,0},... | collective-permute-start | bytes 442376 | tf_op jit(solution)/shard_map/ppermute | solution.py:42
  73.1 10.9 %collective-permute-start.15 = (bf16[2,1,8,72,128]{4,3,2,1,0:T(8,128)(2,1)S(1)}, bf16[2,1,8,72,128]{4,3,2,1,0:T(8,128)(2,1)S(1)}, u32[]{:S(2)}, u32[]{:S(2)}) collective-permute-start(bf16[2,1,8,72,128]{4,3,2,1,0:T(8,128)(2,1)S(1)} %get-tuple-element.75.refs_26_), channel_id=1, source_target_pairs={{0,4},{2,6},{4,0},{6,2},{8,12},{10,14},{12,8},{14,10},{16,20},{18,... | collective-permute-start | bytes 884744 | tf_op jit(solution)/shard_map/ppermute | solution.py:42
  74.7 16.4 %collective-permute-start.21 = (bf16[1,1,8,280,128]{4,3,2,1,0:T(8,128)(2,1)S(1)}, bf16[1,1,8,280,128]{4,3,2,1,0:T(8,128)(2,1)S(1)}, u32[]{:S(2)}, u32[]{:S(2)}) collective-permute-start(bf16[1,1,8,280,128]{4,3,2,1,0:T(8,128)(2,1)S(1)} %get-tuple-element.89), channel_id=1, source_target_pairs={{0,8},{2,10},{4,12},{6,14},{8,0},{10,2},{12,4},{14,6},{16,24},{18,... | collective-permute-start | bytes 1720328 | tf_op jit(solution)/shard_map/ppermute | solution.py:42
  83.4 9.8 %collective-permute-start.18 = (bf16[8,256,128]{2,1,0:T(8,128)(2,1)S(1)}, bf16[8,256,128]{2,1,0:T(8,128)(2,1)S(1)}, u32[]{:S(2)}, u32[]{:S(2)}) collective-permute-start(bf16[8,256,128]{2,1,0:T(8,128)(2,1)S(1)} %get-tuple-element.83), channel_id=1, source_target_pairs={{0,2},{2,0},{4,6},{6,4},{8,10},{10,8},{12,14},{14,12},{16,18},{18,... | collective-permute-start | bytes 1572872 | tf_op jit(solution)/shard_map/ppermute | solution.py:42
  83.4 12.2 %collective-permute-start.19 = (bf16[8,256,128]{2,1,0:T(8,128)(2,1)S(1)}, bf16[8,256,128]{2,1,0:T(8,128)(2,1)S(1)}, u32[]{:S(2)}, u32[]{:S(2)}) collective-permute-start(bf16[8,256,128]{2,1,0:T(8,128)(2,1)S(1)} %get-tuple-element.87), channel_id=1, source_target_pairs={{0,2},{2,0},{4,6},{6,4},{8,10},{10,8},{12,14},{14,12},{16,18},{18,... | collective-permute-start | bytes 1572872 | tf_op jit(solution)/shard_map/ppermute | solution.py:42
  83.9 11.7 %collective-permute-start.20 = (bf16[8,256,128]{2,1,0:T(8,128)(2,1)S(1)}, bf16[8,256,128]{2,1,0:T(8,128)(2,1)S(1)}, u32[]{:S(2)}, u32[]{:S(2)}) collective-permute-start(bf16[8,256,128]{2,1,0:T(8,128)(2,1)S(1)} %get-tuple-element.88), channel_id=1, source_target_pairs={{0,2},{2,0},{4,6},{6,4},{8,10},{10,8},{12,14},{14,12},{16,18},{18,... | collective-permute-start | bytes 1572872 | tf_op jit(solution)/shard_map/ppermute | solution.py:42
  84.0 12.5 %collective-permute-start.22 = (bf16[2,1,8,72,128]{4,3,2,1,0:T(8,128)(2,1)S(1)}, bf16[2,1,8,72,128]{4,3,2,1,0:T(8,128)(2,1)S(1)}, u32[]{:S(2)}, u32[]{:S(2)}) collective-permute-start(bf16[2,1,8,72,128]{4,3,2,1,0:T(8,128)(2,1)S(1)} %collective-permute-done.15.refs_5_), channel_id=1, source_target_pairs={{0,8},{2,10},{4,12},{6,14},{8,0},{10,2},{12,4},{14,6},{16,24},{18,... | collective-permute-start | bytes 884744 | tf_op jit(solution)/shard_map/ppermute | solution.py:42
  98.0 1.9 %collective-permute-start.23 = (bf16[2,8,112,128]{3,2,1,0:T(8,128)(2,1)S(1)}, bf16[2,8,112,128]{3,2,1,0:T(8,128)(2,1)S(1)}, u32[]{:S(2)}, u32[]{:S(2)}) collective-permute-start(bf16[2,8,112,128]{3,2,1,0:T(8,128)(2,1)S(1)} %get-tuple-element.95), channel_id=1, source_target_pairs={{0,2},{2,0},{4,6},{6,4},{8,10},{10,8},{12,14},{14,12},{16,18},{18,... | collective-permute-start | bytes 1376264 | tf_op jit(solution)/shard_map/ppermute | solution.py:42
